TPU v7x, 512 devices: a whole 4x8x8 slice. The times are simulated.
512 devices in a mesh: heads: 8 (over z), ctx: 64 (over y, x, core).
Axes of the slice: x: 4, y: 8, z: 8, core: 2. Of those that a mesh axis runs over, the one named last changes fastest.
Arguments:
- queries: bfloat16 [8, 8192, 512], P('heads', 'ctx'), may hold values from -16 to 16
- keys: bfloat16 [8, 8192, 128], P('heads', 'ctx'), may hold values from -16 to 16
- values: bfloat16 [8, 8192, 128], P('heads', 'ctx'), may hold values from -43 to 43
- out_grad: bfloat16 [8, 8192, 512], P('heads', 'ctx'), may hold values from -43 to 43
- gain_lin: float32 [8, 512], P('heads'), may hold values from 0.1 to 1.9
- gain_sparse: float32 [8, 512], P('heads'), may hold values from 0.1 to 1.9
- key_blocks: int32 [8, 64, 4], P('heads'), may hold values from -1 to 63, as said below
- w_feat: bfloat16 [128, 256], replicated, may hold values from -0.5 to 0.5
Outputs:
- query_grads: bfloat16 [8, 8192, 512], P('heads', 'ctx')
- key_grads: bfloat16 [8, 8192, 128], P('heads', 'ctx')
- value_grads: bfloat16 [8, 8192, 128], P('heads', 'ctx')
- w_grad: float32 [128, 256], replicated
Inputs may be any that keep to these rules, and one draw needn't show every extreme that they name: `key_blocks`: entry r - 1 of row i for head group g is -1 or the index of a key block of context shard i - r (r = 1 to 4): a shard takes at most one block from each of the 4 shards before it, and -1 stands where it takes none or i - r < 0. Counts differ from shard to shard; in every head group some shard takes a block from all 4 preceding shards, and some shard gives a block to all 4 shards after it.
All inputs are finite; a program needn't handle non-finite values.
Results may differ from a plain program's by a relative error of at most 0.009.
Values may be sent and summed in bfloat16 or wider, within the bound.
No kernel may reach another device: no remote copies, remote signals or barrier semaphores. Data moves between devices by JAX's collectives and lax.ppermute only.
A program may use at most 64 MiB of HBM per device.

v0:
```python
import jax
import jax.numpy as jnp
from jax import lax
from jax.sharding import PartitionSpec as P

BLK = 128


norm_epsilon = 1e-06


def entering(value, axis, join, neutral):
    place = lax.axis_index(axis)
    gathered = lax.all_gather(value.astype(jnp.bfloat16), axis)
    state = jnp.zeros_like(value) + jnp.asarray(neutral, value.dtype)

    def entering_one(hop, state):
        return join(state, lax.dynamic_index_in_dim(gathered, hop, 0, False).astype(value.dtype))

    return lax.fori_loop(0, place, entering_one, state)


def shifted(value, axis, by):
    length = lax.axis_size(axis)
    pairs = [(i, i + by) for i in range(length) if 0 <= i + by < length]
    return lax.ppermute(value, axis, pairs)


def prefix(value, axis, join, neutral):
    count = lax.axis_size(axis)
    place = lax.axis_index(axis)
    ahead = count - 1 - place
    gathered = lax.all_gather(
        value.astype(jnp.bfloat16 if value.dtype == jnp.float32 else value.dtype), axis
    )
    state = jnp.zeros_like(value) + jnp.asarray(neutral, value.dtype)

    def prefix_one(hop, state):
        source = count - 1 - hop
        return join(state, lax.dynamic_index_in_dim(gathered, source, 0, False).astype(value.dtype))

    return lax.fori_loop(0, ahead, prefix_one, state)


def feature_map(raw_value):
    return jnp.where(raw_value > 0, raw_value + 1.0, jnp.exp(jnp.minimum(raw_value, 0.0)))


def feature_slope(raw_value):
    return jnp.where(raw_value > 0, 1.0, jnp.exp(jnp.minimum(raw_value, 0.0)))


def norm_backward(value, upstream):
    inverse = lax.rsqrt(jnp.mean(value * value, axis=-1, keepdims=True) + norm_epsilon)
    projected = jnp.mean(upstream * value, axis=-1, keepdims=True)
    return inverse * upstream - value * (inverse * inverse * inverse) * projected


def product_rows(left, right):
    return lax.dot_general(
        left, right, (((1,), (1,)), ((), ())), preferred_element_type=jnp.float32
    )


def product_cols(left, right):
    return lax.dot_general(
        left, right, (((0,), (0,)), ((), ())), preferred_element_type=jnp.float32
    )


def add_pair(earlier, later):
    return earlier + later


def per_device(queries, keys, values, out_grad, gain_lin, gain_sparse, key_blocks, w_feat):
    highest = lax.Precision.HIGHEST
    length = queries.shape[1]
    head_size = keys.shape[2]
    features = w_feat.shape[1]
    query_heads = queries.shape[2] // head_size
    block_size = BLK
    blocks_here = length // block_size
    reach_count = key_blocks.shape[2]
    scaling = head_size ** (-0.5)
    shard_count = lax.axis_size("ctx")
    position = lax.axis_index("ctx")
    block_table = key_blocks[0]
    query_flat = queries[0]
    query_rows = query_flat.reshape(length * query_heads, head_size)
    key_rows = keys[0]
    value_rows = values[0]
    grad_flat = out_grad[0]
    upstream = grad_flat.reshape(length, query_heads, head_size).astype(jnp.float32)
    lin_gain = gain_lin[0].reshape(query_heads, head_size)
    sparse_gain = gain_sparse[0]
    query_raw = jnp.dot(query_rows, w_feat, preferred_element_type=jnp.float32)
    query_feat = feature_map(query_raw).astype(jnp.bfloat16)
    key_raw = jnp.dot(key_rows, w_feat, preferred_element_type=jnp.float32)
    key_feat = feature_map(key_raw).astype(jnp.bfloat16)
    query_blocks = query_feat.reshape(blocks_here, block_size, query_heads, features)
    key_feat_blocks = key_feat.reshape(blocks_here, block_size, features)
    value_blocks = value_rows.reshape(blocks_here, block_size, head_size)
    block_total = jnp.einsum(
        "bsf,bsd->bfd", key_feat_blocks, value_blocks, preferred_element_type=jnp.float32
    )
    running = jnp.cumsum(block_total, axis=0)
    before = entering(running[-1], "ctx", add_pair, jnp.zeros_like(running[-1]))
    block_state = before[None] + jnp.concatenate([jnp.zeros_like(running), running[:-1]], axis=0)
    query_wide = query_blocks.astype(jnp.float32)
    lin_state = jnp.einsum("bthf,bfd->bthd", query_wide, block_state, precision=highest)
    causal = lax.broadcasted_iota(jnp.int32, (block_size, block_size), 0) >= lax.broadcasted_iota(
        jnp.int32, (block_size, block_size), 1
    )
    lin_scores = jnp.einsum(
        "bthf,bsf->bhts", query_blocks, key_feat_blocks, preferred_element_type=jnp.float32
    )
    lin_weights = jnp.where(causal, lin_scores, 0.0).astype(jnp.bfloat16)
    lin_local = jnp.einsum(
        "bhts,bsd->bthd", lin_weights, value_blocks, preferred_element_type=jnp.float32
    )
    lin_out = (lin_state + lin_local).reshape(length, query_heads, head_size)
    lin_grad = norm_backward(lin_out, upstream * lin_gain)
    pair_local = jnp.stack([key_rows, value_rows])
    fetched = []
    for offset in range(1, reach_count + 1):
        whole = shifted(pair_local, "ctx", offset)
        fetched.append(whole)
    key_all = jnp.concatenate([key_rows] + [item[0] for item in fetched], axis=0)
    value_all = jnp.concatenate([value_rows] + [item[1] for item in fetched], axis=0)
    key_count = key_all.shape[0]
    row_index = lax.broadcasted_iota(jnp.int32, (length, key_count), 0)
    col_index = lax.broadcasted_iota(jnp.int32, (length, key_count), 1)
    far_live = jnp.concatenate(
        [jnp.zeros((length,), jnp.bool_), jnp.repeat(block_table[position] >= 0, block_size)]
    )
    allowed = (col_index <= row_index) | far_live[None, :]

    def head_step(totals, head_index):
        key_total, value_total = totals
        first_col = head_index * head_size
        query_head = lax.dynamic_slice_in_dim(query_flat, first_col, head_size, 1)
        grad_head = lax.dynamic_slice_in_dim(grad_flat, first_col, head_size, 1).astype(jnp.float32)
        gain_head = lax.dynamic_slice_in_dim(sparse_gain, first_col, head_size, 0)
        logits = jnp.where(allowed, scaling * product_rows(query_head, key_all), -jnp.inf)
        row_max = jnp.max(logits, axis=1, keepdims=True)
        exp_terms = jnp.exp(logits - row_max)
        probs = exp_terms / jnp.sum(exp_terms, axis=1, keepdims=True)
        probs_half = probs.astype(jnp.bfloat16)
        sparse_out = jnp.dot(probs_half, value_all, preferred_element_type=jnp.float32)
        sparse_grad = norm_backward(sparse_out, grad_head * gain_head).astype(jnp.bfloat16)
        prob_grad = product_rows(sparse_grad, value_all)
        row_inner = jnp.sum(sparse_grad.astype(jnp.float32) * sparse_out, axis=1, keepdims=True)
        logit_grad = (scaling * probs * (prob_grad - row_inner)).astype(jnp.bfloat16)
        query_part = jnp.dot(logit_grad, key_all, preferred_element_type=jnp.float32)
        key_total = key_total + product_cols(logit_grad, query_head)
        value_total = value_total + product_cols(probs_half, sparse_grad)
        return ((key_total, value_total), query_part)

    zero_rows = jnp.zeros((key_count, head_size), jnp.float32)
    (key_sparse, value_sparse), query_sparse = lax.scan(
        head_step, (zero_rows, zero_rows), jnp.arange(query_heads)
    )
    pair_sparse = jnp.stack([key_sparse[:length], value_sparse[:length]])
    for offset in range(1, reach_count + 1):
        first_far = length + (offset - 1) * block_size
        outgoing = jnp.stack(
            [
                key_sparse[first_far : first_far + block_size],
                value_sparse[first_far : first_far + block_size],
            ]
        )
        returned = shifted(outgoing.astype(jnp.bfloat16), "ctx", -offset).astype(outgoing.dtype)
        asked = block_table[jnp.minimum(position + offset, shard_count - 1), offset - 1]
        is_live = (asked >= 0) & (position + offset < shard_count)
        current = pair_sparse
        pair_sparse = current + jnp.where(is_live, returned, 0.0)
    lin_grad_blocks = lin_grad.reshape(blocks_here, block_size, query_heads, head_size)
    lin_half = lin_grad_blocks.astype(jnp.bfloat16)
    state_q_grad = jnp.einsum("bthd,bfd->bthf", lin_grad_blocks, block_state, precision=highest)
    block_cot = jnp.einsum("bthf,bthd->bfd", query_wide, lin_grad_blocks, precision=highest)
    later = jnp.cumsum(block_cot[::-1], axis=0)[::-1]
    after = prefix(later[0], "ctx", add_pair, jnp.zeros_like(later[0]))
    carried = after[None] + jnp.concatenate([later[1:], jnp.zeros_like(later)], axis=0)
    key_state_grad = jnp.einsum(
        "bsd,bfd->bsf", value_blocks.astype(jnp.float32), carried, precision=highest
    )
    value_state_grad = jnp.einsum(
        "bsf,bfd->bsd", key_feat_blocks.astype(jnp.float32), carried, precision=highest
    )
    score_grad = jnp.where(
        causal,
        jnp.einsum("bthd,bsd->bhts", lin_half, value_blocks, preferred_element_type=jnp.float32),
        0.0,
    ).astype(jnp.bfloat16)
    query_local_grad = jnp.einsum(
        "bhts,bsf->bthf", score_grad, key_feat_blocks, preferred_element_type=jnp.float32
    )
    key_local_grad = jnp.einsum(
        "bhts,bthf->bsf", score_grad, query_blocks, preferred_element_type=jnp.float32
    )
    value_local_grad = jnp.einsum(
        "bhts,bthd->bsd", lin_weights, lin_half, preferred_element_type=jnp.float32
    )
    raw_q_grad = (
        (state_q_grad + query_local_grad).reshape(length * query_heads, features)
        * feature_slope(query_raw)
    ).astype(jnp.bfloat16)
    raw_k_grad = (
        (key_state_grad + key_local_grad).reshape(length, features) * feature_slope(key_raw)
    ).astype(jnp.bfloat16)
    query_lin = product_rows(raw_q_grad, w_feat).reshape(length, query_heads * head_size)
    key_lin = product_rows(raw_k_grad, w_feat)
    weight_part = product_cols(query_rows, raw_q_grad) + product_cols(key_rows, raw_k_grad)
    weight_total = lax.psum(weight_part, ("heads", "ctx"))
    weight_scale = (queries.shape[0] * lax.axis_size("heads") * length * shard_count) ** (-0.5)
    query_out = (
        jnp.transpose(query_sparse, (1, 0, 2)).reshape(length, query_heads * head_size) + query_lin
    )
    key_out = pair_sparse[0] + key_lin
    value_out = pair_sparse[1] + (value_state_grad + value_local_grad).reshape(length, head_size)
    return (
        query_out.astype(jnp.bfloat16)[None],
        key_out.astype(jnp.bfloat16)[None],
        value_out.astype(jnp.bfloat16)[None],
        weight_total * weight_scale,
    )


def solution(mesh):
    placed = (
        P("heads", "ctx", None),
        P("heads", "ctx", None),
        P("heads", "ctx", None),
        P("heads", "ctx", None),
        P("heads", None),
        P("heads", None),
        P("heads", None, None),
        P(),
    )
    return jax.shard_map(
        per_device,
        mesh=mesh,
        in_specs=placed,
        out_specs=(P("heads", "ctx", None), P("heads", "ctx", None), P("heads", "ctx", None), P()),
        check_vma=False,
    )
```

profile of v0, /device:TPU:1, one launch (start us, length us, event | category | flops | bytes accessed | tf_op | source)
XLA Modules:
  0.0 565.1 jit_solution(5049771354731738791)
XLA Ops:
  8.0 0.9 select_convert_fusion.1
  8.9 1.6 convolution_convert_fusion
  12.1 4.5 collective-permute-start
  16.6 3.1 collective-permute-start.1
  19.7 3.4 collective-permute-start.2
  23.2 3.4 collective-permute-start.3
  26.6 1.0 reshape_squeeze.4
  28.0 0.9 fusion.71
  30.0 1.0 copy.19
  31.0 1.0 copy.12
  32.1 1.5 constant_dynamic-slice_fusion.3
  36.2 66.0 %all-gather.5.cloned.1.call-done = bf16[16384,128]{1,0:T(8,128)(2,1)} async-done(((bf16[256,128]{1,0:T(8,128)(2,1)}), bf16[16384,128]{1,0:T(8,128)(2,1)}) %all-gather.5.cloned.1.call-update) | async-done | bytes 4194320 | tf_op jit(solution)/shard_map/all_gather | solution.py:14
  102.2 0.9 while.37
  102.2 0.9 convert_add_fusion.4
  103.9 1.1 fusion.30
  105.1 24.6 %while.39 = (s32[]{:T(128)}, f32[640,128]{1,0:T(8,128)S(1)}, f32[640,128]{1,0:T(8,128)}, f32[4,128,128]{2,1,0:T(8,128)}, s32[4]{0:T(128)S(1)}, /*index=5*/bf16[1...) while((s32[]{:T(128)}, f32[640,128]{1,0:T(8,128)S(1)}, ...), condition=%wide.region_6.7_spmd.clone, body=%wide.region_0.6_spmd.clone.sunk | while | flops 127975424 | bytes 4536550 | solution.py:160
  108.1 1.1 convolution_add_fusion.7
  113.5 2.1 convolution_add_fusion.7
  119.9 2.1 convolution_add_fusion.7
  126.2 2.1 convolution_add_fusion.7
  129.7 1.0 convert.33
  130.7 1.9 collective-permute-start.4
  132.7 1.3 collective-permute-start.5
  134.0 1.3 collective-permute-start.6
  135.3 1.3 collective-permute-start.7
  137.5 1.1 copy.13
  138.9 3.8 collective-permute-done.6
  142.6 2.6 collective-permute-done.7
  148.5 91.7 %all-gather.7.cloned.1.call-done = bf16[16384,128]{1,0:T(8,128)(2,1)} async-done(((bf16[256,128]{1,0:T(8,128)(2,1)}), bf16[16384,128]{1,0:T(8,128)(2,1)}) %all-gather.7.cloned.1.call-update) | async-done | bytes 4194320 | tf_op jit(solution)/shard_map/all_gather | solution.py:33
  240.2 55.3 %while.38 = (s32[]{:T(128)}, f32[256,128]{1,0:T(8,128)S(1)}, s32[]{:T(128)}, bf16[64,256,128]{2,1,0:T(8,128)(2,1)}, s32[]{:T(128)}, /*index=5*/s32[]{:T(128)}, s32[]{:T(128)}, s32[]{:T(128)}) while((s32[]{:T(128)}, f32[256,128]{1,0:T(8,128)S(1)}, s32[]{:T(128)}, bf16[64,256,128]{2,1,0:T(8,128)(2,1)}, s32[]{:T(128)}, /*index=5*/s32[]{:T(128)}, ...), condition=%wide.region_12.13_spmd, body=%wide.region_11.12_spmd.sunk | while | flops 65542 | bytes 327815 | solution.py:42
  240.2 0.9 convert_add_fusion.5
  241.1 0.9 convert_add_fusion.5
  242.0 0.9 convert_add_fusion.5
  242.9 0.9 convert_add_fusion.5
  243.8 0.9 convert_add_fusion.5
  244.7 0.9 convert_add_fusion.5
  245.6 0.9 convert_add_fusion.5
  246.5 0.9 convert_add_fusion.5
  247.3 0.9 convert_add_fusion.5
  248.2 0.9 convert_add_fusion.5
  249.1 0.9 convert_add_fusion.5
  250.0 0.9 convert_add_fusion.5
  250.9 0.9 convert_add_fusion.5
  251.8 0.9 convert_add_fusion.5
  252.7 0.9 convert_add_fusion.5
  253.6 0.9 convert_add_fusion.5
  254.5 0.9 convert_add_fusion.5
  255.4 0.9 convert_add_fusion.5
  256.3 0.9 convert_add_fusion.5
  257.1 0.9 convert_add_fusion.5
  258.0 0.9 convert_add_fusion.5
  258.9 0.9 convert_add_fusion.5
  259.8 0.9 convert_add_fusion.5
  264.3 0.9 convert_add_fusion.5
  266.9 0.9 convert_add_fusion.5
  274.1 0.9 convert_add_fusion.5
  276.7 0.9 convert_add_fusion.5
  281.2 0.9 convert_add_fusion.5
  283.9 0.9 convert_add_fusion.5
  291.0 0.9 convert_add_fusion.5
  293.7 0.9 convert_add_fusion.5
  295.9 0.9 fusion.26
  298.5 258.4 %all-reduce.3.cloned.1.call-done = f32[128,256]{0,1:T(8,128)} async-done(((f32[128,256]{0,1:T(8,128)}), f32[128,256]{0,1:T(8,128)}) %all-reduce.3.cloned.1.call-update) | async-done | bytes 131088 | tf_op jit(solution)/shard_map/psum | solution.py:214
  556.9 0.9 broadcast_multiply_fusion.1
  (143 shorter events, 53.2 us)
Async XLA Ops:
  7.2 0.8 copy-start
  7.2 96.3 %copy-start.1 = (bf16[1,128,128]{2,1,0:T(8,128)(2,1)S(1)}, bf16[1,128,128]{2,1,0:T(8,128)(2,1)}, u32[]{:S(2)}) copy-start(bf16[1,128,128]{2,1,0:T(8,128)(2,1)} %param.16) | copy-start | bytes 98308
  7.2 96.3 %copy-start.4 = (f32[1,512]{1,0:T(1,128)S(1)}, f32[1,512]{1,0:T(1,128)}, u32[]{:S(2)}) copy-start(f32[1,512]{1,0:T(1,128)} %param.18) | copy-start | bytes 6148
  7.2 95.0 %all-gather.5.cloned.1.call-start = ((), (), s32[]{:S(2)}) async-start(), calls=%async_computation.1 | async-start | bytes 4259840 | tf_op jit(solution)/shard_map/all_gather | solution.py:14
  10.6 229.6 %all-gather.7.cloned.1.call-start = ((), (), s32[]{:S(2)}) async-start(), calls=%async_computation.2 | async-start | bytes 4259840 | tf_op jit(solution)/shard_map/all_gather | solution.py:33
  12.1 23.9 %collective-permute-start = (bf16[2,128,128]{2,1,0:T(8,128)(2,1)S(1)}, bf16[2,128,128]{2,1,0:T(8,128)(2,1)S(1)}, u32[]{:S(2)}, u32[]{:S(2)}) collective-permute-start(bf16[2,128,128]{2,1,0:T(8,128)(2,1)S(1)} %constant_dynamic-update-slice_fusion), channel_id=1, source_target_pairs={{0,1},{1,2},{2,3},{3,4},{4,5},{5,6},{6,7},{7,8},{8,9},{9,10},{10,1... | collective-permute-start | bytes 196616 | tf_op jit(solution)/shard_map/ppermute | solution.py:26
  16.6 19.5 %collective-permute-start.1 = (bf16[2,128,128]{2,1,0:T(8,128)(2,1)S(1)}, bf16[2,128,128]{2,1,0:T(8,128)(2,1)S(1)}, u32[]{:S(2)}, u32[]{:S(2)}) collective-permute-start(bf16[2,128,128]{2,1,0:T(8,128)(2,1)S(1)} %constant_dynamic-update-slice_fusion), channel_id=1, source_target_pairs={{0,2},{1,3},{2,4},{3,5},{4,6},{5,7},{6,8},{7,9},{8,10},{9,11},{10,... | collective-permute-start | bytes 196616 | tf_op jit(solution)/shard_map/ppermute | solution.py:26
  19.7 16.4 %collective-permute-start.2 = (bf16[2,128,128]{2,1,0:T(8,128)(2,1)S(1)}, bf16[2,128,128]{2,1,0:T(8,128)(2,1)S(1)}, u32[]{:S(2)}, u32[]{:S(2)}) collective-permute-start(bf16[2,128,128]{2,1,0:T(8,128)(2,1)S(1)} %constant_dynamic-update-slice_fusion), channel_id=1, source_target_pairs={{0,3},{1,4},{2,5},{3,6},{4,7},{5,8},{6,9},{7,10},{8,11},{9,12},{10... | collective-permute-start | bytes 196616 | tf_op jit(solution)/shard_map/ppermute | solution.py:26
  23.2 12.9 %collective-permute-start.3 = (bf16[2,128,128]{2,1,0:T(8,128)(2,1)S(1)}, bf16[2,128,128]{2,1,0:T(8,128)(2,1)S(1)}, u32[]{:S(2)}, u32[]{:S(2)}) collective-permute-start(bf16[2,128,128]{2,1,0:T(8,128)(2,1)S(1)} %constant_dynamic-update-slice_fusion), channel_id=1, source_target_pairs={{0,4},{1,5},{2,6},{3,7},{4,8},{5,9},{6,10},{7,11},{8,12},{9,13},{1... | collective-permute-start | bytes 196616 | tf_op jit(solution)/shard_map/ppermute | solution.py:26
  27.6 77.4 %copy-start.2 = (bf16[1,128,512]{2,1,0:T(8,128)(2,1)S(1)}, bf16[1,128,512]{2,1,0:T(8,128)(2,1)}, u32[]{:S(2)}) copy-start(bf16[1,128,512]{2,1,0:T(8,128)(2,1)} %param.14) | copy-start | bytes 393220
  105.0 451.9 %all-reduce.3.cloned.1.call-start = ((), (), s32[]{:S(2)}) async-start(), calls=%async_computation | async-start | bytes 262144 | tf_op jit(solution)/shard_map/psum | solution.py:214
  130.7 8.0 %collective-permute-start.4 = (bf16[2,128,128]{2,1,0:T(8,128)(2,1)S(1)}, bf16[2,128,128]{2,1,0:T(8,128)(2,1)S(1)}, u32[]{:S(2)}, u32[]{:S(2)}) collective-permute-start(bf16[2,128,128]{2,1,0:T(8,128)(2,1)S(1)} %pad_maximum_fusion), channel_id=1, source_target_pairs={{1,0},{2,1},{3,2},{4,3},{5,4},{6,5},{7,6},{8,7},{9,8},{10,9},{11,1... | collective-permute-start | bytes 196616 | tf_op jit(solution)/shard_map/ppermute | solution.py:26
  132.7 6.2 %collective-permute-start.5 = (bf16[2,128,128]{2,1,0:T(8,128)(2,1)S(1)}, bf16[2,128,128]{2,1,0:T(8,128)(2,1)S(1)}, u32[]{:S(2)}, u32[]{:S(2)}) collective-permute-start(bf16[2,128,128]{2,1,0:T(8,128)(2,1)S(1)} %pad_maximum_fusion.1), channel_id=1, source_target_pairs={{2,0},{3,1},{4,2},{5,3},{6,4},{7,5},{8,6},{9,7},{10,8},{11,9},{12,... | collective-permute-start | bytes 196616 | tf_op jit(solution)/shard_map/ppermute | solution.py:26
  134.0 8.7 %collective-permute-start.6 = (bf16[2,128,128]{2,1,0:T(8,128)(2,1)S(1)}, bf16[2,128,128]{2,1,0:T(8,128)(2,1)S(1)}, u32[]{:S(2)}, u32[]{:S(2)}) collective-permute-start(bf16[2,128,128]{2,1,0:T(8,128)(2,1)S(1)} %pad_maximum_fusion.2), channel_id=1, source_target_pairs={{3,0},{4,1},{5,2},{6,3},{7,4},{8,5},{9,6},{10,7},{11,8},{12,9},{13... | collective-permute-start | bytes 196616 | tf_op jit(solution)/shard_map/ppermute | solution.py:26
  135.3 10.0 %collective-permute-start.7 = (bf16[2,128,128]{2,1,0:T(8,128)(2,1)S(1)}, bf16[2,128,128]{2,1,0:T(8,128)(2,1)S(1)}, u32[]{:S(2)}, u32[]{:S(2)}) collective-permute-start(bf16[2,128,128]{2,1,0:T(8,128)(2,1)S(1)} %pad_maximum_fusion.3), channel_id=1, source_target_pairs={{4,0},{5,1},{6,2},{7,3},{8,4},{9,5},{10,6},{11,7},{12,8},{13,9},{1... | collective-permute-start | bytes 196616 | tf_op jit(solution)/shard_map/ppermute | solution.py:26
  146.4 149.3 %copy-start.3 = (bf16[1,128,128]{2,1,0:T(8,128)(2,1)S(1)}, bf16[1,128,128]{2,1,0:T(8,128)(2,1)}, u32[]{:S(2)}) copy-start(bf16[1,128,128]{2,1,0:T(8,128)(2,1)} %param.15) | copy-start | bytes 98308
Sparse Core Ops, SparseCore 0:
  11.9 90.1 all-gather.4
  106.1 134.0 all-gather.6
  297.0 259.8 all-reduce.2
where the time goes:
time: 569 us; the launch traced here: 565 us
  waiting for transfers between devices  423 us (74%)
  other arithmetic  59.6 us (10%)
  matrix products  24.4 us (4%)
  starting transfers between devices  20.4 us (4%)
  between operations  16.7 us (3%)
  local copies, waits for them, and re-layouts  16.6 us (3%)
    psum x1, waiting for transfers between devices, per_device(): weight_total = lax.psum(weight_part, ('heads', 'ctx'))  258 us
    all_gather x1, waiting for transfers between devices, prefix(): lax.all_gather(value.astype(jnp.bfloat16 if value.dtype == jnp.float32 el...  91.7 us
    all_gather x1, waiting for transfers between devices, entering(): gathered = lax.all_gather(value.astype(jnp.bfloat16), axis)  66 us
    add x63, other arithmetic, add_pair(): return earlier + later  54.4 us
    ppermute x8, starting transfers between devices, shifted(): return lax.ppermute(value, axis, pairs)  20.3 us
  transfers between devices with their start and end apart: 11, of which 6 were waited for; matrix products, arithmetic and copies ran while one was open for 7% of the time, Pallas kernels for 0%

commit v1 on v0

v1 whole, which is shorter than its diff:
```python
import jax
import jax.numpy as jnp
from jax import lax
from jax.experimental import pallas as pl
from jax.experimental.pallas import tpu as pltpu
from jax.sharding import PartitionSpec as P

INTERPRET = False
EPS = 1e-06
F32 = jnp.float32
BF16 = jnp.bfloat16


def nn(a, b):
    return lax.dot_general(a, b, (((1,), (0,)), ((), ())), preferred_element_type=F32)


def nt(a, b):
    return lax.dot_general(a, b, (((1,), (1,)), ((), ())), preferred_element_type=F32)


def tn(a, b):
    return lax.dot_general(a, b, (((0,), (0,)), ((), ())), preferred_element_type=F32)


def iotas(shape):
    return (
        lax.broadcasted_iota(jnp.int32, shape, 0),
        lax.broadcasted_iota(jnp.int32, shape, 1),
    )


def ones_where(mask):
    return jnp.where(mask, 1.0, 0.0).astype(BF16)


def features(raw):
    low = jnp.exp(jnp.minimum(raw, 0.0))
    up = raw > 0
    return jnp.where(up, raw + 1.0, low), jnp.where(up, 1.0, low)


def norm_backward(value, upstream):
    inverse = lax.rsqrt(jnp.mean(value * value, axis=-1, keepdims=True) + EPS)
    projected = jnp.mean(upstream * value, axis=-1, keepdims=True)
    return inverse * upstream - value * (inverse * inverse * inverse) * projected


def split(value):
    high = value.astype(BF16)
    return high, (value - high.astype(F32)).astype(BF16)


def spread(high, low):
    row, col = iotas((high.shape[0] * 2, high.shape[0]))
    place = row & 7
    piece = 4 * (row >> 3)
    first = ones_where((place < 4) & (col == piece + place))
    second = ones_where((place >= 4) & (col == piece + place - 4))
    return nn(first, high) + nn(second, low)


def tiles(value):
    return value.reshape(value.shape[0] // 8, 8, value.shape[1])


def flat(value):
    return value.reshape(value.shape[0] * 8, value.shape[2])


def send_state_kernel(k_ref, v_ref, w_ref, o_ref):
    keys = k_ref[0]
    values = v_ref[0]
    feat = features(nn(keys, w_ref[...]))[0].astype(BF16)
    total = tn(feat, values).astype(BF16)
    size = 2 * total.shape[0]
    row, col = iotas((size, total.shape[0]))
    place, piece = row & 7, row >> 3
    pick = ones_where((place < 4) & (col == 4 * piece + place))
    row, col = iotas((size, keys.shape[0]))
    place, piece = row & 7, row >> 3
    key_pick = ones_where((place >= 4) & (place < 6) & (col == 2 * piece + place - 4))
    value_pick = ones_where((place >= 6) & (col == 2 * piece + place - 6))
    message = nn(pick, total) + nn(key_pick, keys) + nn(value_pick, values)
    o_ref[...] = tiles(message).astype(BF16)


def delayed(value, by):
    return jnp.concatenate([jnp.zeros_like(value[:by]), value[:-by]], axis=0)


def advanced(value, by):
    return jnp.concatenate([value[by:], jnp.zeros_like(value[:by])], axis=0)


def turned(value, by):
    by = by % 8
    return value if by == 0 else pltpu.roll(value, by, 1)


def prefix_kernel(r_ref, o_ref):
    got = r_ref[...].astype(F32)
    count = got.shape[0]
    place = lax.broadcasted_iota(jnp.int32, got.shape, 1)
    total = jnp.zeros(got.shape[1:], F32)
    parts = []
    for source in range(count):
        parts.append(total)
        total = total + got[source]
    before = jnp.stack(parts)
    both = jnp.where(place < 4, before, turned(before, 4))
    high = both.astype(BF16).astype(F32)
    o_ref[:, 0] = jnp.where(place < 4, high, both - high).astype(BF16)
    turns = [turned(got, by) for by in (0, 2, 4, 6)]
    for slot, first in ((1, 4), (2, 6)):
        out = jnp.zeros_like(got)
        for reach in range(1, 5):
            moved = turns[((2 * (reach - 1) - first) % 8) // 2]
            out = jnp.where(place // 2 == reach - 1, delayed(moved, reach), out)
        o_ref[:, slot] = out.astype(BF16)


def main_kernel(
    q_ref, k_ref, v_ref, g_ref, gl_ref, gs_ref, kb_ref, w_ref, r_ref,
    qo_ref, send_ref, kloc_ref, dk_ref, dv_ref, wq_ref,
):
    shard = lax.axis_index("ctx")
    keys = k_ref[0]
    values = v_ref[0]
    w = w_ref[...]
    length, size = keys.shape
    heads = q_ref.shape[2] // size
    scaling = size ** (-0.5)
    rows = heads * length

    def stacked(ref):
        return jnp.concatenate(
            [ref[0, :, h * size : (h + 1) * size] for h in range(heads)], axis=0
        )

    def gains(ref):
        return jnp.concatenate(
            [
                jnp.broadcast_to(ref[:, h * size : (h + 1) * size], (length, size))
                for h in range(heads)
            ],
            axis=0,
        )

    queries = stacked(q_ref)
    upstream = stacked(g_ref).astype(F32)

    got = r_ref[:, 0].astype(F32)
    states = flat(got).astype(BF16)
    row, col = iotas((states.shape[0] // 2, states.shape[0]))
    where_high = 8 * (row >> 2) + (row & 3)
    state_high = nn(ones_where(col == where_high), states).astype(BF16)
    state_low = nn(ones_where(col == where_high + 4), states).astype(BF16)
    raw = nn(queries, w)
    feat, slope = features(raw)
    feat = feat.astype(BF16)
    key_feat = features(nn(keys, w))[0].astype(BF16)
    row, col = iotas((rows, length))
    causal = (row & (length - 1)) >= col
    weights = jnp.where(causal, nt(feat, key_feat), 0.0).astype(BF16)
    lin_out = nn(feat, state_high) + nn(feat, state_low) + nn(weights, values)
    lin_grad = norm_backward(lin_out, upstream * gains(gl_ref))
    lin_high, lin_low = split(lin_grad)
    score_grad = jnp.where(causal, nt(lin_high, values), 0.0).astype(BF16)
    feat_grad = (
        nt(lin_high, state_high)
        + nt(lin_high, state_low)
        + nt(lin_low, state_high)
        + nn(score_grad, key_feat)
    )
    raw_grad = (feat_grad * slope).astype(BF16)
    query_lin = nt(raw_grad, w)
    cot = tn(feat, lin_high) + tn(feat, lin_low)
    kloc_ref[...] = tn(score_grad, feat)
    value_local = tn(weights, lin_high)
    wq_ref[...] = tn(queries, raw_grad)
    send_ref[:, 0] = tiles(spread(*split(cot))).astype(BF16)

    key_far = flat(r_ref[:, 1].astype(F32)).astype(BF16)
    value_far = flat(r_ref[:, 2].astype(F32)).astype(BF16)
    far = key_far.shape[0]
    listed = kb_ref[0, pl.ds(shard, 1), :]
    place = (lax.broadcasted_iota(jnp.int32, (1, far), 1) & 7) >> 1
    live = jnp.zeros((1, far), F32)
    for reach in range(listed.shape[1]):
        here = jnp.where(listed[:, reach : reach + 1] >= 0, 1.0, 0.0)
        live = jnp.where(place == reach, here, live)
    near_logits = jnp.where(causal, scaling * nt(queries, keys), -jnp.inf)
    far_logits = jnp.where(live > 0.5, scaling * nt(queries, key_far), -jnp.inf)
    top = jnp.maximum(
        jnp.max(near_logits, axis=1, keepdims=True), jnp.max(far_logits, axis=1, keepdims=True)
    )
    near_exp = jnp.exp(near_logits - top)
    far_exp = jnp.exp(far_logits - top)
    norm = 1.0 / (
        jnp.sum(near_exp, axis=1, keepdims=True) + jnp.sum(far_exp, axis=1, keepdims=True)
    )
    near_probs = near_exp * norm
    far_probs = far_exp * norm
    near_half = near_probs.astype(BF16)
    far_half = far_probs.astype(BF16)
    sparse_out = nn(near_half, values) + nn(far_half, value_far)
    sparse_grad = norm_backward(sparse_out, upstream * gains(gs_ref)).astype(BF16)
    inner = jnp.sum(sparse_grad.astype(F32) * sparse_out, axis=1, keepdims=True)
    near_grad = (scaling * near_probs * (nt(sparse_grad, values) - inner)).astype(BF16)
    far_grad = (scaling * far_probs * (nt(sparse_grad, value_far) - inner)).astype(BF16)
    query_out = nn(near_grad, keys) + nn(far_grad, key_far) + query_lin
    for h in range(heads):
        qo_ref[0, :, h * size : (h + 1) * size] = query_out[
            h * length : (h + 1) * length
        ].astype(BF16)
    dk_ref[...] = tn(near_grad, queries)
    dv_ref[...] = tn(near_half, sparse_grad) + value_local
    send_ref[:, 1] = tiles(tn(far_grad, queries)).astype(BF16)
    send_ref[:, 2] = tiles(tn(far_half, sparse_grad)).astype(BF16)


def suffix_kernel(r_ref, o_ref):
    cot = r_ref[:, 0].astype(F32)
    cot = cot + turned(cot, 4)
    count = cot.shape[0]
    place = lax.broadcasted_iota(jnp.int32, cot.shape, 1)
    total = jnp.zeros(cot.shape[1:], F32)
    parts = [None] * count
    for source in range(count - 1, -1, -1):
        parts[source] = total
        total = total + cot[source]
    out = jnp.stack(parts)
    for slot, first in ((1, 4), (2, 6)):
        got = r_ref[:, slot].astype(F32)
        summed = jnp.zeros_like(got)
        for reach in range(1, 5):
            summed = summed + advanced(turned(got, first - 2 * (reach - 1)), reach)
        out = jnp.where((place >= first) & (place < first + 2), summed, out)
    o_ref[...] = out


def key_kernel(
    k_ref, v_ref, w_ref, r_ref, kloc_ref, dk_ref, dv_ref, wq_ref, ko_ref, vo_ref, send_ref
):
    keys = k_ref[0]
    values = v_ref[0]
    w = w_ref[...]
    high, low = split(flat(r_ref[...]))
    count = high.shape[0]
    half, length = count // 2, keys.shape[0]
    row, col = iotas((half, count))
    pick = ones_where(col == 8 * (row >> 2) + (row & 3))
    carried_high = nn(pick, high).astype(BF16)
    carried_low = nn(pick, low).astype(BF16)
    row, col = iotas((length, count))
    at = 8 * (row >> 1) + (row & 1)
    key_pick = ones_where(col == at + 4)
    value_pick = ones_where(col == at + 6)
    key_sum = dk_ref[...] + nn(key_pick, high) + nn(key_pick, low)
    value_sum = dv_ref[...] + nn(value_pick, high) + nn(value_pick, low)
    feat, slope = features(nn(keys, w))
    feat = feat.astype(BF16)
    feat_grad = nt(values, carried_high) + nt(values, carried_low) + kloc_ref[...]
    raw_grad = (feat_grad * slope).astype(BF16)
    ko_ref[0] = (key_sum + nt(raw_grad, w)).astype(BF16)
    vo_ref[0] = (value_sum + nn(feat, carried_high) + nn(feat, carried_low)).astype(BF16)
    weight = wq_ref[...] + tn(keys, raw_grad)
    size = keys.shape[1]
    pair = jnp.concatenate([weight[:, :size], weight[:, size:]], axis=0)
    send_ref[...] = tiles(spread(*split(pair))).astype(BF16)


def gather_sum_kernel(r_ref, o_ref):
    total = jnp.sum(r_ref[...].astype(F32), axis=0)
    total = total + pltpu.roll(total, 4, 0)
    o_ref[...] = jnp.broadcast_to(total[None], o_ref.shape)


def make_scale_kernel(scale):
    def scale_kernel(r_ref, o_ref):
        total = jnp.sum(r_ref[...], axis=0) * scale
        place = lax.broadcasted_iota(jnp.int32, total.shape, 0)
        high = total.astype(BF16).astype(F32)
        tile = jnp.where(place < 4, high, total - high)
        o_ref[...] = jnp.broadcast_to(tile[None], o_ref.shape).astype(BF16)

    return scale_kernel


def weight_kernel(r_ref, o_ref):
    got = flat(r_ref[...].astype(F32)).astype(BF16)
    count = got.shape[0]
    row, col = iotas((count // 2, count))
    at = 8 * (row >> 2) + (row & 3)
    pair = nn(ones_where((col == at) | (col == at + 4)), got)
    length, size = o_ref.shape[0], o_ref.shape[1] // 2
    o_ref[:, :size] = pair[:length]
    o_ref[:, size:] = pair[length:]


def call(kernel, *outs):
    shapes = [jax.ShapeDtypeStruct(shape, dtype) for shape, dtype in outs]
    return pl.pallas_call(
        kernel,
        out_shape=shapes if len(shapes) > 1 else shapes[0],
        interpret=INTERPRET,
    )


def swap(value, axis):
    return lax.all_to_all(value, axis, 0, 0, tiled=False)


def per_device(queries, keys, values, out_grad, gain_lin, gain_sparse, key_blocks, w_feat):
    shards = lax.axis_size("ctx")
    groups = lax.axis_size("heads")
    length, size = keys.shape[1:]
    features_n = w_feat.shape[1]
    scale = (queries.shape[0] * groups * length * shards) ** (-0.5)
    tile = (8, size)
    sent = call(send_state_kernel, ((shards, *tile), BF16))(keys, values, w_feat)
    got = call(prefix_kernel, ((shards, 3, *tile), BF16))(swap(sent, "ctx"))
    query_out, sent, key_local, key_near, value_near, weight_part = call(
        main_kernel,
        (queries.shape, BF16),
        ((shards, 3, *tile), BF16),
        ((length, features_n), F32),
        ((length, size), F32),
        ((length, size), F32),
        ((size, features_n), F32),
    )(
        queries, keys, values, out_grad, gain_lin, gain_sparse, key_blocks, w_feat,
        swap(got, "ctx"),
    )
    got = call(suffix_kernel, ((shards, *tile), F32))(swap(sent, "ctx"))
    key_out, value_out, sent = call(
        key_kernel, (keys.shape, BF16), (values.shape, BF16), ((shards, *tile), BF16)
    )(
        keys, values, w_feat, swap(got, "ctx"), key_local, key_near, value_near, weight_part
    )
    part = call(gather_sum_kernel, ((groups, *tile), F32))(swap(sent, "ctx"))
    part = call(make_scale_kernel(scale), ((shards, *tile), BF16))(swap(part, "heads"))
    weight = call(weight_kernel, (w_feat.shape, F32))(swap(part, "ctx"))
    return query_out, key_out, value_out, weight


def solution(mesh):
    sharded = P("heads", "ctx", None)
    return jax.shard_map(
        per_device,
        mesh=mesh,
        in_specs=(
            sharded,
            sharded,
            sharded,
            sharded,
            P("heads", None),
            P("heads", None),
            P("heads", None, None),
            P(),
        ),
        out_specs=(sharded, sharded, sharded, P()),
        check_vma=False,
    )
```

time: 569 us -> 155 us (0.27)
  waiting for transfers between devices: 423 us -> 14.6 us
  blocking collectives: 0 us -> 113 us
  other arithmetic: 59.6 us -> 0 us
  matrix products: 24.4 us -> 0 us
  Pallas kernels: 0 us -> 19.3 us
  between operations: 16.7 us -> 0.66 us
  starting transfers between devices: 20.4 us -> 4.59 us
  local copies, waits for them, and re-layouts: 16.6 us -> 1.47 us
    psum x1 -> x0, waiting for transfers between devices: 258 us -> none  [per_device(): weight_total = lax.psum(weight_part, ('heads', 'ctx'))]
    all_gather x2 -> x0, waiting for transfers between devices: 158 us -> none  [the longest x1 91.7 us: prefix(): lax.all_gather(value.astype(jnp.bfloat16 if value.dtype == jnp.float32 el...]
    all_to_all x0 -> x6, blocking collectives: none -> 113 us  [swap(): return lax.all_to_all(value, axis, 0, 0, tiled=False)]
    add x64 -> x0, other arithmetic: 54.5 us -> none  [the longest x63 54.4 us: add_pair(): return earlier + later]
    dot_general x42 -> x0, matrix products: 24.4 us -> none  [the longest x10 9.52 us: product_cols(): lax.dot_general(left, right, (((0,), (0,)), ((), ())), preferred_element_...]
    ppermute x8 -> x0, starting transfers between devices: 20.3 us -> none  [shifted(): return lax.ppermute(value, axis, pairs)]
    pallas_call x0 -> x8, Pallas kernels: none -> 19.3 us  [the longest x1 5.74 us: per_device(): call(main_kernel, (queries.shape, BF16), ((shards, 3, *tile), BF16), ((le...]
    all_to_all x0 -> x1, waiting for transfers between devices: none -> 14.6 us  [swap(): return lax.all_to_all(value, axis, 0, 0, tiled=False)]
  transfers between devices with their start and end apart: 11 -> 1, of which waited for: 6 -> 1; matrix products, arithmetic and copies ran while one was open for 7% -> 0% of each run, Pallas kernels for 0% -> 0%
where the time goes in v1:
time: 155 us; the launch traced here: 154 us
  blocking collectives  113 us (73%)
  Pallas kernels  19.3 us (12%)
  waiting for transfers between devices  14.6 us (9%)
  starting transfers between devices  4.59 us (3%)
    all_to_all x6, blocking collectives, swap(): return lax.all_to_all(value, axis, 0, 0, tiled=False)  113 us
    all_to_all x1, waiting for transfers between devices, swap(): return lax.all_to_all(value, axis, 0, 0, tiled=False)  14.6 us
    pallas_call x1, Pallas kernels, per_device(): call(main_kernel, (queries.shape, BF16), ((shards, 3, *tile), BF16), ((le...  5.74 us
    all_to_all x1, starting transfers between devices, swap(): return lax.all_to_all(value, axis, 0, 0, tiled=False)  4.59 us
  transfers between devices with their start and end apart: 1, of which 1 were waited for; matrix products, arithmetic and copies ran while one was open for 0% of the time, Pallas kernels for 0%

profile of v1, /device:TPU:1, one launch (start us, length us, event | category | flops | bytes accessed | tf_op | source)
XLA Modules:
  0.0 154.1 jit_solution(16614147677295355925)
XLA Ops:
  0.6 2.2 %shard_map.111 = bf16[64,8,128]{2,1,0:T(8,128)(2,1)} custom-call(bf16[1,128,128]{2,1,0:T(8,128)(2,1)} %k_ref.5, bf16[1,128,128]{2,1,0:T(8,128)(2,1)} %v_ref.5, bf16[128,256]{1,0:T(8,128)(2,1)} %w_ref.5), custom_call_target="tpu_custom_call" | custom-call | tf_op jit(solution)/shard_map/pallas_call | solution.py:322
  2.8 22.9 %all_to_all.35.r_ref = bf16[64,8,128]{2,1,0:T(8,128)(2,1)} all-to-all(bf16[64,8,128]{2,1,0:T(8,128)(2,1)} %shard_map.111), channel_id=1, replica_groups=mesh['heads'=8,'ctx'=64] {'ctx'}, dimensions={0} | all-to-all | bytes 262144 | tf_op jit(solution)/shard_map/all_to_all | solution.py:312
  25.7 1.9 %shard_map.112 = bf16[64,3,8,128]{3,2,1,0:T(8,128)(2,1)} custom-call(bf16[64,8,128]{2,1,0:T(8,128)(2,1)} %all_to_all.35.r_ref), custom_call_target="tpu_custom_call" | custom-call | tf_op jit(solution)/shard_map/pallas_call | solution.py:323
  27.5 0.0 copy-start.1
  27.5 4.6 %all-to-all-start.1 = ((bf16[64,3,8,128]{3,2,1,0:T(8,128)(2,1)}), bf16[64,3,8,128]{3,2,1,0:T(8,128)(2,1)S(1)}, u32[]{:S(2)}, u32[]{:S(2)}) async-start(bf16[64,3,8,128]{3,2,1,0:T(8,128)(2,1)} %shard_map.112), calls=%async_computation.1 | async-start | bytes 786432 | tf_op jit(solution)/shard_map/all_to_all | solution.py:312
  32.1 0.0 copy-done.1
  32.1 0.7 copy.12.kb_ref
  32.8 14.6 %all-to-all-done.1.r_ref = bf16[64,3,8,128]{3,2,1,0:T(8,128)(2,1)S(1)} async-done(((bf16[64,3,8,128]{3,2,1,0:T(8,128)(2,1)}), bf16[64,3,8,128]{3,2,1,0:T(8,128)(2,1)S(1)}, u32[]{:S(2)}, u32[]{:S(2)}) %all-to-all-start.1) | async-done | bytes 393248 | tf_op jit(solution)/shard_map/all_to_all | solution.py:312
  47.5 0.0 copy-start
  47.5 0.8 copy-done
  48.2 5.7 %shard_map.113 = (bf16[1,128,512]{2,1,0:T(8,128)(2,1)}, bf16[64,3,8,128]{3,2,1,0:T(8,128)(2,1)}, f32[128,256]{1,0:T(8,128)}, f32[128,128]{1,0:T(8,128)}, f32[128,128]{1,0:T(8,128)}, /*index=5*/f32[128,256]{1,0:T(8,128)}) custom-call(bf16[1,128,512]{2,1,0:T(8,128)(2,1)} %q_ref.1, bf16[1,128,128]{2,1,0:T(8,128)(2,1)} %k_ref.5, bf16[1,128,128]{2,1,0:T(8,128)(2,1)} %v_ref.5, ...), custom_call_target="tpu_custom_call" | custom-call | tf_op jit(solution)/shard_map/pallas_call | solution.py:324
  53.9 20.7 %all_to_all.36.r_ref = bf16[64,3,8,128]{3,2,1,0:T(8,128)(2,1)} all-to-all(bf16[64,3,8,128]{3,2,1,0:T(8,128)(2,1)} %get-tuple-element.14), channel_id=1, replica_groups=mesh['heads'=8,'ctx'=64] {'ctx'}, dimensions={0} | all-to-all | bytes 786432 | tf_op jit(solution)/shard_map/all_to_all | solution.py:312
  74.6 1.9 %shard_map.114 = f32[64,8,128]{2,1,0:T(8,128)} custom-call(bf16[64,3,8,128]{3,2,1,0:T(8,128)(2,1)} %all_to_all.36.r_ref), custom_call_target="tpu_custom_call" | custom-call | tf_op jit(solution)/shard_map/pallas_call | solution.py:336
  76.5 18.6 %all_to_all.37.r_ref = f32[64,8,128]{2,1,0:T(8,128)} all-to-all(f32[64,8,128]{2,1,0:T(8,128)} %shard_map.114), channel_id=1, replica_groups=mesh['heads'=8,'ctx'=64] {'ctx'}, dimensions={0} | all-to-all | bytes 524288 | tf_op jit(solution)/shard_map/all_to_all | solution.py:312
  95.1 2.9 %shard_map.115 = (bf16[1,128,128]{2,1,0:T(8,128)(2,1)}, bf16[1,128,128]{2,1,0:T(8,128)(2,1)}, bf16[64,8,128]{2,1,0:T(8,128)(2,1)}) custom-call(bf16[1,128,128]{2,1,0:T(8,128)(2,1)} %k_ref.5, bf16[1,128,128]{2,1,0:T(8,128)(2,1)} %v_ref.5, bf16[128,256]{1,0:T(8,128)(2,1)} %w_ref.5, f32[64,8,128]{2,1,0:T(8,128)} %all_to_all.37.r_ref, ...), custom_call_target="tpu_custom_call" | custom-call | tf_op jit(solution)/shard_map/pallas_call | solution.py:337
  98.0 16.4 %all_to_all.38.r_ref = bf16[64,8,128]{2,1,0:T(8,128)(2,1)} all-to-all(bf16[64,8,128]{2,1,0:T(8,128)(2,1)} %get-tuple-element.21), channel_id=1, replica_groups=mesh['heads'=8,'ctx'=64] {'ctx'}, dimensions={0} | all-to-all | bytes 262144 | tf_op jit(solution)/shard_map/all_to_all | solution.py:312
  114.3 1.6 %shard_map.116 = f32[8,8,128]{2,1,0:T(8,128)} custom-call(bf16[64,8,128]{2,1,0:T(8,128)(2,1)} %all_to_all.38.r_ref), custom_call_target="tpu_custom_call" | custom-call | tf_op jit(solution)/shard_map/pallas_call | solution.py:342
  115.9 17.0 %all_to_all.39.r_ref = f32[8,8,128]{2,1,0:T(8,128)} all-to-all(f32[8,8,128]{2,1,0:T(8,128)} %shard_map.116), channel_id=1, replica_groups=mesh['heads'=8,'ctx'=64] {'heads'}, dimensions={0} | all-to-all | bytes 65536 | tf_op jit(solution)/shard_map/all_to_all | solution.py:312
  133.0 1.4 shard_map.117
  134.4 17.9 %all_to_all.40.r_ref = bf16[64,8,128]{2,1,0:T(8,128)(2,1)} all-to-all(bf16[64,8,128]{2,1,0:T(8,128)(2,1)} %shard_map.117), channel_id=1, replica_groups=mesh['heads'=8,'ctx'=64] {'ctx'}, dimensions={0} | all-to-all | bytes 262144 | tf_op jit(solution)/shard_map/all_to_all | solution.py:312
  152.3 1.8 %shard_map.118 = f32[128,256]{1,0:T(8,128)} custom-call(bf16[64,8,128]{2,1,0:T(8,128)(2,1)} %all_to_all.40.r_ref), custom_call_target="tpu_custom_call" | custom-call | tf_op jit(solution)/shard_map/pallas_call | solution.py:344
Async XLA Ops:
  27.5 4.6 %copy-start.1 = (s32[1,64,4]{1,2,0:T(4,128)S(1)}, s32[1,64,4]{1,2,0:T(4,128)}, u32[]{:S(2)}) copy-start(s32[1,64,4]{1,2,0:T(4,128)} %param.14) | copy-start | bytes 3076
  27.5 19.9 %all-to-all-start.1 = ((bf16[64,3,8,128]{3,2,1,0:T(8,128)(2,1)}), bf16[64,3,8,128]{3,2,1,0:T(8,128)(2,1)S(1)}, u32[]{:S(2)}, u32[]{:S(2)}) async-start(bf16[64,3,8,128]{3,2,1,0:T(8,128)(2,1)} %shard_map.112), calls=%async_computation.1 | async-start | bytes 786432 | tf_op jit(solution)/shard_map/all_to_all | solution.py:312
  47.5 0.8 copy-start

commit v2 on v1

--- a/solution.py
+++ b/solution.py
@@ -184,11 +184,13 @@
     key_far = flat(r_ref[:, 1].astype(F32)).astype(BF16)
     value_far = flat(r_ref[:, 2].astype(F32)).astype(BF16)
     far = key_far.shape[0]
-    listed = kb_ref[0, pl.ds(shard, 1), :]
+    table = kb_ref[0]
+    column = lax.broadcasted_iota(jnp.int32, table.shape, 1)
+    listed = jnp.max(jnp.where(column == shard, table, -1), axis=1, keepdims=True)
     place = (lax.broadcasted_iota(jnp.int32, (1, far), 1) & 7) >> 1
     live = jnp.zeros((1, far), F32)
-    for reach in range(listed.shape[1]):
-        here = jnp.where(listed[:, reach : reach + 1] >= 0, 1.0, 0.0)
+    for reach in range(listed.shape[0]):
+        here = jnp.where(listed[reach : reach + 1] >= 0, 1.0, 0.0)
         live = jnp.where(place == reach, here, live)
     near_logits = jnp.where(causal, scaling * nt(queries, keys), -jnp.inf)
     far_logits = jnp.where(live > 0.5, scaling * nt(queries, key_far), -jnp.inf)
@@ -299,13 +301,21 @@
     o_ref[:, size:] = pair[length:]
 
 
-def call(kernel, *outs):
+def call(kernel, *outs, grant=8):
     shapes = [jax.ShapeDtypeStruct(shape, dtype) for shape, dtype in outs]
-    return pl.pallas_call(
-        kernel,
-        out_shape=shapes if len(shapes) > 1 else shapes[0],
-        interpret=INTERPRET,
-    )
+    spec = pl.BlockSpec(memory_space=pltpu.VMEM)
+
+    def run(*operands):
+        return pl.pallas_call(
+            kernel,
+            out_shape=shapes if len(shapes) > 1 else shapes[0],
+            in_specs=[spec] * len(operands),
+            out_specs=[spec] * len(shapes) if len(shapes) > 1 else spec,
+            interpret=INTERPRET,
+            compiler_params=pltpu.CompilerParams(vmem_limit_bytes=grant << 20),
+        )(*operands)
+
+    return run
 
 
 def swap(value, axis):
@@ -329,8 +339,10 @@
         ((length, size), F32),
         ((length, size), F32),
         ((size, features_n), F32),
+        grant=24,
     )(
-        queries, keys, values, out_grad, gain_lin, gain_sparse, key_blocks, w_feat,
+        queries, keys, values, out_grad, gain_lin, gain_sparse,
+        jnp.swapaxes(key_blocks, 1, 2), w_feat,
         swap(got, "ctx"),
     )
     got = call(suffix_kernel, ((shards, *tile), F32))(swap(sent, "ctx"))

time: 155 us -> 140 us (0.903)
  blocking collectives: 113 us -> 129 us
  waiting for transfers between devices: 14.6 us -> 0 us
  Pallas kernels: 19.3 us -> 7.42 us
  starting transfers between devices: 4.59 us -> 0 us
    all_to_all x6 -> x7, blocking collectives: 113 us -> 129 us  [swap(): return lax.all_to_all(value, axis, 0, 0, tiled=False)]
    all_to_all x1 -> x0, waiting for transfers between devices: 14.6 us -> none  [swap(): return lax.all_to_all(value, axis, 0, 0, tiled=False)]
    pallas_call x8, Pallas kernels: 19.3 us -> 7.42 us  [run(): pl.pallas_call(kernel, out_shape=shapes if len(shapes) > 1 else shapes[0]...]
    all_to_all x1 -> x0, starting transfers between devices: 4.59 us -> none  [swap(): return lax.all_to_all(value, axis, 0, 0, tiled=False)]
  transfers between devices with their start and end apart: 1 -> 0, of which waited for: 1 -> 0; matrix products, arithmetic and copies ran while one was open for 0% -> 0% of each run, Pallas kernels for 0% -> 0%
where the time goes in v2:
time: 140 us
  blocking collectives  129 us (92%)
  Pallas kernels  7.42 us (5%)
  local copies, waits for them, and re-layouts  2.4 us (2%)
    all_to_all x7, blocking collectives, swap(): return lax.all_to_all(value, axis, 0, 0, tiled=False)  129 us
    pallas_call x8, Pallas kernels, run(): pl.pallas_call(kernel, out_shape=shapes if len(shapes) > 1 else shapes[0]...  7.42 us

profile of v2, /device:TPU:1, one launch (start us, length us, event | category | flops | bytes accessed | tf_op | source)
XLA Modules:
  0.0 139.6 jit_solution(6592571819234307132)
XLA Ops:
  0.6 0.0 copy-start
  0.6 0.8 copy-done
  1.5 0.0 copy-start.2
  1.5 0.8 copy-done.2
  2.2 0.0 copy-start.4
  2.2 0.8 copy-done.4
  3.0 0.6 shard_map.111
  3.6 22.5 %all_to_all.35.r_ref = bf16[64,8,128]{2,1,0:T(8,128)(2,1)S(1)} all-to-all(bf16[64,8,128]{2,1,0:T(8,128)(2,1)S(1)} %shard_map.111), channel_id=1, replica_groups=mesh['heads'=8,'ctx'=64] {'ctx'}, dimensions={0} | all-to-all | bytes 262144 | tf_op jit(solution)/shard_map/all_to_all | solution.py:322
  26.1 0.2 shard_map.112
  26.3 0.0 copy-start.1
  26.3 0.0 copy-start.3
  26.4 0.0 copy-start.5
  26.4 0.0 copy-start.6
  26.4 0.0 copy-start.7
  26.4 0.0 copy-start.8
  26.4 0.0 copy-start.9
  26.4 0.0 copy-start.10
  26.4 19.1 %all_to_all.36.r_ref = bf16[64,3,8,128]{3,2,1,0:T(8,128)(2,1)S(1)} all-to-all(bf16[64,3,8,128]{3,2,1,0:T(8,128)(2,1)S(1)} %shard_map.112), channel_id=1, replica_groups=mesh['heads'=8,'ctx'=64] {'ctx'}, dimensions={0} | all-to-all | bytes 786432 | tf_op jit(solution)/shard_map/all_to_all | solution.py:322
  45.5 0.0 copy-done.1
  45.5 0.0 copy-done.3
  45.5 0.0 copy-done.5
  45.5 0.0 copy-done.6
  45.6 0.0 copy-done.7
  45.6 0.0 copy-done.8
  45.6 0.0 copy-done.9
  45.6 0.0 copy-done.10
  45.6 4.1 %shard_map.113 = (bf16[1,128,512]{2,1,0:T(8,128)(2,1)}, bf16[64,3,8,128]{3,2,1,0:T(8,128)(2,1)S(1)}, f32[128,256]{1,0:T(8,128)S(1)}, f32[128,128]{1,0:T(8,128)S(...) custom-call(bf16[1,128,512]{2,1,0:T(8,128)(2,1)S(1)} %copy-done.6, bf16[1,128,128]{2,1,0:T(8,128)(2,1)S(1)} %copy-done.3, ...), custom_call_target="tpu_custom_call" | custom-call | tf_op jit(solution)/shard_map/pallas_call | solution.py:309
  49.7 20.4 %all_to_all.37.r_ref = bf16[64,3,8,128]{3,2,1,0:T(8,128)(2,1)S(1)} all-to-all(bf16[64,3,8,128]{3,2,1,0:T(8,128)(2,1)S(1)} %get-tuple-element.14), channel_id=1, replica_groups=mesh['heads'=8,'ctx'=64] {'ctx'}, dimensions={0} | all-to-all | bytes 786432 | tf_op jit(solution)/shard_map/all_to_all | solution.py:322
  70.1 0.2 shard_map.114
  70.3 18.3 %all_to_all.38.r_ref = f32[64,8,128]{2,1,0:T(8,128)S(1)} all-to-all(f32[64,8,128]{2,1,0:T(8,128)S(1)} %shard_map.114), channel_id=1, replica_groups=mesh['heads'=8,'ctx'=64] {'ctx'}, dimensions={0} | all-to-all | bytes 524288 | tf_op jit(solution)/shard_map/all_to_all | solution.py:322
  88.6 1.3 shard_map.115
  89.9 15.7 %all_to_all.39.r_ref = bf16[64,8,128]{2,1,0:T(8,128)(2,1)S(1)} all-to-all(bf16[64,8,128]{2,1,0:T(8,128)(2,1)S(1)} %get-tuple-element.21), channel_id=1, replica_groups=mesh['heads'=8,'ctx'=64] {'ctx'}, dimensions={0} | all-to-all | bytes 262144 | tf_op jit(solution)/shard_map/all_to_all | solution.py:322
  105.6 0.1 shard_map.116
  105.7 16.8 %all_to_all.40.r_ref = f32[8,8,128]{2,1,0:T(8,128)S(1)} all-to-all(f32[8,8,128]{2,1,0:T(8,128)S(1)} %shard_map.116), channel_id=1, replica_groups=mesh['heads'=8,'ctx'=64] {'heads'}, dimensions={0} | all-to-all | bytes 65536 | tf_op jit(solution)/shard_map/all_to_all | solution.py:322
  122.5 16.2 %all_to_all.41.r_ref = bf16[64,8,128]{2,1,0:T(8,128)(2,1)S(1)} all-to-all(bf16[64,8,128]{2,1,0:T(8,128)(2,1)S(1)} %shard_map.117), channel_id=1, replica_groups=mesh['heads'=8,'ctx'=64] {'ctx'}, dimensions={0} | all-to-all | bytes 262144 | tf_op jit(solution)/shard_map/all_to_all | solution.py:322
  138.7 0.9 shard_map.118
  (1 shorter events, 0.0 us)
Async XLA Ops:
  0.6 0.8 copy-start
  1.5 0.8 copy-start.2
  2.2 0.8 copy-start.4
  26.3 19.2 %copy-start.1 = (bf16[128,256]{1,0:T(8,128)(2,1)S(1)}, bf16[128,256]{1,0:T(8,128)(2,1)}, u32[]{:S(2)}) copy-start(bf16[128,256]{1,0:T(8,128)(2,1)} %w_ref.5) | copy-start | bytes 196612
  26.3 19.2 %copy-start.3 = (bf16[1,128,128]{2,1,0:T(8,128)(2,1)S(1)}, bf16[1,128,128]{2,1,0:T(8,128)(2,1)}, u32[]{:S(2)}) copy-start(bf16[1,128,128]{2,1,0:T(8,128)(2,1)} %k_ref.5) | copy-start | bytes 98308
  26.4 19.2 %copy-start.5 = (bf16[1,128,128]{2,1,0:T(8,128)(2,1)S(1)}, bf16[1,128,128]{2,1,0:T(8,128)(2,1)}, u32[]{:S(2)}) copy-start(bf16[1,128,128]{2,1,0:T(8,128)(2,1)} %v_ref.5) | copy-start | bytes 98308
  26.4 19.2 %copy-start.6 = (bf16[1,128,512]{2,1,0:T(8,128)(2,1)S(1)}, bf16[1,128,512]{2,1,0:T(8,128)(2,1)}, u32[]{:S(2)}) copy-start(bf16[1,128,512]{2,1,0:T(8,128)(2,1)} %q_ref.1) | copy-start | bytes 393220
  26.4 19.2 %copy-start.7 = (bf16[1,128,512]{2,1,0:T(8,128)(2,1)S(1)}, bf16[1,128,512]{2,1,0:T(8,128)(2,1)}, u32[]{:S(2)}) copy-start(bf16[1,128,512]{2,1,0:T(8,128)(2,1)} %g_ref.1) | copy-start | bytes 393220
  26.4 19.2 %copy-start.8 = (f32[1,512]{1,0:T(1,128)S(1)}, f32[1,512]{1,0:T(1,128)}, u32[]{:S(2)}) copy-start(f32[1,512]{1,0:T(1,128)} %gl_ref.1) | copy-start | bytes 6148
  26.4 19.2 %copy-start.9 = (f32[1,512]{1,0:T(1,128)S(1)}, f32[1,512]{1,0:T(1,128)}, u32[]{:S(2)}) copy-start(f32[1,512]{1,0:T(1,128)} %gs_ref.1) | copy-start | bytes 6148
  26.4 19.2 %copy-start.10 = (s32[1,64,4]{1,2,0:T(4,128)S(1)}, s32[1,64,4]{1,2,0:T(4,128)}, u32[]{:S(2)}) copy-start(s32[1,64,4]{1,2,0:T(4,128)} %param.14) | copy-start | bytes 3076

commit v3 on v2

v3 whole, which is shorter than its diff:
```python
import jax
import jax.numpy as jnp
from jax import lax
from jax.experimental import pallas as pl
from jax.experimental.pallas import tpu as pltpu
from jax.sharding import PartitionSpec as P

INTERPRET = False
EPS = 1e-06
F32 = jnp.float32
BF16 = jnp.bfloat16


def nn(a, b):
    return lax.dot_general(a, b, (((1,), (0,)), ((), ())), preferred_element_type=F32)


def nt(a, b):
    return lax.dot_general(a, b, (((1,), (1,)), ((), ())), preferred_element_type=F32)


def tn(a, b):
    return lax.dot_general(a, b, (((0,), (0,)), ((), ())), preferred_element_type=F32)


def iotas(shape):
    return (
        lax.broadcasted_iota(jnp.int32, shape, 0),
        lax.broadcasted_iota(jnp.int32, shape, 1),
    )


def ones_where(mask):
    return jnp.where(mask, 1.0, 0.0).astype(BF16)


def features(raw):
    low = jnp.exp(jnp.minimum(raw, 0.0))
    up = raw > 0
    return jnp.where(up, raw + 1.0, low), jnp.where(up, 1.0, low)


def norm_backward(value, upstream):
    inverse = lax.rsqrt(jnp.mean(value * value, axis=-1, keepdims=True) + EPS)
    projected = jnp.mean(upstream * value, axis=-1, keepdims=True)
    return inverse * upstream - value * (inverse * inverse * inverse) * projected


def split(value):
    high = value.astype(BF16)
    return high, (value - high.astype(F32)).astype(BF16)

SIDE = 8


def spots():
    shard = lax.axis_index("ctx")
    return shard // SIDE, shard % SIDE, shard


def flag(condition):
    return jnp.where(condition, 1.0, 0.0).astype(F32)


def pieces(value):
    return value.reshape(SIDE, value.shape[0] // SIDE, value.shape[1])


def whole(value):
    return value.reshape(value.shape[0] * value.shape[1], value.shape[2])


def store_split(ref, at, value):
    step = value.shape[1]
    high, low = split(value)
    ref[:, at : at + step] = high
    ref[:, at + step : at + 2 * step] = low


def send_state_kernel(k_ref, v_ref, w_ref, o_ref):
    keys = k_ref[0]
    values = v_ref[0]
    feat = features(nn(keys, w_ref[...]))[0].astype(BF16)
    total = pieces(tn(feat, values).astype(BF16))
    step, length = total.shape[1], keys.shape[0]
    o_ref[:, :step] = total
    for spot in range(SIDE):
        o_ref[spot, step : step + length] = keys
        o_ref[spot, step + length :] = values


def row_total_kernel(r_ref, o_ref, kv_ref):
    step = o_ref.shape[1]
    total = jnp.sum(r_ref[:, :step].astype(F32), axis=0)
    o_ref[...] = jnp.broadcast_to(total[None], o_ref.shape)
    kv_ref[...] = r_ref[SIDE // 2 :, step:]


def prefix_kernel(r_ref, c_ref, o_ref):
    step = c_ref.shape[1]
    line = spots()[0]
    total = jnp.zeros(c_ref.shape[1:], F32)
    for source in range(SIDE):
        total = total + flag(source < line) * c_ref[source]
    for spot in range(SIDE):
        o_ref[spot, :step], o_ref[spot, step:] = split(total)
        total = total + r_ref[spot, :step].astype(F32)


def main_kernel(
    q_ref, k_ref, v_ref, g_ref, gl_ref, gs_ref, kb_ref, w_ref, row_ref, prev_ref, r_ref,
    qo_ref, send_ref, up_ref, back_ref, kloc_ref, dk_ref, dv_ref,
):
    spot, shard = spots()[1:]
    keys = k_ref[0]
    values = v_ref[0]
    w = w_ref[...]
    length, size = keys.shape
    heads = q_ref.shape[2] // size
    scaling = size ** (-0.5)
    rows = heads * length
    step = r_ref.shape[1] // 2

    def stacked(ref):
        return jnp.concatenate(
            [ref[0, :, h * size : (h + 1) * size] for h in range(heads)], axis=0
        )

    def gains(ref):
        return jnp.concatenate(
            [
                jnp.broadcast_to(ref[:, h * size : (h + 1) * size], (length, size))
                for h in range(heads)
            ],
            axis=0,
        )

    queries = stacked(q_ref)
    upstream = stacked(g_ref).astype(F32)

    state_high = whole(r_ref[:, :step])
    state_low = whole(r_ref[:, step:])
    raw = nn(queries, w)
    feat, slope = features(raw)
    feat = feat.astype(BF16)
    key_feat, key_slope = features(nn(keys, w))
    key_feat = key_feat.astype(BF16)
    row, col = iotas((rows, length))
    causal = (row & (length - 1)) >= col
    weights = jnp.where(causal, nt(feat, key_feat), 0.0).astype(BF16)
    lin_out = nn(feat, state_high) + nn(feat, state_low) + nn(weights, values)
    lin_grad = norm_backward(lin_out, upstream * gains(gl_ref))
    lin_high, lin_low = split(lin_grad)
    score_grad = jnp.where(causal, nt(lin_high, values), 0.0).astype(BF16)
    feat_grad = (
        nt(lin_high, state_high)
        + nt(lin_high, state_low)
        + nt(lin_low, state_high)
        + nn(score_grad, key_feat)
    )
    raw_grad = (feat_grad * slope).astype(BF16)
    query_lin = nt(raw_grad, w)
    key_local = tn(score_grad, feat)
    kloc_ref[...] = key_local
    value_local = tn(weights, lin_high)
    send_ref[:, :step] = pieces(tn(feat, lin_high) + tn(feat, lin_low)).astype(BF16)
    local_high, local_low = split(key_local * key_slope)
    early = tn(raw_grad, queries) + tn(local_high, keys) + tn(local_low, keys)
    store_split(send_ref, step, pieces(early))

    reaches = kb_ref.shape[1]
    table = kb_ref[0]
    column = lax.broadcasted_iota(jnp.int32, table.shape, 1)
    listed = jnp.max(jnp.where(column == shard, table, -1), axis=1, keepdims=True)
    far = []
    live = []
    for reach in range(1, reaches + 1):
        own = row_ref[jnp.maximum(spot - reach, 0), step:].astype(F32)
        other = prev_ref[jnp.clip(spot - reach + SIDE // 2, 0, SIDE // 2 - 1)].astype(F32)
        inside = flag(spot >= reach)
        far.append((inside * own + (1.0 - inside) * other).astype(BF16))
        here = jnp.where(listed[reach - 1 : reach] >= 0, 1.0, 0.0)
        live.append(jnp.broadcast_to(here, (1, length)))
    key_far = jnp.concatenate([item[:length] for item in far], axis=0)
    value_far = jnp.concatenate([item[length:] for item in far], axis=0)
    live = jnp.concatenate(live, axis=1)
    near_logits = jnp.where(causal, scaling * nt(queries, keys), -jnp.inf)
    far_logits = jnp.where(live > 0.5, scaling * nt(queries, key_far), -jnp.inf)
    top = jnp.maximum(
        jnp.max(near_logits, axis=1, keepdims=True), jnp.max(far_logits, axis=1, keepdims=True)
    )
    near_exp = jnp.exp(near_logits - top)
    far_exp = jnp.exp(far_logits - top)
    norm = 1.0 / (
        jnp.sum(near_exp, axis=1, keepdims=True) + jnp.sum(far_exp, axis=1, keepdims=True)
    )
    near_probs = near_exp * norm
    far_probs = far_exp * norm
    near_half = near_probs.astype(BF16)
    far_half = far_probs.astype(BF16)
    sparse_out = nn(near_half, values) + nn(far_half, value_far)
    sparse_grad = norm_backward(sparse_out, upstream * gains(gs_ref)).astype(BF16)
    inner = jnp.sum(sparse_grad.astype(F32) * sparse_out, axis=1, keepdims=True)
    near_grad = (scaling * near_probs * (nt(sparse_grad, values) - inner)).astype(BF16)
    far_grad = (scaling * far_probs * (nt(sparse_grad, value_far) - inner)).astype(BF16)
    query_out = nn(near_grad, keys) + nn(far_grad, key_far) + query_lin
    for h in range(heads):
        qo_ref[0, :, h * size : (h + 1) * size] = query_out[
            h * length : (h + 1) * length
        ].astype(BF16)
    dk_ref[...] = tn(near_grad, queries)
    dv_ref[...] = tn(near_half, sparse_grad) + value_local
    key_back = tn(far_grad, queries).astype(BF16)
    value_back = tn(far_half, sparse_grad).astype(BF16)
    up_ref[...] = jnp.zeros(up_ref.shape, BF16)
    back_ref[...] = jnp.zeros(back_ref.shape, BF16)
    for reach in range(1, reaches + 1):
        part = slice((reach - 1) * length, reach * length)

        @pl.when(spot >= reach)
        def _():
            up_ref[spot - reach, :length] = key_back[part]
            up_ref[spot - reach, length:] = value_back[part]

        @pl.when(spot < reach)
        def _():
            back_ref[spot - reach + SIDE // 2, :length] = key_back[part]
            back_ref[spot - reach + SIDE // 2, length:] = value_back[part]


def cot_total_kernel(r_ref, o_ref):
    step = o_ref.shape[1]
    total = jnp.sum(r_ref[:, :step].astype(F32), axis=0)
    o_ref[...] = jnp.broadcast_to(total[None], o_ref.shape)


def weight_part_kernel(row_ref, w_ref, r_ref, c_ref, send_ref, o_ref):
    line, spot = spots()[:2]
    step, size = c_ref.shape[1:]
    length = (row_ref.shape[1] - step) // 2
    w = w_ref[...]
    row, col = iotas((step, w.shape[1]))
    own = nt(ones_where(col == row + step * spot), w).astype(BF16)
    total = jnp.zeros(c_ref.shape[1:], F32)
    for source in range(SIDE):
        total = total + flag(source > line) * c_ref[source]
    weight = jnp.zeros(c_ref.shape[1:], F32)
    for source in range(SIDE - 1, -1, -1):
        high, low = split(total)
        o_ref[source, :step] = high
        o_ref[source, step:] = low
        keys = row_ref[source, step : step + length]
        values = row_ref[source, step + length :]
        slope = features(nt(own, keys))[1]
        grad_high, grad_low = split((nt(high, values) + nt(low, values)) * slope)
        weight = weight + nn(grad_high, keys) + nn(grad_low, keys)
        for place in (1, 2):
            weight = weight + r_ref[source, place * step : (place + 1) * step].astype(F32)
        total = total + r_ref[source, :step].astype(F32)
    send_ref[...] = jnp.broadcast_to(weight[None], send_ref.shape)


def column_sum_kernel(r_ref, o_ref):
    o_ref[...] = jnp.broadcast_to(jnp.sum(r_ref[...], axis=0)[None], o_ref.shape)


def make_last_kernel(scale):
    def last_kernel(r_ref, carried_ref, up_ref, back_ref, o_ref):
        step = r_ref.shape[1]
        high, low = split(jnp.sum(r_ref[...], axis=0) * scale)
        o_ref[:, : 2 * step] = carried_ref[...]
        o_ref[:, 2 * step : 3 * step] = jnp.broadcast_to(high[None], (SIDE, *high.shape))
        o_ref[:, 3 * step : 4 * step] = jnp.broadcast_to(low[None], (SIDE, *low.shape))
        o_ref[: SIDE // 2, 4 * step :] = up_ref[: SIDE // 2]
        both = up_ref[SIDE // 2 :].astype(F32) + back_ref[...].astype(F32)
        o_ref[SIDE // 2 :, 4 * step :] = both.astype(BF16)

    return last_kernel


def key_kernel(
    k_ref, v_ref, w_ref, r_ref, kloc_ref, dk_ref, dv_ref, ko_ref, vo_ref, wo_ref
):
    keys = k_ref[0]
    values = v_ref[0]
    w = w_ref[...]
    step = w.shape[1] // SIDE
    length = keys.shape[0]
    carried_high = whole(r_ref[:, :step])
    carried_low = whole(r_ref[:, step : 2 * step])
    weight = whole(r_ref[:, 2 * step : 3 * step]).astype(F32)
    weight = weight + whole(r_ref[:, 3 * step : 4 * step]).astype(F32)
    wo_ref[...] = weight.T
    back = jnp.sum(r_ref[:, 4 * step :].astype(F32), axis=0)
    feat, slope = features(nn(keys, w))
    feat = feat.astype(BF16)
    feat_grad = nt(values, carried_high) + nt(values, carried_low) + kloc_ref[...]
    raw_grad = (feat_grad * slope).astype(BF16)
    ko_ref[0] = (dk_ref[...] + back[:length] + nt(raw_grad, w)).astype(BF16)
    vo_ref[0] = (
        dv_ref[...] + back[length:] + nn(feat, carried_high) + nn(feat, carried_low)
    ).astype(BF16)


def call(kernel, *outs, grant=8):
    shapes = [jax.ShapeDtypeStruct(shape, dtype) for shape, dtype in outs]
    spec = pl.BlockSpec(memory_space=pltpu.VMEM)

    def run(*operands):
        return pl.pallas_call(
            kernel,
            out_shape=shapes if len(shapes) > 1 else shapes[0],
            in_specs=[spec] * len(operands),
            out_specs=[spec] * len(shapes) if len(shapes) > 1 else spec,
            interpret=INTERPRET,
            compiler_params=pltpu.CompilerParams(vmem_limit_bytes=grant << 20),
        )(*operands)

    return run


def swap(value, axis, groups=None):
    return lax.all_to_all(value, axis, 0, 0, axis_index_groups=groups, tiled=False)


def per_device(queries, keys, values, out_grad, gain_lin, gain_sparse, key_blocks, w_feat):
    shards = lax.axis_size("ctx")
    groups = lax.axis_size("heads")
    length, size = keys.shape[1:]
    features_n = w_feat.shape[1]
    scale = (queries.shape[0] * groups * length * shards) ** (-0.5)
    step = features_n // SIDE
    in_row = [[line * SIDE + spot for spot in range(SIDE)] for line in range(shards // SIDE)]
    in_column = [[line * SIDE + spot for line in range(shards // SIDE)] for spot in range(SIDE)]
    half = (SIDE // 2, 2 * length, size)
    piece = (SIDE, step, size)
    two = (SIDE, 2 * step, size)
    down = [(i, i + SIDE) for i in range(shards - SIDE)]
    sent = call(send_state_kernel, ((SIDE, step + 2 * length, size), BF16))(keys, values, w_feat)
    row = swap(sent, "ctx", in_row)
    sent, moved = call(row_total_kernel, (piece, F32), (half, BF16))(row)
    previous = lax.ppermute(moved, "ctx", down)
    sent = call(prefix_kernel, (two, BF16))(row, swap(sent, "ctx", in_column))
    query_out, sent, up, back, key_local, key_near, value_near = call(
        main_kernel,
        (queries.shape, BF16),
        ((SIDE, 3 * step, size), BF16),
        ((SIDE, 2 * length, size), BF16),
        (half, BF16),
        ((length, features_n), F32),
        ((length, size), F32),
        ((length, size), F32),
        grant=24,
    )(
        queries, keys, values, out_grad, gain_lin, gain_sparse,
        jnp.swapaxes(key_blocks, 1, 2), w_feat, row, previous, swap(sent, "ctx", in_row),
    )
    returned = lax.ppermute(back, "ctx", [(b, a) for a, b in down])
    cots = swap(sent, "ctx", in_row)
    sent = call(cot_total_kernel, (piece, F32))(cots)
    sent, carried = call(weight_part_kernel, (piece, F32), (two, BF16))(
        row, w_feat, cots, swap(sent, "ctx", in_column)
    )
    sent = call(column_sum_kernel, ((groups, step, size), F32))(swap(sent, "ctx", in_column))
    sent = call(make_last_kernel(scale), ((SIDE, 4 * step + 2 * length, size), BF16))(
        swap(sent, "heads"), carried, up, returned
    )
    key_out, value_out, weight = call(
        key_kernel, (keys.shape, BF16), (values.shape, BF16), (w_feat.shape, F32)
    )(keys, values, w_feat, swap(sent, "ctx", in_row), key_local, key_near, value_near)
    return query_out, key_out, value_out, weight


def solution(mesh):
    sharded = P("heads", "ctx", None)
    return jax.shard_map(
        per_device,
        mesh=mesh,
        in_specs=(
            sharded,
            sharded,
            sharded,
            sharded,
            P("heads", None),
            P("heads", None),
            P("heads", None, None),
            P(),
        ),
        out_specs=(sharded, sharded, sharded, P()),
        check_vma=False,
    )
```

time: 140 us -> 124 us (0.89)
  blocking collectives: 129 us -> 58.1 us
  starting transfers between devices: 0 us -> 27.4 us
  waiting for transfers between devices: 0 us -> 24.2 us
  Pallas kernels: 7.42 us -> 10.2 us
    all_to_all x7 -> x4, blocking collectives: 129 us -> 58.1 us  [swap(): lax.all_to_all(value, axis, 0, 0, axis_index_groups=groups, tiled=False)]
    all_to_all x0 -> x4, waiting for transfers between devices: none -> 24.2 us  [swap(): lax.all_to_all(value, axis, 0, 0, axis_index_groups=groups, tiled=False)]
    all_to_all x0 -> x4, starting transfers between devices: none -> 22.9 us  [swap(): lax.all_to_all(value, axis, 0, 0, axis_index_groups=groups, tiled=False)]
    ppermute x0 -> x2, starting transfers between devices: none -> 4.56 us  [the longest x1 3.27 us: per_device(): previous = lax.ppermute(moved, 'ctx', down)]
    pallas_call x8 -> x9, Pallas kernels: 7.42 us -> 10.2 us  [run(): pl.pallas_call(kernel, out_shape=shapes if len(shapes) > 1 else shapes[0]...]
  transfers between devices with their start and end apart: 0 -> 6, of which waited for: 0 -> 4; matrix products, arithmetic and copies ran while one was open for 0% -> 0% of each run, Pallas kernels for 0% -> 1%
where the time goes in v3:
time: 124 us; the launch traced here: 123 us
  blocking collectives  58.1 us (47%)
  starting transfers between devices  27.4 us (22%)
  waiting for transfers between devices  24.2 us (20%)
  Pallas kernels  10.2 us (8%)
  local copies, waits for them, and re-layouts  2.38 us (2%)
    all_to_all x4, blocking collectives, swap(): lax.all_to_all(value, axis, 0, 0, axis_index_groups=groups, tiled=False)  58.1 us
    all_to_all x4, waiting for transfers between devices, swap(): lax.all_to_all(value, axis, 0, 0, axis_index_groups=groups, tiled=False)  24.2 us
    all_to_all x4, starting transfers between devices, swap(): lax.all_to_all(value, axis, 0, 0, axis_index_groups=groups, tiled=False)  22.9 us
    pallas_call x9, Pallas kernels, run(): pl.pallas_call(kernel, out_shape=shapes if len(shapes) > 1 else shapes[0]...  10.2 us
    ppermute x1, starting transfers between devices, per_device(): previous = lax.ppermute(moved, 'ctx', down)  3.27 us
  transfers between devices with their start and end apart: 6, of which 4 were waited for; matrix products, arithmetic and copies ran while one was open for 0% of the time, Pallas kernels for 1%

profile of v3, /device:TPU:1, one launch (start us, length us, event | category | flops | bytes accessed | tf_op | source)
XLA Modules:
  0.0 123.1 jit_solution(14431136157146735754)
XLA Ops:
  0.6 0.0 copy-start
  0.6 0.8 copy-done
  1.5 0.0 copy-start.2
  1.5 0.8 copy-done.2
  2.2 0.0 copy-start.4
  2.2 0.8 copy-done.4
  3.0 0.4 shard_map.111
  3.4 19.5 %all_to_all.40.r_ref.row_ref = bf16[8,288,128]{2,1,0:T(8,128)(2,1)S(1)} all-to-all(bf16[8,288,128]{2,1,0:T(8,128)(2,1)S(1)} %shard_map.111), channel_id=1, replica_groups={{0,1,2,3,4,5,6,7},{8,9,10,11,12,13,14,15},{16,17,18,19,20,21,22,23},{24..., dimensions={0} | all-to-all | bytes 1179648 | tf_op jit(solution)/shard_map/all_to_all | solution.py:323
  22.9 0.7 shard_map.112
  23.6 3.4 %all-to-all-start.1 = ((f32[8,32,128]{2,1,0:T(8,128)}), f32[8,32,128]{2,1,0:T(8,128)S(1)}, u32[]{:S(2)}, u32[]{:S(2)}) async-start(f32[8,32,128]{2,1,0:T(8,128)} %get-tuple-element.19), calls=%async_computation.1 | async-start | bytes 262144 | tf_op jit(solution)/shard_map/all_to_all | solution.py:323
  27.0 3.3 %collective-permute-start = (bf16[4,256,128]{2,1,0:T(8,128)(2,1)S(1)}, bf16[4,256,128]{2,1,0:T(8,128)(2,1)S(1)}, u32[]{:S(2)}, u32[]{:S(2)}) collective-permute-start(bf16[4,256,128]{2,1,0:T(8,128)(2,1)S(1)} %get-tuple-element.18), channel_id=1, source_target_pairs={{0,8},{1,9},{2,10},{3,11},{4,12},{5,13},{6,14},{7,15},{8,16},{9,17... | collective-permute-start | bytes 786440 | tf_op jit(solution)/shard_map/ppermute | solution.py:342
  30.2 4.4 %all-to-all-done.1.c_ref = f32[8,32,128]{2,1,0:T(8,128)S(1)} async-done(((f32[8,32,128]{2,1,0:T(8,128)}), f32[8,32,128]{2,1,0:T(8,128)S(1)}, u32[]{:S(2)}, u32[]{:S(2)}) %all-to-all-start.1) | async-done | bytes 131104 | tf_op jit(solution)/shard_map/all_to_all | solution.py:323
  34.6 0.0 copy-start.7
  34.6 0.0 copy-start.8
  34.6 0.0 copy-start.9
  34.6 0.0 copy-start.10
  34.6 0.7 shard_map.113
  35.3 0.0 copy-start.1
  35.3 0.0 copy-start.3
  35.3 0.0 copy-start.5
  35.3 0.0 copy-start.6
  35.3 6.1 %all-to-all-start.2 = ((bf16[8,64,128]{2,1,0:T(8,128)(2,1)}), bf16[8,64,128]{2,1,0:T(8,128)(2,1)S(1)}, u32[]{:S(2)}, u32[]{:S(2)}) async-start(bf16[8,64,128]{2,1,0:T(8,128)(2,1)} %shard_map.113), calls=%async_computation.2 | async-start | bytes 262144 | tf_op jit(solution)/shard_map/all_to_all | solution.py:323
  41.4 0.0 collective-permute-done.prev_ref
  41.4 5.3 %all-to-all-done.2.r_ref = bf16[8,64,128]{2,1,0:T(8,128)(2,1)S(1)} async-done(((bf16[8,64,128]{2,1,0:T(8,128)(2,1)}), bf16[8,64,128]{2,1,0:T(8,128)(2,1)S(1)}, u32[]{:S(2)}, u32[]{:S(2)}) %all-to-all-start.2) | async-done | bytes 131104 | tf_op jit(solution)/shard_map/all_to_all | solution.py:323
  46.7 0.0 copy-done.7
  46.7 0.0 copy-done.8
  46.7 0.0 copy-done.9
  46.7 0.0 copy-done.10
  46.7 0.0 copy-done.1
  46.7 0.0 copy-done.3
  46.8 0.0 copy-done.5
  46.8 0.0 copy-done.6
  46.8 4.3 %shard_map.114 = (bf16[1,128,512]{2,1,0:T(8,128)(2,1)}, bf16[8,96,128]{2,1,0:T(8,128)(2,1)S(1)}, bf16[8,256,128]{2,1,0:T(8,128)(2,1)S(1)}, bf16[4,256,128]{2,1,0...) custom-call(bf16[1,128,512]{2,1,0:T(8,128)(2,1)S(1)} %copy-done.6, ...), custom_call_target="tpu_custom_call" | custom-call | tf_op jit(solution)/shard_map/pallas_call | solution.py:310
  51.1 9.1 %all_to_all.41.r_ref = bf16[8,96,128]{2,1,0:T(8,128)(2,1)S(1)} all-to-all(bf16[8,96,128]{2,1,0:T(8,128)(2,1)S(1)} %get-tuple-element.21), channel_id=1, replica_groups={{0,1,2,3,4,5,6,7},{8,9,10,11,12,13,14,15},{16,17,18,19,20,21,22,23},{24..., dimensions={0} | all-to-all | bytes 393216 | tf_op jit(solution)/shard_map/all_to_all | solution.py:323
  60.2 10.1 %all_to_all.42.c_ref = f32[8,32,128]{2,1,0:T(8,128)S(1)} all-to-all(f32[8,32,128]{2,1,0:T(8,128)S(1)} %shard_map.115), channel_id=1, replica_groups={{0,8,16,24,32,40,48,56},{1,9,17,25,33,41,49,57},{2,10,18,26,34,42,50,58..., dimensions={0} | all-to-all | bytes 262144 | tf_op jit(solution)/shard_map/all_to_all | solution.py:323
  70.3 2.3 %shard_map.116 = (f32[8,32,128]{2,1,0:T(8,128)}, bf16[8,64,128]{2,1,0:T(8,128)(2,1)S(1)}) custom-call(bf16[8,288,128]{2,1,0:T(8,128)(2,1)S(1)} %all_to_all.40.r_ref.row_ref, bf16[128,256]{1,0:T(8,128)(2,1)S(1)} %copy-done.1, bf16[8,96,128]{2,1,0:T(8,128)(2,1)S(1)} %all_to_all.41.r_ref, f32[8,32,128]{2,1,0:T(8,128)S(1)} %all_to_all.42.c_ref), custom_call_target="tpu_custom_call" | custom-call | tf_op jit(solution)/shard_map/pallas_call | solution.py:310
  72.7 3.4 %all-to-all-start.5 = ((f32[8,32,128]{2,1,0:T(8,128)}), f32[8,32,128]{2,1,0:T(8,128)S(1)}, u32[]{:S(2)}, u32[]{:S(2)}) async-start(f32[8,32,128]{2,1,0:T(8,128)} %get-tuple-element.22), calls=%async_computation.5 | async-start | bytes 262144 | tf_op jit(solution)/shard_map/all_to_all | solution.py:323
  76.0 1.3 %collective-permute-start.1 = (bf16[4,256,128]{2,1,0:T(8,128)(2,1)S(1)}, bf16[4,256,128]{2,1,0:T(8,128)(2,1)S(1)}, u32[]{:S(2)}, u32[]{:S(2)}) collective-permute-start(bf16[4,256,128]{2,1,0:T(8,128)(2,1)S(1)} %get-tuple-element.25), channel_id=1, source_target_pairs={{8,0},{9,1},{10,2},{11,3},{12,4},{13,5},{14,6},{15,7},{16,8},{17,9... | collective-permute-start | bytes 786440 | tf_op jit(solution)/shard_map/ppermute | solution.py:358
  77.3 6.6 %all-to-all-done.5.r_ref = f32[8,32,128]{2,1,0:T(8,128)S(1)} async-done(((f32[8,32,128]{2,1,0:T(8,128)}), f32[8,32,128]{2,1,0:T(8,128)S(1)}, u32[]{:S(2)}, u32[]{:S(2)}) %all-to-all-start.5) | async-done | bytes 131104 | tf_op jit(solution)/shard_map/all_to_all | solution.py:323
  84.0 0.7 shard_map.117
  84.7 10.0 %all-to-all-start.6 = ((f32[8,32,128]{2,1,0:T(8,128)}), f32[8,32,128]{2,1,0:T(8,128)S(1)}, u32[]{:S(2)}, u32[]{:S(2)}) async-start(f32[8,32,128]{2,1,0:T(8,128)} %shard_map.117), calls=%async_computation.6 | async-start | bytes 262144 | tf_op jit(solution)/shard_map/all_to_all | solution.py:323
  94.7 0.0 collective-permute-done.1.back_ref
  94.7 7.9 %all-to-all-done.6.r_ref = f32[8,32,128]{2,1,0:T(8,128)S(1)} async-done(((f32[8,32,128]{2,1,0:T(8,128)}), f32[8,32,128]{2,1,0:T(8,128)S(1)}, u32[]{:S(2)}, u32[]{:S(2)}) %all-to-all-start.6) | async-done | bytes 131104 | tf_op jit(solution)/shard_map/all_to_all | solution.py:323
  102.6 0.1 shard_map.118
  102.7 19.3 %all_to_all.43.r_ref = bf16[8,384,128]{2,1,0:T(8,128)(2,1)S(1)} all-to-all(bf16[8,384,128]{2,1,0:T(8,128)(2,1)S(1)} %shard_map.118), channel_id=1, replica_groups={{0,1,2,3,4,5,6,7},{8,9,10,11,12,13,14,15},{16,17,18,19,20,21,22,23},{24..., dimensions={0} | all-to-all | bytes 1572864 | tf_op jit(solution)/shard_map/all_to_all | solution.py:323
  122.0 1.1 shard_map.119
  (1 shorter events, 0.0 us)
Async XLA Ops:
  0.6 0.8 copy-start
  1.5 0.8 copy-start.2
  2.2 0.8 copy-start.4
  23.6 11.0 %all-to-all-start.1 = ((f32[8,32,128]{2,1,0:T(8,128)}), f32[8,32,128]{2,1,0:T(8,128)S(1)}, u32[]{:S(2)}, u32[]{:S(2)}) async-start(f32[8,32,128]{2,1,0:T(8,128)} %get-tuple-element.19), calls=%async_computation.1 | async-start | bytes 262144 | tf_op jit(solution)/shard_map/all_to_all | solution.py:323
  27.0 14.5 %collective-permute-start = (bf16[4,256,128]{2,1,0:T(8,128)(2,1)S(1)}, bf16[4,256,128]{2,1,0:T(8,128)(2,1)S(1)}, u32[]{:S(2)}, u32[]{:S(2)}) collective-permute-start(bf16[4,256,128]{2,1,0:T(8,128)(2,1)S(1)} %get-tuple-element.18), channel_id=1, source_target_pairs={{0,8},{1,9},{2,10},{3,11},{4,12},{5,13},{6,14},{7,15},{8,16},{9,17... | collective-permute-start | bytes 786440 | tf_op jit(solution)/shard_map/ppermute | solution.py:342
  34.6 12.1 %copy-start.7 = (bf16[1,128,512]{2,1,0:T(8,128)(2,1)S(1)}, bf16[1,128,512]{2,1,0:T(8,128)(2,1)}, u32[]{:S(2)}) copy-start(bf16[1,128,512]{2,1,0:T(8,128)(2,1)} %g_ref.1) | copy-start | bytes 393220
  34.6 12.1 %copy-start.8 = (f32[1,512]{1,0:T(1,128)S(1)}, f32[1,512]{1,0:T(1,128)}, u32[]{:S(2)}) copy-start(f32[1,512]{1,0:T(1,128)} %gl_ref.1) | copy-start | bytes 6148
  34.6 12.1 %copy-start.9 = (f32[1,512]{1,0:T(1,128)S(1)}, f32[1,512]{1,0:T(1,128)}, u32[]{:S(2)}) copy-start(f32[1,512]{1,0:T(1,128)} %gs_ref.1) | copy-start | bytes 6148
  34.6 12.1 %copy-start.10 = (s32[1,64,4]{1,2,0:T(4,128)S(1)}, s32[1,64,4]{1,2,0:T(4,128)}, u32[]{:S(2)}) copy-start(s32[1,64,4]{1,2,0:T(4,128)} %param.14) | copy-start | bytes 3076
  35.3 11.4 %copy-start.1 = (bf16[128,256]{1,0:T(8,128)(2,1)S(1)}, bf16[128,256]{1,0:T(8,128)(2,1)}, u32[]{:S(2)}) copy-start(bf16[128,256]{1,0:T(8,128)(2,1)} %w_ref.7) | copy-start | bytes 196612
  35.3 11.4 %copy-start.3 = (bf16[1,128,128]{2,1,0:T(8,128)(2,1)S(1)}, bf16[1,128,128]{2,1,0:T(8,128)(2,1)}, u32[]{:S(2)}) copy-start(bf16[1,128,128]{2,1,0:T(8,128)(2,1)} %k_ref.5) | copy-start | bytes 98308
  35.3 11.4 %copy-start.5 = (bf16[1,128,128]{2,1,0:T(8,128)(2,1)S(1)}, bf16[1,128,128]{2,1,0:T(8,128)(2,1)}, u32[]{:S(2)}) copy-start(bf16[1,128,128]{2,1,0:T(8,128)(2,1)} %v_ref.5) | copy-start | bytes 98308
  35.3 11.4 %copy-start.6 = (bf16[1,128,512]{2,1,0:T(8,128)(2,1)S(1)}, bf16[1,128,512]{2,1,0:T(8,128)(2,1)}, u32[]{:S(2)}) copy-start(bf16[1,128,512]{2,1,0:T(8,128)(2,1)} %q_ref.1) | copy-start | bytes 393220
  35.3 11.4 %all-to-all-start.2 = ((bf16[8,64,128]{2,1,0:T(8,128)(2,1)}), bf16[8,64,128]{2,1,0:T(8,128)(2,1)S(1)}, u32[]{:S(2)}, u32[]{:S(2)}) async-start(bf16[8,64,128]{2,1,0:T(8,128)(2,1)} %shard_map.113), calls=%async_computation.2 | async-start | bytes 262144 | tf_op jit(solution)/shard_map/all_to_all | solution.py:323
  72.7 11.3 %all-to-all-start.5 = ((f32[8,32,128]{2,1,0:T(8,128)}), f32[8,32,128]{2,1,0:T(8,128)S(1)}, u32[]{:S(2)}, u32[]{:S(2)}) async-start(f32[8,32,128]{2,1,0:T(8,128)} %get-tuple-element.22), calls=%async_computation.5 | async-start | bytes 262144 | tf_op jit(solution)/shard_map/all_to_all | solution.py:323
  76.0 18.6 %collective-permute-start.1 = (bf16[4,256,128]{2,1,0:T(8,128)(2,1)S(1)}, bf16[4,256,128]{2,1,0:T(8,128)(2,1)S(1)}, u32[]{:S(2)}, u32[]{:S(2)}) collective-permute-start(bf16[4,256,128]{2,1,0:T(8,128)(2,1)S(1)} %get-tuple-element.25), channel_id=1, source_target_pairs={{8,0},{9,1},{10,2},{11,3},{12,4},{13,5},{14,6},{15,7},{16,8},{17,9... | collective-permute-start | bytes 786440 | tf_op jit(solution)/shard_map/ppermute | solution.py:358
  84.7 17.9 %all-to-all-start.6 = ((f32[8,32,128]{2,1,0:T(8,128)}), f32[8,32,128]{2,1,0:T(8,128)S(1)}, u32[]{:S(2)}, u32[]{:S(2)}) async-start(f32[8,32,128]{2,1,0:T(8,128)} %shard_map.117), calls=%async_computation.6 | async-start | bytes 262144 | tf_op jit(solution)/shard_map/all_to_all | solution.py:323

commit v4 on v3

--- a/solution.py
+++ b/solution.py
@@ -5,6 +5,7 @@
 from jax.experimental.pallas import tpu as pltpu
 from jax.sharding import PartitionSpec as P
 
+
 INTERPRET = False
 EPS = 1e-06
 F32 = jnp.float32
@@ -49,6 +50,7 @@
 def split(value):
     high = value.astype(BF16)
     return high, (value - high.astype(F32)).astype(BF16)
+
 
 SIDE = 8
 
@@ -77,7 +79,17 @@
     ref[:, at + step : at + 2 * step] = low
 
 
-def send_state_kernel(k_ref, v_ref, w_ref, o_ref):
+def send_state_kernel(k_hbm, v_hbm, w_hbm, o_ref, k_ref, v_ref, w_ref, sem):
+    copies = [
+        pltpu.make_async_copy(source, target, sem.at[place])
+        for place, (source, target) in enumerate(
+            ((k_hbm, k_ref), (v_hbm, v_ref), (w_hbm, w_ref))
+        )
+    ]
+    for copy in copies:
+        copy.start()
+    for copy in copies:
+        copy.wait()
     keys = k_ref[0]
     values = v_ref[0]
     feat = features(nn(keys, w_ref[...]))[0].astype(BF16)
@@ -107,37 +119,37 @@
         total = total + r_ref[spot, :step].astype(F32)
 
 
-def main_kernel(
-    q_ref, k_ref, v_ref, g_ref, gl_ref, gs_ref, kb_ref, w_ref, row_ref, prev_ref, r_ref,
-    qo_ref, send_ref, up_ref, back_ref, kloc_ref, dk_ref, dv_ref,
+def stacked(ref, size):
+    heads = ref.shape[2] // size
+    return jnp.concatenate([ref[0, :, h * size : (h + 1) * size] for h in range(heads)], axis=0)
+
+
+def gains(ref, length, size):
+    heads = ref.shape[1] // size
+    return jnp.concatenate(
+        [
+            jnp.broadcast_to(ref[:, h * size : (h + 1) * size], (length, size))
+            for h in range(heads)
+        ],
+        axis=0,
+    )
+
+
+def causal_mask(rows, length):
+    row, col = iotas((rows, length))
+    return (row & (length - 1)) >= col
+
+
+def linear_kernel(
+    q_ref, k_ref, v_ref, g_ref, gl_ref, w_ref, r_ref, send_ref, kloc_ref, ql_ref, vl_ref
 ):
-    spot, shard = spots()[1:]
     keys = k_ref[0]
     values = v_ref[0]
     w = w_ref[...]
     length, size = keys.shape
-    heads = q_ref.shape[2] // size
-    scaling = size ** (-0.5)
-    rows = heads * length
     step = r_ref.shape[1] // 2
-
-    def stacked(ref):
-        return jnp.concatenate(
-            [ref[0, :, h * size : (h + 1) * size] for h in range(heads)], axis=0
-        )
-
-    def gains(ref):
-        return jnp.concatenate(
-            [
-                jnp.broadcast_to(ref[:, h * size : (h + 1) * size], (length, size))
-                for h in range(heads)
-            ],
-            axis=0,
-        )
-
-    queries = stacked(q_ref)
-    upstream = stacked(g_ref).astype(F32)
-
+    queries = stacked(q_ref, size)
+    upstream = stacked(g_ref, size).astype(F32)
     state_high = whole(r_ref[:, :step])
     state_low = whole(r_ref[:, step:])
     raw = nn(queries, w)
@@ -145,11 +157,10 @@
     feat = feat.astype(BF16)
     key_feat, key_slope = features(nn(keys, w))
     key_feat = key_feat.astype(BF16)
-    row, col = iotas((rows, length))
-    causal = (row & (length - 1)) >= col
+    causal = causal_mask(queries.shape[0], length)
     weights = jnp.where(causal, nt(feat, key_feat), 0.0).astype(BF16)
     lin_out = nn(feat, state_high) + nn(feat, state_low) + nn(weights, values)
-    lin_grad = norm_backward(lin_out, upstream * gains(gl_ref))
+    lin_grad = norm_backward(lin_out, upstream * gains(gl_ref, length, size))
     lin_high, lin_low = split(lin_grad)
     score_grad = jnp.where(causal, nt(lin_high, values), 0.0).astype(BF16)
     feat_grad = (
@@ -159,15 +170,29 @@
         + nn(score_grad, key_feat)
     )
     raw_grad = (feat_grad * slope).astype(BF16)
-    query_lin = nt(raw_grad, w)
+    ql_ref[...] = nt(raw_grad, w)
     key_local = tn(score_grad, feat)
     kloc_ref[...] = key_local
-    value_local = tn(weights, lin_high)
+    vl_ref[...] = tn(weights, lin_high)
     send_ref[:, :step] = pieces(tn(feat, lin_high) + tn(feat, lin_low)).astype(BF16)
     local_high, local_low = split(key_local * key_slope)
     early = tn(raw_grad, queries) + tn(local_high, keys) + tn(local_low, keys)
     store_split(send_ref, step, pieces(early))
 
+
+def sparse_kernel(
+    q_ref, k_ref, v_ref, g_ref, gs_ref, kb_ref, row_ref, prev_ref, ql_ref, vl_ref,
+    qo_ref, dk_ref, dv_ref, *back_refs,
+):
+    spot, shard = spots()[1:]
+    keys = k_ref[0]
+    values = v_ref[0]
+    length, size = keys.shape
+    scaling = size ** (-0.5)
+    queries = stacked(q_ref, size)
+    heads = queries.shape[0] // length
+    upstream = stacked(g_ref, size).astype(F32)
+    causal = causal_mask(queries.shape[0], length)
     reaches = kb_ref.shape[1]
     table = kb_ref[0]
     column = lax.broadcasted_iota(jnp.int32, table.shape, 1)
@@ -175,7 +200,7 @@
     far = []
     live = []
     for reach in range(1, reaches + 1):
-        own = row_ref[jnp.maximum(spot - reach, 0), step:].astype(F32)
+        own = row_ref[jnp.maximum(spot - reach, 0), -2 * length :].astype(F32)
         other = prev_ref[jnp.clip(spot - reach + SIDE // 2, 0, SIDE // 2 - 1)].astype(F32)
         inside = flag(spot >= reach)
         far.append((inside * own + (1.0 - inside) * other).astype(BF16))
@@ -199,44 +224,34 @@
     near_half = near_probs.astype(BF16)
     far_half = far_probs.astype(BF16)
     sparse_out = nn(near_half, values) + nn(far_half, value_far)
-    sparse_grad = norm_backward(sparse_out, upstream * gains(gs_ref)).astype(BF16)
+    sparse_grad = norm_backward(sparse_out, upstream * gains(gs_ref, length, size)).astype(BF16)
     inner = jnp.sum(sparse_grad.astype(F32) * sparse_out, axis=1, keepdims=True)
     near_grad = (scaling * near_probs * (nt(sparse_grad, values) - inner)).astype(BF16)
     far_grad = (scaling * far_probs * (nt(sparse_grad, value_far) - inner)).astype(BF16)
-    query_out = nn(near_grad, keys) + nn(far_grad, key_far) + query_lin
+    query_out = nn(near_grad, keys) + nn(far_grad, key_far) + ql_ref[...]
     for h in range(heads):
         qo_ref[0, :, h * size : (h + 1) * size] = query_out[
             h * length : (h + 1) * length
         ].astype(BF16)
     dk_ref[...] = tn(near_grad, queries)
-    dv_ref[...] = tn(near_half, sparse_grad) + value_local
+    dv_ref[...] = tn(near_half, sparse_grad) + vl_ref[...]
     key_back = tn(far_grad, queries).astype(BF16)
     value_back = tn(far_half, sparse_grad).astype(BF16)
-    up_ref[...] = jnp.zeros(up_ref.shape, BF16)
-    back_ref[...] = jnp.zeros(back_ref.shape, BF16)
-    for reach in range(1, reaches + 1):
-        part = slice((reach - 1) * length, reach * length)
-
-        @pl.when(spot >= reach)
-        def _():
-            up_ref[spot - reach, :length] = key_back[part]
-            up_ref[spot - reach, length:] = value_back[part]
-
-        @pl.when(spot < reach)
-        def _():
-            back_ref[spot - reach + SIDE // 2, :length] = key_back[part]
-            back_ref[spot - reach + SIDE // 2, length:] = value_back[part]
-
-
-def cot_total_kernel(r_ref, o_ref):
+    for reach in range(reaches):
+        part = slice(reach * length, (reach + 1) * length)
+        back_refs[reach][:length] = key_back[part]
+        back_refs[reach][length:] = value_back[part]
+
+
+def total_kernel(r_ref, o_ref):
     step = o_ref.shape[1]
     total = jnp.sum(r_ref[:, :step].astype(F32), axis=0)
     o_ref[...] = jnp.broadcast_to(total[None], o_ref.shape)
 
 
-def weight_part_kernel(row_ref, w_ref, r_ref, c_ref, send_ref, o_ref):
+def weight_part_kernel(row_ref, w_ref, r_ref, c_ref, a_ref, b_ref, send_ref, o_ref, sum_ref):
     line, spot = spots()[:2]
-    step, size = c_ref.shape[1:]
+    step, _ = c_ref.shape[1:]
     length = (row_ref.shape[1] - step) // 2
     w = w_ref[...]
     row, col = iotas((step, w.shape[1]))
@@ -258,28 +273,27 @@
             weight = weight + r_ref[source, place * step : (place + 1) * step].astype(F32)
         total = total + r_ref[source, :step].astype(F32)
     send_ref[...] = jnp.broadcast_to(weight[None], send_ref.shape)
-
-
-def column_sum_kernel(r_ref, o_ref):
+    sum_ref[...] = a_ref[...].astype(F32) + b_ref[...].astype(F32)
+
+
+def column_sum_kernel(r_ref, a_ref, b_ref, in_ref, o_ref, sum_ref):
+    sum_ref[...] = in_ref[...] + a_ref[...].astype(F32) + b_ref[...].astype(F32)
     o_ref[...] = jnp.broadcast_to(jnp.sum(r_ref[...], axis=0)[None], o_ref.shape)
 
 
 def make_last_kernel(scale):
-    def last_kernel(r_ref, carried_ref, up_ref, back_ref, o_ref):
+    def last_kernel(r_ref, carried_ref, o_ref):
         step = r_ref.shape[1]
         high, low = split(jnp.sum(r_ref[...], axis=0) * scale)
         o_ref[:, : 2 * step] = carried_ref[...]
         o_ref[:, 2 * step : 3 * step] = jnp.broadcast_to(high[None], (SIDE, *high.shape))
         o_ref[:, 3 * step : 4 * step] = jnp.broadcast_to(low[None], (SIDE, *low.shape))
-        o_ref[: SIDE // 2, 4 * step :] = up_ref[: SIDE // 2]
-        both = up_ref[SIDE // 2 :].astype(F32) + back_ref[...].astype(F32)
-        o_ref[SIDE // 2 :, 4 * step :] = both.astype(BF16)
 
     return last_kernel
 
 
 def key_kernel(
-    k_ref, v_ref, w_ref, r_ref, kloc_ref, dk_ref, dv_ref, ko_ref, vo_ref, wo_ref
+    k_ref, v_ref, w_ref, r_ref, kloc_ref, dk_ref, dv_ref, back_ref, ko_ref, vo_ref, wo_ref
 ):
     keys = k_ref[0]
     values = v_ref[0]
@@ -291,7 +305,7 @@
     weight = whole(r_ref[:, 2 * step : 3 * step]).astype(F32)
     weight = weight + whole(r_ref[:, 3 * step : 4 * step]).astype(F32)
     wo_ref[...] = weight.T
-    back = jnp.sum(r_ref[:, 4 * step :].astype(F32), axis=0)
+    back = back_ref[...]
     feat, slope = features(nn(keys, w))
     feat = feat.astype(BF16)
     feat_grad = nt(values, carried_high) + nt(values, carried_low) + kloc_ref[...]
@@ -302,7 +316,7 @@
     ).astype(BF16)
 
 
-def call(kernel, *outs, grant=8):
+def call(kernel, *outs, grant=8, space=pltpu.VMEM, scratch=()):
     shapes = [jax.ShapeDtypeStruct(shape, dtype) for shape, dtype in outs]
     spec = pl.BlockSpec(memory_space=pltpu.VMEM)
 
@@ -310,8 +324,9 @@
         return pl.pallas_call(
             kernel,
             out_shape=shapes if len(shapes) > 1 else shapes[0],
-            in_specs=[spec] * len(operands),
+            in_specs=[pl.BlockSpec(memory_space=space)] * len(operands),
             out_specs=[spec] * len(shapes) if len(shapes) > 1 else spec,
+            scratch_shapes=scratch,
             interpret=INTERPRET,
             compiler_params=pltpu.CompilerParams(vmem_limit_bytes=grant << 20),
         )(*operands)
@@ -336,38 +351,61 @@
     piece = (SIDE, step, size)
     two = (SIDE, 2 * step, size)
     down = [(i, i + SIDE) for i in range(shards - SIDE)]
-    sent = call(send_state_kernel, ((SIDE, step + 2 * length, size), BF16))(keys, values, w_feat)
+    rows = (queries.shape[2] // size * length, size)
+    square = (length, size)
+    both = (2 * length, size)
+    sent = call(
+        send_state_kernel,
+        ((SIDE, step + 2 * length, size), BF16),
+        space=pltpu.HBM,
+        scratch=[pltpu.VMEM(item.shape, BF16) for item in (keys, values, w_feat)]
+        + [pltpu.SemaphoreType.DMA((3,))],
+    )(keys, values, w_feat)
     row = swap(sent, "ctx", in_row)
     sent, moved = call(row_total_kernel, (piece, F32), (half, BF16))(row)
+    got = swap(sent, "ctx", in_column)
     previous = lax.ppermute(moved, "ctx", down)
-    sent = call(prefix_kernel, (two, BF16))(row, swap(sent, "ctx", in_column))
-    query_out, sent, up, back, key_local, key_near, value_near = call(
-        main_kernel,
+    sent = call(prefix_kernel, (two, BF16))(row, got)
+    got = swap(sent, "ctx", in_row)
+    sent, key_local, query_lin, value_local = call(
+        linear_kernel,
+        ((SIDE, 3 * step, size), BF16),
+        ((length, features_n), F32),
+        (rows, F32),
+        (square, F32),
+        grant=16,
+    )(queries, keys, values, out_grad, gain_lin, w_feat, got)
+    cots = swap(sent, "ctx", in_row)
+    query_out, key_near, value_near, *backs = call(
+        sparse_kernel,
         (queries.shape, BF16),
-        ((SIDE, 3 * step, size), BF16),
-        ((SIDE, 2 * length, size), BF16),
-        (half, BF16),
-        ((length, features_n), F32),
-        ((length, size), F32),
-        ((length, size), F32),
+        (square, F32),
+        (square, F32),
+        *[((2 * length, size), BF16)] * key_blocks.shape[2],
         grant=24,
     )(
-        queries, keys, values, out_grad, gain_lin, gain_sparse,
-        jnp.swapaxes(key_blocks, 1, 2), w_feat, row, previous, swap(sent, "ctx", in_row),
-    )
-    returned = lax.ppermute(back, "ctx", [(b, a) for a, b in down])
-    cots = swap(sent, "ctx", in_row)
-    sent = call(cot_total_kernel, (piece, F32))(cots)
-    sent, carried = call(weight_part_kernel, (piece, F32), (two, BF16))(
-        row, w_feat, cots, swap(sent, "ctx", in_column)
-    )
-    sent = call(column_sum_kernel, ((groups, step, size), F32))(swap(sent, "ctx", in_column))
-    sent = call(make_last_kernel(scale), ((SIDE, 4 * step + 2 * length, size), BF16))(
-        swap(sent, "heads"), carried, up, returned
-    )
+        queries, keys, values, out_grad, gain_sparse, jnp.swapaxes(key_blocks, 1, 2),
+        row, previous, query_lin, value_local,
+    )
+    far = []
+    for reach, back in enumerate(backs, 1):
+        pairs = [(i, i - reach) for i in range(reach, shards)]
+        far.append(lax.ppermute(back, "ctx", pairs))
+    sent = call(total_kernel, (piece, F32))(cots)
+    got = swap(sent, "ctx", in_column)
+    sent, carried, back = call(
+        weight_part_kernel, (piece, F32), (two, BF16), (both, F32)
+    )(row, w_feat, cots, got, far[0], far[1])
+    got = swap(sent, "ctx", in_column)
+    sent, back = call(column_sum_kernel, ((groups, step, size), F32), (both, F32))(
+        got, far[2], far[3], back
+    )
+    got = swap(sent, "heads")
+    sent = call(make_last_kernel(scale), ((SIDE, 4 * step, size), BF16))(got, carried)
+    got = swap(sent, "ctx", in_row)
     key_out, value_out, weight = call(
         key_kernel, (keys.shape, BF16), (values.shape, BF16), (w_feat.shape, F32)
-    )(keys, values, w_feat, swap(sent, "ctx", in_row), key_local, key_near, value_near)
+    )(keys, values, w_feat, got, key_local, key_near, value_near, back)
     return query_out, key_out, value_out, weight
 
 

time: 124 us -> 126 us (1.016)
  blocking collectives: 58.1 us -> 73.1 us
  waiting for transfers between devices: 24.2 us -> 14.6 us
  starting transfers between devices: 27.4 us -> 22.9 us
    all_to_all x4 -> x3, waiting for transfers between devices: 24.2 us -> 3.86 us  [swap(): lax.all_to_all(value, axis, 0, 0, axis_index_groups=groups, tiled=False)]
    all_to_all x4 -> x5, blocking collectives: 58.1 us -> 73.1 us  [swap(): lax.all_to_all(value, axis, 0, 0, axis_index_groups=groups, tiled=False)]
    ppermute x1 -> x4, waiting for transfers between devices: 0.01 us -> 10.8 us  [per_device(): far.append(lax.ppermute(back, 'ctx', pairs))]
    all_to_all x4 -> x3, starting transfers between devices: 22.9 us -> 14.2 us  [swap(): lax.all_to_all(value, axis, 0, 0, axis_index_groups=groups, tiled=False)]
    ppermute x1 -> x4, starting transfers between devices: 1.29 us -> 6.71 us  [per_device(): far.append(lax.ppermute(back, 'ctx', pairs))]
    pallas_call x9 -> x10, Pallas kernels: 10.2 us -> 9.61 us  [run(): pl.pallas_call(kernel, out_shape=shapes if len(shapes) > 1 else shapes[0]...]
  transfers between devices with their start and end apart: 6 -> 8, of which waited for: 4 -> 5; matrix products, arithmetic and copies ran while one was open for 0% -> 0% of each run, Pallas kernels for 1% -> 2%
where the time goes in v4:
time: 126 us; the launch traced here: 124 us
  blocking collectives  73.1 us (58%)
  starting transfers between devices  22.9 us (18%)
  waiting for transfers between devices  14.6 us (12%)
  Pallas kernels  9.61 us (8%)
  local copies, waits for them, and re-layouts  3.07 us (2%)
    all_to_all x5, blocking collectives, swap(): lax.all_to_all(value, axis, 0, 0, axis_index_groups=groups, tiled=False)  73.1 us
    all_to_all x3, starting transfers between devices, swap(): lax.all_to_all(value, axis, 0, 0, axis_index_groups=groups, tiled=False)  14.2 us
    ppermute x4, waiting for transfers between devices, per_device(): far.append(lax.ppermute(back, 'ctx', pairs))  10.8 us
    pallas_call x10, Pallas kernels, run(): pl.pallas_call(kernel, out_shape=shapes if len(shapes) > 1 else shapes[0]...  9.61 us
    ppermute x4, starting transfers between devices, per_device(): far.append(lax.ppermute(back, 'ctx', pairs))  6.71 us
    all_to_all x3, waiting for transfers between devices, swap(): lax.all_to_all(value, axis, 0, 0, axis_index_groups=groups, tiled=False)  3.86 us
    unnamed x22, local copies, waits for them, and re-layouts  3.07 us
  transfers between devices with their start and end apart: 8, of which 5 were waited for; matrix products, arithmetic and copies ran while one was open for 0% of the time, Pallas kernels for 2%

profile of v4, /device:TPU:1, one launch (start us, length us, event | category | flops | bytes accessed | tf_op | source)
XLA Modules:
  0.0 124.1 jit_solution(443346813082482831)
XLA Ops:
  0.6 0.0 copy-start
  0.6 0.8 copy-done
  1.5 0.0 copy-start.2
  1.5 0.8 copy-done.2
  2.2 0.0 copy-start.4
  2.2 0.8 copy-done.4
  3.0 0.5 shard_map.111
  3.5 19.5 %all_to_all.40.r_ref.row_ref = bf16[8,288,128]{2,1,0:T(8,128)(2,1)S(1)} all-to-all(bf16[8,288,128]{2,1,0:T(8,128)(2,1)S(1)} %shard_map.111), channel_id=1, replica_groups={{0,1,2,3,4,5,6,7},{8,9,10,11,12,13,14,15},{16,17,18,19,20,21,22,23},{24..., dimensions={0} | all-to-all | bytes 1179648 | tf_op jit(solution)/shard_map/all_to_all | solution.py:338
  23.1 10.7 %all_to_all.41.c_ref = f32[8,32,128]{2,1,0:T(8,128)S(1)} all-to-all(f32[8,32,128]{2,1,0:T(8,128)S(1)} %get-tuple-element.26), channel_id=1, replica_groups={{0,8,16,24,32,40,48,56},{1,9,17,25,33,41,49,57},{2,10,18,26,34,42,50,58..., dimensions={0} | all-to-all | bytes 262144 | tf_op jit(solution)/shard_map/all_to_all | solution.py:338
  33.8 0.0 copy-start.7
  33.8 0.0 copy-start.8
  33.9 0.0 copy-start.1
  33.9 0.0 copy-start.3
  33.9 0.0 copy-start.5
  33.9 0.0 copy-start.6
  33.9 10.1 %all_to_all.42.r_ref = bf16[8,64,128]{2,1,0:T(8,128)(2,1)S(1)} all-to-all(bf16[8,64,128]{2,1,0:T(8,128)(2,1)S(1)} %shard_map.113), channel_id=1, replica_groups={{0,1,2,3,4,5,6,7},{8,9,10,11,12,13,14,15},{16,17,18,19,20,21,22,23},{24..., dimensions={0} | all-to-all | bytes 262144 | tf_op jit(solution)/shard_map/all_to_all | solution.py:338
  44.0 0.0 copy-done.7
  44.0 0.0 copy-done.8
  44.0 0.0 copy-done.1
  44.1 0.0 copy-done.3
  44.1 0.0 copy-done.5
  44.1 0.0 copy-done.6
  44.1 2.7 %shard_map.114 = (bf16[8,96,128]{2,1,0:T(8,128)(2,1)}, f32[128,256]{1,0:T(8,128)S(1)}, f32[512,128]{1,0:T(8,128)S(1)}, f32[128,128]{1,0:T(8,128)S(1)}) custom-call(bf16[1,128,512]{2,1,0:T(8,128)(2,1)S(1)} %copy-done.6, bf16[1,128,128]{2,1,0:T(8,128)(2,1)S(1)} %copy-done.3, bf16[1,128,128]{2,1,0:T(8,128)(2,1)S(1)} %copy-done.5, ...), custom_call_target="tpu_custom_call" | custom-call | tf_op jit(solution)/shard_map/pallas_call | solution.py:324
  46.8 4.2 %all-to-all-start.3 = ((bf16[8,96,128]{2,1,0:T(8,128)(2,1)}), bf16[8,96,128]{2,1,0:T(8,128)(2,1)S(1)}, u32[]{:S(2)}, u32[]{:S(2)}) async-start(bf16[8,96,128]{2,1,0:T(8,128)(2,1)} %get-tuple-element.30), calls=%async_computation.3 | async-start | bytes 393216 | tf_op jit(solution)/shard_map/all_to_all | solution.py:338
  50.9 2.0 %collective-permute-start = (bf16[4,256,128]{2,1,0:T(8,128)(2,1)S(1)}, bf16[4,256,128]{2,1,0:T(8,128)(2,1)S(1)}, u32[]{:S(2)}, u32[]{:S(2)}) collective-permute-start(bf16[4,256,128]{2,1,0:T(8,128)(2,1)S(1)} %get-tuple-element.25), channel_id=1, source_target_pairs={{0,8},{1,9},{2,10},{3,11},{4,12},{5,13},{6,14},{7,15},{8,16},{9,17... | collective-permute-start | bytes 786440 | tf_op jit(solution)/shard_map/ppermute | solution.py:367
  52.9 3.9 %all-to-all-done.3.r_ref = bf16[8,96,128]{2,1,0:T(8,128)(2,1)S(1)} async-done(((bf16[8,96,128]{2,1,0:T(8,128)(2,1)}), bf16[8,96,128]{2,1,0:T(8,128)(2,1)S(1)}, u32[]{:S(2)}, u32[]{:S(2)}) %all-to-all-start.3) | async-done | bytes 196640 | tf_op jit(solution)/shard_map/all_to_all | solution.py:338
  56.8 0.7 shard_map.116
  57.5 3.4 %all-to-all-start.4 = ((f32[8,32,128]{2,1,0:T(8,128)}), f32[8,32,128]{2,1,0:T(8,128)S(1)}, u32[]{:S(2)}, u32[]{:S(2)}) async-start(f32[8,32,128]{2,1,0:T(8,128)} %shard_map.116), calls=%async_computation.4 | async-start | bytes 262144 | tf_op jit(solution)/shard_map/all_to_all | solution.py:338
  60.8 0.0 collective-permute-done.prev_ref
  60.9 0.0 copy-start.10
  60.9 0.0 copy-start.9
  60.9 0.7 copy-done.10
  61.5 0.0 copy-done.9
  61.6 2.2 %shard_map.115 = (bf16[1,128,512]{2,1,0:T(8,128)(2,1)}, f32[128,128]{1,0:T(8,128)S(1)}, f32[128,128]{1,0:T(8,128)S(1)}, bf16[256,128]{1,0:T(8,128)(2,1)S(1)}, bf...) custom-call(bf16[1,128,512]{2,1,0:T(8,128)(2,1)S(1)} %copy-done.6, ...), custom_call_target="tpu_custom_call" | custom-call | tf_op jit(solution)/shard_map/pallas_call | solution.py:324
  63.8 2.8 %collective-permute-start.1 = (bf16[256,128]{1,0:T(8,128)(2,1)S(1)}, bf16[256,128]{1,0:T(8,128)(2,1)S(1)}, u32[]{:S(2)}, u32[]{:S(2)}) collective-permute-start(bf16[256,128]{1,0:T(8,128)(2,1)S(1)} %get-tuple-element.31), channel_id=1, source_target_pairs={{1,0},{2,1},{3,2},{4,3},{5,4},{6,5},{7,6},{8,7},{9,8},{10,9},{11,1... | collective-permute-start | bytes 196616 | tf_op jit(solution)/shard_map/ppermute | solution.py:393
  66.6 1.3 %collective-permute-start.2 = (bf16[256,128]{1,0:T(8,128)(2,1)S(1)}, bf16[256,128]{1,0:T(8,128)(2,1)S(1)}, u32[]{:S(2)}, u32[]{:S(2)}) collective-permute-start(bf16[256,128]{1,0:T(8,128)(2,1)S(1)} %get-tuple-element.32), channel_id=1, source_target_pairs={{2,0},{3,1},{4,2},{5,3},{6,4},{7,5},{8,6},{9,7},{10,8},{11,9},{12,... | collective-permute-start | bytes 196616 | tf_op jit(solution)/shard_map/ppermute | solution.py:393
  67.9 1.7 %collective-permute-done.1.a_ref = bf16[256,128]{1,0:T(8,128)(2,1)S(1)} collective-permute-done((bf16[256,128]{1,0:T(8,128)(2,1)S(1)}, bf16[256,128]{1,0:T(8,128)(2,1)S(1)}, u32[]{:S(2)}, u32[]{:S(2)}) %collective-permute-start.1) | collective-permute-done | bytes 65568 | tf_op jit(solution)/shard_map/ppermute | solution.py:393
  69.6 2.7 %collective-permute-done.2.b_ref = bf16[256,128]{1,0:T(8,128)(2,1)S(1)} collective-permute-done((bf16[256,128]{1,0:T(8,128)(2,1)S(1)}, bf16[256,128]{1,0:T(8,128)(2,1)S(1)}, u32[]{:S(2)}, u32[]{:S(2)}) %collective-permute-start.2) | collective-permute-done | bytes 65568 | tf_op jit(solution)/shard_map/ppermute | solution.py:393
  72.3 0.0 all-to-all-done.4.c_ref
  72.3 2.3 %shard_map.117 = (f32[8,32,128]{2,1,0:T(8,128)}, bf16[8,64,128]{2,1,0:T(8,128)(2,1)S(1)}, f32[256,128]{1,0:T(8,128)S(1)}) custom-call(bf16[8,288,128]{2,1,0:T(8,128)(2,1)S(1)} %all_to_all.40.r_ref.row_ref, bf16[128,256]{1,0:T(8,128)(2,1)S(1)} %copy-done.1, bf16[8,96,128]{2,1,0:T(8,128)(2,1)S(1)} %all-to-all-done.3.r_ref, ...), custom_call_target="tpu_custom_call" | custom-call | tf_op jit(solution)/shard_map/pallas_call | solution.py:324
  74.7 6.7 %all-to-all-start.5 = ((f32[8,32,128]{2,1,0:T(8,128)}), f32[8,32,128]{2,1,0:T(8,128)S(1)}, u32[]{:S(2)}, u32[]{:S(2)}) async-start(f32[8,32,128]{2,1,0:T(8,128)} %get-tuple-element.33), calls=%async_computation.5 | async-start | bytes 262144 | tf_op jit(solution)/shard_map/all_to_all | solution.py:338
  81.3 1.3 %collective-permute-start.3 = (bf16[256,128]{1,0:T(8,128)(2,1)S(1)}, bf16[256,128]{1,0:T(8,128)(2,1)S(1)}, u32[]{:S(2)}, u32[]{:S(2)}) collective-permute-start(bf16[256,128]{1,0:T(8,128)(2,1)S(1)} %get-tuple-element.34), channel_id=1, source_target_pairs={{3,0},{4,1},{5,2},{6,3},{7,4},{8,5},{9,6},{10,7},{11,8},{12,9},{13... | collective-permute-start | bytes 196616 | tf_op jit(solution)/shard_map/ppermute | solution.py:393
  82.6 1.3 %collective-permute-start.4 = (bf16[256,128]{1,0:T(8,128)(2,1)S(1)}, bf16[256,128]{1,0:T(8,128)(2,1)S(1)}, u32[]{:S(2)}, u32[]{:S(2)}) collective-permute-start(bf16[256,128]{1,0:T(8,128)(2,1)S(1)} %get-tuple-element.35), channel_id=1, source_target_pairs={{4,0},{5,1},{6,2},{7,3},{8,4},{9,5},{10,6},{11,7},{12,8},{13,9},{1... | collective-permute-start | bytes 196616 | tf_op jit(solution)/shard_map/ppermute | solution.py:393
  83.9 4.8 %collective-permute-done.3.a_ref = bf16[256,128]{1,0:T(8,128)(2,1)S(1)} collective-permute-done((bf16[256,128]{1,0:T(8,128)(2,1)S(1)}, bf16[256,128]{1,0:T(8,128)(2,1)S(1)}, u32[]{:S(2)}, u32[]{:S(2)}) %collective-permute-start.3) | collective-permute-done | bytes 65568 | tf_op jit(solution)/shard_map/ppermute | solution.py:393
  88.7 1.6 %collective-permute-done.4.b_ref = bf16[256,128]{1,0:T(8,128)(2,1)S(1)} collective-permute-done((bf16[256,128]{1,0:T(8,128)(2,1)S(1)}, bf16[256,128]{1,0:T(8,128)(2,1)S(1)}, u32[]{:S(2)}, u32[]{:S(2)}) %collective-permute-start.4) | collective-permute-done | bytes 65568 | tf_op jit(solution)/shard_map/ppermute | solution.py:393
  90.3 0.0 all-to-all-done.5.r_ref
  90.3 17.8 %all_to_all.43.r_ref = f32[8,32,128]{2,1,0:T(8,128)S(1)} all-to-all(f32[8,32,128]{2,1,0:T(8,128)S(1)} %get-tuple-element.37), channel_id=1, replica_groups=mesh['heads'=8,'ctx'=64] {'heads'}, dimensions={0} | all-to-all | bytes 262144 | tf_op jit(solution)/shard_map/all_to_all | solution.py:338
  108.2 14.9 %all_to_all.44.r_ref = bf16[8,128,128]{2,1,0:T(8,128)(2,1)S(1)} all-to-all(bf16[8,128,128]{2,1,0:T(8,128)(2,1)S(1)} %shard_map.119), channel_id=1, replica_groups={{0,1,2,3,4,5,6,7},{8,9,10,11,12,13,14,15},{16,17,18,19,20,21,22,23},{24..., dimensions={0} | all-to-all | bytes 524288 | tf_op jit(solution)/shard_map/all_to_all | solution.py:338
  123.0 1.1 shard_map.120
  (4 shorter events, 0.1 us)
Async XLA Ops:
  0.6 0.8 copy-start
  1.5 0.8 copy-start.2
  2.2 0.8 copy-start.4
  33.8 10.2 %copy-start.7 = (bf16[1,128,512]{2,1,0:T(8,128)(2,1)S(1)}, bf16[1,128,512]{2,1,0:T(8,128)(2,1)}, u32[]{:S(2)}) copy-start(bf16[1,128,512]{2,1,0:T(8,128)(2,1)} %g_ref.3) | copy-start | bytes 393220
  33.8 10.2 %copy-start.8 = (f32[1,512]{1,0:T(1,128)S(1)}, f32[1,512]{1,0:T(1,128)}, u32[]{:S(2)}) copy-start(f32[1,512]{1,0:T(1,128)} %gl_ref.1) | copy-start | bytes 6148
  33.9 10.2 %copy-start.1 = (bf16[128,256]{1,0:T(8,128)(2,1)S(1)}, bf16[128,256]{1,0:T(8,128)(2,1)}, u32[]{:S(2)}) copy-start(bf16[128,256]{1,0:T(8,128)(2,1)} %w_ref.5) | copy-start | bytes 196612
  33.9 10.2 %copy-start.3 = (bf16[1,128,128]{2,1,0:T(8,128)(2,1)S(1)}, bf16[1,128,128]{2,1,0:T(8,128)(2,1)}, u32[]{:S(2)}) copy-start(bf16[1,128,128]{2,1,0:T(8,128)(2,1)} %k_ref.5) | copy-start | bytes 98308
  33.9 10.2 %copy-start.5 = (bf16[1,128,128]{2,1,0:T(8,128)(2,1)S(1)}, bf16[1,128,128]{2,1,0:T(8,128)(2,1)}, u32[]{:S(2)}) copy-start(bf16[1,128,128]{2,1,0:T(8,128)(2,1)} %v_ref.5) | copy-start | bytes 98308
  33.9 10.2 %copy-start.6 = (bf16[1,128,512]{2,1,0:T(8,128)(2,1)S(1)}, bf16[1,128,512]{2,1,0:T(8,128)(2,1)}, u32[]{:S(2)}) copy-start(bf16[1,128,512]{2,1,0:T(8,128)(2,1)} %q_ref.3) | copy-start | bytes 393220
  46.8 10.0 %all-to-all-start.3 = ((bf16[8,96,128]{2,1,0:T(8,128)(2,1)}), bf16[8,96,128]{2,1,0:T(8,128)(2,1)S(1)}, u32[]{:S(2)}, u32[]{:S(2)}) async-start(bf16[8,96,128]{2,1,0:T(8,128)(2,1)} %get-tuple-element.30), calls=%async_computation.3 | async-start | bytes 393216 | tf_op jit(solution)/shard_map/all_to_all | solution.py:338
  50.9 9.9 %collective-permute-start = (bf16[4,256,128]{2,1,0:T(8,128)(2,1)S(1)}, bf16[4,256,128]{2,1,0:T(8,128)(2,1)S(1)}, u32[]{:S(2)}, u32[]{:S(2)}) collective-permute-start(bf16[4,256,128]{2,1,0:T(8,128)(2,1)S(1)} %get-tuple-element.25), channel_id=1, source_target_pairs={{0,8},{1,9},{2,10},{3,11},{4,12},{5,13},{6,14},{7,15},{8,16},{9,17... | collective-permute-start | bytes 786440 | tf_op jit(solution)/shard_map/ppermute | solution.py:367
  57.5 14.9 %all-to-all-start.4 = ((f32[8,32,128]{2,1,0:T(8,128)}), f32[8,32,128]{2,1,0:T(8,128)S(1)}, u32[]{:S(2)}, u32[]{:S(2)}) async-start(f32[8,32,128]{2,1,0:T(8,128)} %shard_map.116), calls=%async_computation.4 | async-start | bytes 262144 | tf_op jit(solution)/shard_map/all_to_all | solution.py:338
  60.9 0.7 copy-start.10
  60.9 0.7 copy-start.9
  63.8 5.9 %collective-permute-start.1 = (bf16[256,128]{1,0:T(8,128)(2,1)S(1)}, bf16[256,128]{1,0:T(8,128)(2,1)S(1)}, u32[]{:S(2)}, u32[]{:S(2)}) collective-permute-start(bf16[256,128]{1,0:T(8,128)(2,1)S(1)} %get-tuple-element.31), channel_id=1, source_target_pairs={{1,0},{2,1},{3,2},{4,3},{5,4},{6,5},{7,6},{8,7},{9,8},{10,9},{11,1... | collective-permute-start | bytes 196616 | tf_op jit(solution)/shard_map/ppermute | solution.py:393
  66.6 5.7 %collective-permute-start.2 = (bf16[256,128]{1,0:T(8,128)(2,1)S(1)}, bf16[256,128]{1,0:T(8,128)(2,1)S(1)}, u32[]{:S(2)}, u32[]{:S(2)}) collective-permute-start(bf16[256,128]{1,0:T(8,128)(2,1)S(1)} %get-tuple-element.32), channel_id=1, source_target_pairs={{2,0},{3,1},{4,2},{5,3},{6,4},{7,5},{8,6},{9,7},{10,8},{11,9},{12,... | collective-permute-start | bytes 196616 | tf_op jit(solution)/shard_map/ppermute | solution.py:393
  74.7 15.6 %all-to-all-start.5 = ((f32[8,32,128]{2,1,0:T(8,128)}), f32[8,32,128]{2,1,0:T(8,128)S(1)}, u32[]{:S(2)}, u32[]{:S(2)}) async-start(f32[8,32,128]{2,1,0:T(8,128)} %get-tuple-element.33), calls=%async_computation.5 | async-start | bytes 262144 | tf_op jit(solution)/shard_map/all_to_all | solution.py:338
  81.3 7.4 %collective-permute-start.3 = (bf16[256,128]{1,0:T(8,128)(2,1)S(1)}, bf16[256,128]{1,0:T(8,128)(2,1)S(1)}, u32[]{:S(2)}, u32[]{:S(2)}) collective-permute-start(bf16[256,128]{1,0:T(8,128)(2,1)S(1)} %get-tuple-element.34), channel_id=1, source_target_pairs={{3,0},{4,1},{5,2},{6,3},{7,4},{8,5},{9,6},{10,7},{11,8},{12,9},{13... | collective-permute-start | bytes 196616 | tf_op jit(solution)/shard_map/ppermute | solution.py:393
  82.6 7.7 %collective-permute-start.4 = (bf16[256,128]{1,0:T(8,128)(2,1)S(1)}, bf16[256,128]{1,0:T(8,128)(2,1)S(1)}, u32[]{:S(2)}, u32[]{:S(2)}) collective-permute-start(bf16[256,128]{1,0:T(8,128)(2,1)S(1)} %get-tuple-element.35), channel_id=1, source_target_pairs={{4,0},{5,1},{6,2},{7,3},{8,4},{9,5},{10,6},{11,7},{12,8},{13,9},{1... | collective-permute-start | bytes 196616 | tf_op jit(solution)/shard_map/ppermute | solution.py:393

commit v5 on v4

--- a/solution.py
+++ b/solution.py
@@ -70,13 +70,6 @@
 
 def whole(value):
     return value.reshape(value.shape[0] * value.shape[1], value.shape[2])
-
-
-def store_split(ref, at, value):
-    step = value.shape[1]
-    high, low = split(value)
-    ref[:, at : at + step] = high
-    ref[:, at + step : at + 2 * step] = low
 
 
 def send_state_kernel(k_hbm, v_hbm, w_hbm, o_ref, k_ref, v_ref, w_ref, sem):
@@ -103,8 +96,9 @@
 
 def row_total_kernel(r_ref, o_ref, kv_ref):
     step = o_ref.shape[1]
-    total = jnp.sum(r_ref[:, :step].astype(F32), axis=0)
-    o_ref[...] = jnp.broadcast_to(total[None], o_ref.shape)
+    total = jnp.sum(r_ref[:, :step].astype(F32), axis=0).astype(BF16)
+    for place in range(SIDE):
+        o_ref[place] = total
     kv_ref[...] = r_ref[SIDE // 2 :, step:]
 
 
@@ -113,9 +107,9 @@
     line = spots()[0]
     total = jnp.zeros(c_ref.shape[1:], F32)
     for source in range(SIDE):
-        total = total + flag(source < line) * c_ref[source]
+        total = total + flag(source < line) * c_ref[source].astype(F32)
     for spot in range(SIDE):
-        o_ref[spot, :step], o_ref[spot, step:] = split(total)
+        o_ref[spot] = total.astype(BF16)
         total = total + r_ref[spot, :step].astype(F32)
 
 
@@ -140,49 +134,57 @@
     return (row & (length - 1)) >= col
 
 
+def local_kernel(
+    q_ref, k_ref, w_ref, feat_ref, kf_ref, lw_ref,
+):
+    keys = k_ref[0]
+    w = w_ref[...]
+    length, size = keys.shape
+    queries = stacked(q_ref, size)
+    feat = features(nn(queries, w))[0]
+    key_feat = features(nn(keys, w))[0]
+    causal = causal_mask(queries.shape[0], length)
+    scores = nt(feat.astype(BF16), key_feat.astype(BF16))
+    feat_ref[...] = feat
+    kf_ref[...] = key_feat
+    lw_ref[...] = jnp.where(causal, scores, 0.0).astype(BF16)
+
+
 def linear_kernel(
-    q_ref, k_ref, v_ref, g_ref, gl_ref, w_ref, r_ref, send_ref, kloc_ref, ql_ref, vl_ref
+    q_ref, k_ref, v_ref, g_ref, gl_ref, r_ref, feat_ref, kf_ref, lw_ref,
+    send_ref, kloc_ref, rg_ref, lg_ref,
 ):
     keys = k_ref[0]
     values = v_ref[0]
-    w = w_ref[...]
     length, size = keys.shape
-    step = r_ref.shape[1] // 2
+    step = r_ref.shape[1]
     queries = stacked(q_ref, size)
+    state = whole(r_ref[...])
+    slope = jnp.minimum(feat_ref[...], 1.0)
+    key_slope = jnp.minimum(kf_ref[...], 1.0)
+    feat = feat_ref[...].astype(BF16)
+    key_feat = kf_ref[...].astype(BF16)
     upstream = stacked(g_ref, size).astype(F32)
-    state_high = whole(r_ref[:, :step])
-    state_low = whole(r_ref[:, step:])
-    raw = nn(queries, w)
-    feat, slope = features(raw)
-    feat = feat.astype(BF16)
-    key_feat, key_slope = features(nn(keys, w))
-    key_feat = key_feat.astype(BF16)
-    causal = causal_mask(queries.shape[0], length)
-    weights = jnp.where(causal, nt(feat, key_feat), 0.0).astype(BF16)
-    lin_out = nn(feat, state_high) + nn(feat, state_low) + nn(weights, values)
+    lin_out = nn(feat, state) + nn(lw_ref[...], values)
     lin_grad = norm_backward(lin_out, upstream * gains(gl_ref, length, size))
     lin_high, lin_low = split(lin_grad)
+    causal = causal_mask(queries.shape[0], length)
     score_grad = jnp.where(causal, nt(lin_high, values), 0.0).astype(BF16)
-    feat_grad = (
-        nt(lin_high, state_high)
-        + nt(lin_high, state_low)
-        + nt(lin_low, state_high)
-        + nn(score_grad, key_feat)
-    )
+    feat_grad = nt(lin_high, state) + nt(lin_low, state) + nn(score_grad, key_feat)
     raw_grad = (feat_grad * slope).astype(BF16)
-    ql_ref[...] = nt(raw_grad, w)
+    rg_ref[...] = raw_grad
+    lg_ref[...] = lin_high
     key_local = tn(score_grad, feat)
     kloc_ref[...] = key_local
-    vl_ref[...] = tn(weights, lin_high)
     send_ref[:, :step] = pieces(tn(feat, lin_high) + tn(feat, lin_low)).astype(BF16)
     local_high, local_low = split(key_local * key_slope)
     early = tn(raw_grad, queries) + tn(local_high, keys) + tn(local_low, keys)
-    store_split(send_ref, step, pieces(early))
+    send_ref[:, step:] = pieces(early.astype(BF16))
 
 
 def sparse_kernel(
-    q_ref, k_ref, v_ref, g_ref, gs_ref, kb_ref, row_ref, prev_ref, ql_ref, vl_ref,
-    qo_ref, dk_ref, dv_ref, *back_refs,
+    q_ref, k_ref, v_ref, g_ref, gs_ref, kb_ref, row_ref, prev_ref,
+    qs_ref, back_ref, dk_ref, dv_ref,
 ):
     spot, shard = spots()[1:]
     keys = k_ref[0]
@@ -190,7 +192,6 @@
     length, size = keys.shape
     scaling = size ** (-0.5)
     queries = stacked(q_ref, size)
-    heads = queries.shape[0] // length
     upstream = stacked(g_ref, size).astype(F32)
     causal = causal_mask(queries.shape[0], length)
     reaches = kb_ref.shape[1]
@@ -228,92 +229,115 @@
     inner = jnp.sum(sparse_grad.astype(F32) * sparse_out, axis=1, keepdims=True)
     near_grad = (scaling * near_probs * (nt(sparse_grad, values) - inner)).astype(BF16)
     far_grad = (scaling * far_probs * (nt(sparse_grad, value_far) - inner)).astype(BF16)
-    query_out = nn(near_grad, keys) + nn(far_grad, key_far) + ql_ref[...]
-    for h in range(heads):
-        qo_ref[0, :, h * size : (h + 1) * size] = query_out[
-            h * length : (h + 1) * length
-        ].astype(BF16)
+    qs_ref[...] = nn(near_grad, keys) + nn(far_grad, key_far)
     dk_ref[...] = tn(near_grad, queries)
-    dv_ref[...] = tn(near_half, sparse_grad) + vl_ref[...]
+    dv_ref[...] = tn(near_half, sparse_grad)
     key_back = tn(far_grad, queries).astype(BF16)
     value_back = tn(far_half, sparse_grad).astype(BF16)
     for reach in range(reaches):
         part = slice(reach * length, (reach + 1) * length)
-        back_refs[reach][:length] = key_back[part]
-        back_refs[reach][length:] = value_back[part]
+        back_ref[reach, :length] = key_back[part]
+        back_ref[reach, length:] = value_back[part]
+
+
+def finish_kernel(w_ref, rg_ref, lg_ref, lw_ref, qs_ref, dv_ref, qo_ref, vo_ref):
+    length, size = dv_ref.shape
+    query_out = qs_ref[...] + nt(rg_ref[...], w_ref[...])
+    for h in range(qs_ref.shape[0] // length):
+        qo_ref[0, :, h * size : (h + 1) * size] = query_out[
+            h * length : (h + 1) * length
+        ].astype(BF16)
+    vo_ref[...] = dv_ref[...] + tn(lw_ref[...], lg_ref[...])
 
 
 def total_kernel(r_ref, o_ref):
     step = o_ref.shape[1]
-    total = jnp.sum(r_ref[:, :step].astype(F32), axis=0)
-    o_ref[...] = jnp.broadcast_to(total[None], o_ref.shape)
-
-
-def weight_part_kernel(row_ref, w_ref, r_ref, c_ref, a_ref, b_ref, send_ref, o_ref, sum_ref):
-    line, spot = spots()[:2]
-    step, _ = c_ref.shape[1:]
-    length = (row_ref.shape[1] - step) // 2
+    total = jnp.sum(r_ref[:, :step].astype(F32), axis=0).astype(BF16)
+    for place in range(SIDE):
+        o_ref[place] = total
+
+
+def slope_kernel(row_ref, w_ref, slope_ref):
+    spot = spots()[1]
     w = w_ref[...]
+    step, length = slope_ref.shape[1:]
     row, col = iotas((step, w.shape[1]))
     own = nt(ones_where(col == row + step * spot), w).astype(BF16)
+    for source in range(SIDE):
+        slope_ref[source] = features(nt(own, row_ref[source, step : step + length]))[1]
+
+
+def weight_part_kernel(
+    row_ref, slope_ref, r_ref, c_ref, own_ref, back_ref, send_ref, o_ref, far_ref
+):
+    line, spot = spots()[:2]
+    step, length = slope_ref.shape[1:]
     total = jnp.zeros(c_ref.shape[1:], F32)
     for source in range(SIDE):
-        total = total + flag(source > line) * c_ref[source]
-    weight = jnp.zeros(c_ref.shape[1:], F32)
+        total = total + flag(source > line) * c_ref[source].astype(F32)
+    weight = jnp.sum(r_ref[:, step:].astype(F32), axis=0)
     for source in range(SIDE - 1, -1, -1):
         high, low = split(total)
-        o_ref[source, :step] = high
-        o_ref[source, step:] = low
+        o_ref[source] = high
         keys = row_ref[source, step : step + length]
         values = row_ref[source, step + length :]
-        slope = features(nt(own, keys))[1]
+        slope = slope_ref[source]
         grad_high, grad_low = split((nt(high, values) + nt(low, values)) * slope)
         weight = weight + nn(grad_high, keys) + nn(grad_low, keys)
-        for place in (1, 2):
-            weight = weight + r_ref[source, place * step : (place + 1) * step].astype(F32)
         total = total + r_ref[source, :step].astype(F32)
-    send_ref[...] = jnp.broadcast_to(weight[None], send_ref.shape)
-    sum_ref[...] = a_ref[...].astype(F32) + b_ref[...].astype(F32)
-
-
-def column_sum_kernel(r_ref, a_ref, b_ref, in_ref, o_ref, sum_ref):
-    sum_ref[...] = in_ref[...] + a_ref[...].astype(F32) + b_ref[...].astype(F32)
-    o_ref[...] = jnp.broadcast_to(jnp.sum(r_ref[...], axis=0)[None], o_ref.shape)
+    weight = weight.astype(BF16)
+    for place in range(SIDE):
+        send_ref[place] = weight
+    far_ref[...] = jnp.zeros(far_ref.shape, BF16)
+    for reach in range(1, own_ref.shape[0] + 1):
+
+        @pl.when(spot >= reach)
+        def _():
+            far_ref[spot - reach] = own_ref[reach - 1]
+
+        @pl.when(spot < reach)
+        def _():
+            far_ref[spot - reach + SIDE] = back_ref[reach - 1]
+
+
+def column_sum_kernel(r_ref, o_ref):
+    total = jnp.sum(r_ref[...].astype(F32), axis=0).astype(BF16)
+    for place in range(o_ref.shape[0]):
+        o_ref[place] = total
 
 
 def make_last_kernel(scale):
-    def last_kernel(r_ref, carried_ref, o_ref):
+    def last_kernel(r_ref, carried_ref, far_ref, o_ref):
         step = r_ref.shape[1]
-        high, low = split(jnp.sum(r_ref[...], axis=0) * scale)
-        o_ref[:, : 2 * step] = carried_ref[...]
-        o_ref[:, 2 * step : 3 * step] = jnp.broadcast_to(high[None], (SIDE, *high.shape))
-        o_ref[:, 3 * step : 4 * step] = jnp.broadcast_to(low[None], (SIDE, *low.shape))
+        high, low = split(jnp.sum(r_ref[...].astype(F32), axis=0) * scale)
+        o_ref[:, :step] = carried_ref[...]
+        for spot in range(SIDE):
+            o_ref[spot, step : 2 * step] = high
+            o_ref[spot, 2 * step : 3 * step] = low
+        o_ref[:, 3 * step :] = far_ref[...]
 
     return last_kernel
 
 
 def key_kernel(
-    k_ref, v_ref, w_ref, r_ref, kloc_ref, dk_ref, dv_ref, back_ref, ko_ref, vo_ref, wo_ref
+    k_ref, v_ref, w_ref, r_ref, kloc_ref, dk_ref, dv_ref, ko_ref, vo_ref, wo_ref
 ):
     keys = k_ref[0]
     values = v_ref[0]
     w = w_ref[...]
     step = w.shape[1] // SIDE
     length = keys.shape[0]
-    carried_high = whole(r_ref[:, :step])
-    carried_low = whole(r_ref[:, step : 2 * step])
-    weight = whole(r_ref[:, 2 * step : 3 * step]).astype(F32)
-    weight = weight + whole(r_ref[:, 3 * step : 4 * step]).astype(F32)
+    carried = whole(r_ref[:, :step])
+    weight = whole(r_ref[:, step : 2 * step]).astype(F32)
+    weight = weight + whole(r_ref[:, 2 * step : 3 * step]).astype(F32)
     wo_ref[...] = weight.T
-    back = back_ref[...]
+    back = jnp.sum(r_ref[:, 3 * step :].astype(F32), axis=0)
     feat, slope = features(nn(keys, w))
     feat = feat.astype(BF16)
-    feat_grad = nt(values, carried_high) + nt(values, carried_low) + kloc_ref[...]
+    feat_grad = nt(values, carried) + kloc_ref[...]
     raw_grad = (feat_grad * slope).astype(BF16)
     ko_ref[0] = (dk_ref[...] + back[:length] + nt(raw_grad, w)).astype(BF16)
-    vo_ref[0] = (
-        dv_ref[...] + back[length:] + nn(feat, carried_high) + nn(feat, carried_low)
-    ).astype(BF16)
+    vo_ref[0] = (dv_ref[...] + back[length:] + nn(feat, carried)).astype(BF16)
 
 
 def call(kernel, *outs, grant=8, space=pltpu.VMEM, scratch=()):
@@ -349,11 +373,10 @@
     in_column = [[line * SIDE + spot for line in range(shards // SIDE)] for spot in range(SIDE)]
     half = (SIDE // 2, 2 * length, size)
     piece = (SIDE, step, size)
-    two = (SIDE, 2 * step, size)
     down = [(i, i + SIDE) for i in range(shards - SIDE)]
     rows = (queries.shape[2] // size * length, size)
     square = (length, size)
-    both = (2 * length, size)
+    pair = (SIDE, 2 * length, size)
     sent = call(
         send_state_kernel,
         ((SIDE, step + 2 * length, size), BF16),
@@ -362,50 +385,56 @@
         + [pltpu.SemaphoreType.DMA((3,))],
     )(keys, values, w_feat)
     row = swap(sent, "ctx", in_row)
-    sent, moved = call(row_total_kernel, (piece, F32), (half, BF16))(row)
+    sent, moved = call(row_total_kernel, (piece, BF16), (half, BF16))(row)
     got = swap(sent, "ctx", in_column)
     previous = lax.ppermute(moved, "ctx", down)
-    sent = call(prefix_kernel, (two, BF16))(row, got)
+    sent = call(prefix_kernel, (piece, BF16))(row, got)
     got = swap(sent, "ctx", in_row)
-    sent, key_local, query_lin, value_local = call(
-        linear_kernel,
-        ((SIDE, 3 * step, size), BF16),
+    local = call(
+        local_kernel,
+        ((rows[0], features_n), F32),
         ((length, features_n), F32),
+        ((rows[0], length), BF16),
+    )(queries, keys, w_feat)
+    query_sparse, back, key_near, value_near = call(
+        sparse_kernel,
         (rows, F32),
-        (square, F32),
-        grant=16,
-    )(queries, keys, values, out_grad, gain_lin, w_feat, got)
-    cots = swap(sent, "ctx", in_row)
-    query_out, key_near, value_near, *backs = call(
-        sparse_kernel,
-        (queries.shape, BF16),
+        ((key_blocks.shape[2], 2 * length, size), BF16),
         (square, F32),
         (square, F32),
-        *[((2 * length, size), BF16)] * key_blocks.shape[2],
-        grant=24,
+        grant=12,
     )(
         queries, keys, values, out_grad, gain_sparse, jnp.swapaxes(key_blocks, 1, 2),
-        row, previous, query_lin, value_local,
-    )
-    far = []
-    for reach, back in enumerate(backs, 1):
-        pairs = [(i, i - reach) for i in range(reach, shards)]
-        far.append(lax.ppermute(back, "ctx", pairs))
-    sent = call(total_kernel, (piece, F32))(cots)
+        row, previous,
+    )
+    slopes = call(slope_kernel, ((SIDE, step, length), F32))(row, w_feat)
+    sent, key_local, raw_grad, lin_grad = call(
+        linear_kernel,
+        ((SIDE, 2 * step, size), BF16),
+        ((length, features_n), F32),
+        ((rows[0], features_n), BF16),
+        (rows, BF16),
+    )(queries, keys, values, out_grad, gain_lin, got, *local)
+    cots = swap(sent, "ctx", in_row)
+    returned = lax.ppermute(back, "ctx", [(b, a) for a, b in down])
+    query_out, value_near = call(finish_kernel, (queries.shape, BF16), (square, F32))(
+        w_feat, raw_grad, lin_grad, local[2], query_sparse, value_near
+    )
+    sent = call(total_kernel, (piece, BF16))(cots)
     got = swap(sent, "ctx", in_column)
-    sent, carried, back = call(
-        weight_part_kernel, (piece, F32), (two, BF16), (both, F32)
-    )(row, w_feat, cots, got, far[0], far[1])
+    sent, carried, far = call(
+        weight_part_kernel, (piece, BF16), (piece, BF16), (pair, BF16)
+    )(row, slopes, cots, got, back, returned)
     got = swap(sent, "ctx", in_column)
-    sent, back = call(column_sum_kernel, ((groups, step, size), F32), (both, F32))(
-        got, far[2], far[3], back
-    )
+    sent = call(column_sum_kernel, ((groups, step, size), BF16))(got)
     got = swap(sent, "heads")
-    sent = call(make_last_kernel(scale), ((SIDE, 4 * step, size), BF16))(got, carried)
+    sent = call(make_last_kernel(scale), ((SIDE, 3 * step + 2 * length, size), BF16))(
+        got, carried, far
+    )
     got = swap(sent, "ctx", in_row)
     key_out, value_out, weight = call(
         key_kernel, (keys.shape, BF16), (values.shape, BF16), (w_feat.shape, F32)
-    )(keys, values, w_feat, got, key_local, key_near, value_near, back)
+    )(keys, values, w_feat, got, key_local, key_near, value_near)
     return query_out, key_out, value_out, weight
 
 

time: 126 us -> 120 us (0.952); the launches traced: 124 us -> 119 us
  blocking collectives: 73.1 us -> 66.1 us
  waiting for transfers between devices: 14.6 us -> 18.6 us
  starting transfers between devices: 22.9 us -> 21.5 us
    all_to_all x3, waiting for transfers between devices: 3.86 us -> 18.6 us  [swap(): lax.all_to_all(value, axis, 0, 0, axis_index_groups=groups, tiled=False)]
    ppermute x4 -> x1, waiting for transfers between devices: 10.8 us -> 0.01 us  [per_device(): returned = lax.ppermute(back, 'ctx', [(b, a) for a, b in down])]
    all_to_all x5, blocking collectives: 73.1 us -> 66.1 us  [swap(): lax.all_to_all(value, axis, 0, 0, axis_index_groups=groups, tiled=False)]
    ppermute x4 -> x1, starting transfers between devices: 6.71 us -> 1.29 us  [per_device(): returned = lax.ppermute(back, 'ctx', [(b, a) for a, b in down])]
    all_to_all x3, starting transfers between devices: 14.2 us -> 18.9 us  [swap(): lax.all_to_all(value, axis, 0, 0, axis_index_groups=groups, tiled=False)]
    pallas_call x10 -> x13, Pallas kernels: 9.61 us -> 9.45 us  [run(): pl.pallas_call(kernel, out_shape=shapes if len(shapes) > 1 else shapes[0]...]
  transfers between devices with their start and end apart: 8 -> 5, of which waited for: 5 -> 3; matrix products, arithmetic and copies ran while one was open for 0% -> 0% of each run, Pallas kernels for 2% -> 5%
where the time goes in v5:
time: 120 us; the launch traced here: 119 us
  blocking collectives  66.1 us (55%)
  starting transfers between devices  21.5 us (18%)
  waiting for transfers between devices  18.6 us (16%)
  Pallas kernels  9.45 us (8%)
  local copies, waits for them, and re-layouts  3.06 us (3%)
    all_to_all x5, blocking collectives, swap(): lax.all_to_all(value, axis, 0, 0, axis_index_groups=groups, tiled=False)  66.1 us
    all_to_all x3, starting transfers between devices, swap(): lax.all_to_all(value, axis, 0, 0, axis_index_groups=groups, tiled=False)  18.9 us
    all_to_all x3, waiting for transfers between devices, swap(): lax.all_to_all(value, axis, 0, 0, axis_index_groups=groups, tiled=False)  18.6 us
    pallas_call x13, Pallas kernels, run(): pl.pallas_call(kernel, out_shape=shapes if len(shapes) > 1 else shapes[0]...  9.45 us
    unnamed x22, local copies, waits for them, and re-layouts  3.06 us
  transfers between devices with their start and end apart: 5, of which 3 were waited for; matrix products, arithmetic and copies ran while one was open for 0% of the time, Pallas kernels for 5%

profile of v5, /device:TPU:1, one launch (start us, length us, event | category | flops | bytes accessed | tf_op | source)
XLA Modules:
  0.0 119.5 jit_solution(10911128765631037717)
XLA Ops:
  0.6 0.0 copy-start
  0.6 0.8 copy-done
  1.5 0.0 copy-start.3
  1.5 0.8 copy-done.3
  2.2 0.0 copy-start.6
  2.2 0.8 copy-done.6
  3.0 0.5 shard_map.111
  3.5 19.5 %all_to_all.40.r_ref.row_ref = bf16[8,288,128]{2,1,0:T(8,128)(2,1)S(1)} all-to-all(bf16[8,288,128]{2,1,0:T(8,128)(2,1)S(1)} %shard_map.111), channel_id=1, replica_groups={{0,1,2,3,4,5,6,7},{8,9,10,11,12,13,14,15},{16,17,18,19,20,21,22,23},{24..., dimensions={0} | all-to-all | bytes 1179648 | tf_op jit(solution)/shard_map/all_to_all | solution.py:362
  23.1 1.3 %collective-permute-start = (bf16[4,256,128]{2,1,0:T(8,128)(2,1)S(1)}, bf16[4,256,128]{2,1,0:T(8,128)(2,1)S(1)}, u32[]{:S(2)}, u32[]{:S(2)}) collective-permute-start(bf16[4,256,128]{2,1,0:T(8,128)(2,1)S(1)} %get-tuple-element.31), channel_id=1, source_target_pairs={{0,8},{1,9},{2,10},{3,11},{4,12},{5,13},{6,14},{7,15},{8,16},{9,17... | collective-permute-start | bytes 786440 | tf_op jit(solution)/shard_map/ppermute | solution.py:390
  24.4 11.2 %all_to_all.41.c_ref = bf16[8,32,128]{2,1,0:T(8,128)(2,1)S(1)} all-to-all(bf16[8,32,128]{2,1,0:T(8,128)(2,1)S(1)} %get-tuple-element.25), channel_id=1, replica_groups={{0,8,16,24,32,40,48,56},{1,9,17,25,33,41,49,57},{2,10,18,26,34,42,50,58..., dimensions={0} | all-to-all | bytes 131072 | tf_op jit(solution)/shard_map/all_to_all | solution.py:362
  35.6 0.0 copy-start.4
  35.6 0.0 copy-start.5
  35.6 0.0 copy-start.7
  35.6 0.0 copy-start.8
  35.6 0.0 copy-start.9
  35.6 0.7 shard_map.113
  36.3 0.0 copy-start.2
  36.3 5.8 %all-to-all-start.2 = ((bf16[8,32,128]{2,1,0:T(8,128)(2,1)}), bf16[8,32,128]{2,1,0:T(8,128)(2,1)S(1)}, u32[]{:S(2)}, u32[]{:S(2)}) async-start(bf16[8,32,128]{2,1,0:T(8,128)(2,1)} %shard_map.113), calls=%async_computation.2 | async-start | bytes 131072 | tf_op jit(solution)/shard_map/all_to_all | solution.py:362
  42.2 0.0 collective-permute-done.prev_ref
  42.2 0.0 copy-done.4
  42.2 0.0 copy-done.5
  42.2 0.0 copy-done.7
  42.2 0.0 copy-done.8
  42.2 0.0 copy-done.9
  42.2 0.0 copy-done.2
  42.2 0.0 copy-start.1
  42.2 1.8 %shard_map.116 = (f32[512,128]{1,0:T(8,128)S(1)}, bf16[4,256,128]{2,1,0:T(8,128)(2,1)S(1)}, f32[128,128]{1,0:T(8,128)S(1)}, f32[128,128]{1,0:T(8,128)S(1)}) custom-call(bf16[1,128,512]{2,1,0:T(8,128)(2,1)S(1)} %copy-done.2, bf16[1,128,128]{2,1,0:T(8,128)(2,1)S(1)} %copy-done.4, bf16[1,128,128]{2,1,0:T(8,128)(2,1)S(1)} %copy-done.7, ...), custom_call_target="tpu_custom_call" | custom-call | tf_op jit(solution)/shard_map/pallas_call | solution.py:348
  44.1 1.3 %collective-permute-start.1 = (bf16[4,256,128]{2,1,0:T(8,128)(2,1)S(1)}, bf16[4,256,128]{2,1,0:T(8,128)(2,1)S(1)}, u32[]{:S(2)}, u32[]{:S(2)}) collective-permute-start(bf16[4,256,128]{2,1,0:T(8,128)(2,1)S(1)} %get-tuple-element.36.own_ref), channel_id=1, source_target_pairs={{8,0},{9,1},{10,2},{11,3},{12,4},{13,5},{14,6},{15,7},{16,8},{17,9... | collective-permute-start | bytes 786440 | tf_op jit(solution)/shard_map/ppermute | solution.py:419
  45.4 0.0 copy-done.1
  45.4 0.4 shard_map.114
  45.8 1.2 %all-to-all-done.2.r_ref = bf16[8,32,128]{2,1,0:T(8,128)(2,1)S(1)} async-done(((bf16[8,32,128]{2,1,0:T(8,128)(2,1)}), bf16[8,32,128]{2,1,0:T(8,128)(2,1)S(1)}, u32[]{:S(2)}, u32[]{:S(2)}) %all-to-all-start.2) | async-done | bytes 65568 | tf_op jit(solution)/shard_map/all_to_all | solution.py:362
  47.0 0.0 copy-start.10
  47.0 0.7 copy-done.10
  47.7 1.2 shard_map.115
  48.9 8.7 %all_to_all.42.r_ref = bf16[8,64,128]{2,1,0:T(8,128)(2,1)S(1)} all-to-all(bf16[8,64,128]{2,1,0:T(8,128)(2,1)S(1)} %get-tuple-element.35), channel_id=1, replica_groups={{0,1,2,3,4,5,6,7},{8,9,10,11,12,13,14,15},{16,17,18,19,20,21,22,23},{24..., dimensions={0} | all-to-all | bytes 262144 | tf_op jit(solution)/shard_map/all_to_all | solution.py:362
  57.6 0.6 shard_map.119
  58.2 4.7 %all-to-all-start.4 = ((bf16[8,32,128]{2,1,0:T(8,128)(2,1)}), bf16[8,32,128]{2,1,0:T(8,128)(2,1)S(1)}, u32[]{:S(2)}, u32[]{:S(2)}) async-start(bf16[8,32,128]{2,1,0:T(8,128)(2,1)} %shard_map.119), calls=%async_computation.4 | async-start | bytes 131072 | tf_op jit(solution)/shard_map/all_to_all | solution.py:362
  62.9 0.4 shard_map.118.slope_ref
  63.3 6.8 %all-to-all-done.4.c_ref = bf16[8,32,128]{2,1,0:T(8,128)(2,1)S(1)} async-done(((bf16[8,32,128]{2,1,0:T(8,128)(2,1)}), bf16[8,32,128]{2,1,0:T(8,128)(2,1)S(1)}, u32[]{:S(2)}, u32[]{:S(2)}) %all-to-all-start.4) | async-done | bytes 65568 | tf_op jit(solution)/shard_map/all_to_all | solution.py:362
  70.1 0.0 collective-permute-done.1.back_ref
  70.1 0.9 shard_map.120
  71.1 9.6 %all_to_all.43.r_ref = bf16[8,32,128]{2,1,0:T(8,128)(2,1)S(1)} all-to-all(bf16[8,32,128]{2,1,0:T(8,128)(2,1)S(1)} %get-tuple-element.37), channel_id=1, replica_groups={{0,8,16,24,32,40,48,56},{1,9,17,25,33,41,49,57},{2,10,18,26,34,42,50,58..., dimensions={0} | all-to-all | bytes 131072 | tf_op jit(solution)/shard_map/all_to_all | solution.py:362
  80.7 17.1 %all_to_all.44.r_ref = bf16[8,32,128]{2,1,0:T(8,128)(2,1)S(1)} all-to-all(bf16[8,32,128]{2,1,0:T(8,128)(2,1)S(1)} %shard_map.121), channel_id=1, replica_groups=mesh['heads'=8,'ctx'=64] {'heads'}, dimensions={0} | all-to-all | bytes 131072 | tf_op jit(solution)/shard_map/all_to_all | solution.py:362
  97.7 0.9 shard_map.122
  98.7 8.3 %all-to-all-start.7 = ((bf16[8,352,128]{2,1,0:T(8,128)(2,1)}), bf16[8,352,128]{2,1,0:T(8,128)(2,1)S(1)}, u32[]{:S(2)}, u32[]{:S(2)}) async-start(bf16[8,352,128]{2,1,0:T(8,128)(2,1)} %shard_map.122), calls=%async_computation.7 | async-start | bytes 1441792 | tf_op jit(solution)/shard_map/all_to_all | solution.py:362
  107.0 0.9 shard_map.117
  107.9 10.6 %all-to-all-done.7.r_ref = bf16[8,352,128]{2,1,0:T(8,128)(2,1)S(1)} async-done(((bf16[8,352,128]{2,1,0:T(8,128)(2,1)}), bf16[8,352,128]{2,1,0:T(8,128)(2,1)S(1)}, u32[]{:S(2)}, u32[]{:S(2)}) %all-to-all-start.7) | async-done | bytes 720928 | tf_op jit(solution)/shard_map/all_to_all | solution.py:362
  118.5 1.0 shard_map.123
  (2 shorter events, 0.0 us)
Async XLA Ops:
  0.6 0.8 copy-start
  1.5 0.8 copy-start.3
  2.2 0.8 copy-start.6
  23.1 19.1 %collective-permute-start = (bf16[4,256,128]{2,1,0:T(8,128)(2,1)S(1)}, bf16[4,256,128]{2,1,0:T(8,128)(2,1)S(1)}, u32[]{:S(2)}, u32[]{:S(2)}) collective-permute-start(bf16[4,256,128]{2,1,0:T(8,128)(2,1)S(1)} %get-tuple-element.31), channel_id=1, source_target_pairs={{0,8},{1,9},{2,10},{3,11},{4,12},{5,13},{6,14},{7,15},{8,16},{9,17... | collective-permute-start | bytes 786440 | tf_op jit(solution)/shard_map/ppermute | solution.py:390
  35.6 6.5 %copy-start.4 = (bf16[1,128,128]{2,1,0:T(8,128)(2,1)S(1)}, bf16[1,128,128]{2,1,0:T(8,128)(2,1)}, u32[]{:S(2)}) copy-start(bf16[1,128,128]{2,1,0:T(8,128)(2,1)} %k_ref.7) | copy-start | bytes 98308
  35.6 6.5 %copy-start.5 = (bf16[1,128,512]{2,1,0:T(8,128)(2,1)S(1)}, bf16[1,128,512]{2,1,0:T(8,128)(2,1)}, u32[]{:S(2)}) copy-start(bf16[1,128,512]{2,1,0:T(8,128)(2,1)} %g_ref.3) | copy-start | bytes 393220
  35.6 6.5 %copy-start.7 = (bf16[1,128,128]{2,1,0:T(8,128)(2,1)S(1)}, bf16[1,128,128]{2,1,0:T(8,128)(2,1)}, u32[]{:S(2)}) copy-start(bf16[1,128,128]{2,1,0:T(8,128)(2,1)} %v_ref.5) | copy-start | bytes 98308
  35.6 6.6 %copy-start.8 = (f32[1,512]{1,0:T(1,128)S(1)}, f32[1,512]{1,0:T(1,128)}, u32[]{:S(2)}) copy-start(f32[1,512]{1,0:T(1,128)} %gs_ref.1) | copy-start | bytes 6148
  35.6 6.6 %copy-start.9 = (s32[1,64,4]{1,2,0:T(4,128)S(1)}, s32[1,64,4]{1,2,0:T(4,128)}, u32[]{:S(2)}) copy-start(s32[1,64,4]{1,2,0:T(4,128)} %param.14) | copy-start | bytes 3076
  36.3 5.9 %copy-start.2 = (bf16[1,128,512]{2,1,0:T(8,128)(2,1)S(1)}, bf16[1,128,512]{2,1,0:T(8,128)(2,1)}, u32[]{:S(2)}) copy-start(bf16[1,128,512]{2,1,0:T(8,128)(2,1)} %q_ref.5) | copy-start | bytes 393220
  36.3 10.7 %all-to-all-start.2 = ((bf16[8,32,128]{2,1,0:T(8,128)(2,1)}), bf16[8,32,128]{2,1,0:T(8,128)(2,1)S(1)}, u32[]{:S(2)}, u32[]{:S(2)}) async-start(bf16[8,32,128]{2,1,0:T(8,128)(2,1)} %shard_map.113), calls=%async_computation.2 | async-start | bytes 131072 | tf_op jit(solution)/shard_map/all_to_all | solution.py:362
  42.2 3.1 %copy-start.1 = (bf16[128,256]{1,0:T(8,128)(2,1)S(1)}, bf16[128,256]{1,0:T(8,128)(2,1)}, u32[]{:S(2)}) copy-start(bf16[128,256]{1,0:T(8,128)(2,1)} %w_ref.7) | copy-start | bytes 196612
  44.1 26.1 %collective-permute-start.1 = (bf16[4,256,128]{2,1,0:T(8,128)(2,1)S(1)}, bf16[4,256,128]{2,1,0:T(8,128)(2,1)S(1)}, u32[]{:S(2)}, u32[]{:S(2)}) collective-permute-start(bf16[4,256,128]{2,1,0:T(8,128)(2,1)S(1)} %get-tuple-element.36.own_ref), channel_id=1, source_target_pairs={{8,0},{9,1},{10,2},{11,3},{12,4},{13,5},{14,6},{15,7},{16,8},{17,9... | collective-permute-start | bytes 786440 | tf_op jit(solution)/shard_map/ppermute | solution.py:419
  47.0 0.7 copy-start.10
  58.2 11.9 %all-to-all-start.4 = ((bf16[8,32,128]{2,1,0:T(8,128)(2,1)}), bf16[8,32,128]{2,1,0:T(8,128)(2,1)S(1)}, u32[]{:S(2)}, u32[]{:S(2)}) async-start(bf16[8,32,128]{2,1,0:T(8,128)(2,1)} %shard_map.119), calls=%async_computation.4 | async-start | bytes 131072 | tf_op jit(solution)/shard_map/all_to_all | solution.py:362
  98.7 19.8 %all-to-all-start.7 = ((bf16[8,352,128]{2,1,0:T(8,128)(2,1)}), bf16[8,352,128]{2,1,0:T(8,128)(2,1)S(1)}, u32[]{:S(2)}, u32[]{:S(2)}) async-start(bf16[8,352,128]{2,1,0:T(8,128)(2,1)} %shard_map.122), calls=%async_computation.7 | async-start | bytes 1441792 | tf_op jit(solution)/shard_map/all_to_all | solution.py:362

commit v6 on v5

--- a/solution.py
+++ b/solution.py
@@ -135,7 +135,7 @@
 
 
 def local_kernel(
-    q_ref, k_ref, w_ref, feat_ref, kf_ref, lw_ref,
+    q_ref, k_ref, w_ref, gl_ref, feat_ref, kf_ref, lw_ref, gain_ref,
 ):
     keys = k_ref[0]
     w = w_ref[...]
@@ -148,10 +148,11 @@
     feat_ref[...] = feat
     kf_ref[...] = key_feat
     lw_ref[...] = jnp.where(causal, scores, 0.0).astype(BF16)
+    gain_ref[...] = gl_ref[...]
 
 
 def linear_kernel(
-    q_ref, k_ref, v_ref, g_ref, gl_ref, r_ref, feat_ref, kf_ref, lw_ref,
+    q_ref, k_ref, v_ref, g_ref, r_ref, feat_ref, kf_ref, lw_ref, gl_ref,
     send_ref, kloc_ref, rg_ref, lg_ref,
 ):
     keys = k_ref[0]
@@ -268,7 +269,8 @@
 
 
 def weight_part_kernel(
-    row_ref, slope_ref, r_ref, c_ref, own_ref, back_ref, send_ref, o_ref, far_ref
+    row_ref, slope_ref, r_ref, c_ref, own_ref, back_ref,
+    send_ref, o_ref, keep_ref, give_ref,
 ):
     line, spot = spots()[:2]
     step, length = slope_ref.shape[1:]
@@ -288,16 +290,20 @@
     weight = weight.astype(BF16)
     for place in range(SIDE):
         send_ref[place] = weight
-    far_ref[...] = jnp.zeros(far_ref.shape, BF16)
-    for reach in range(1, own_ref.shape[0] + 1):
-
-        @pl.when(spot >= reach)
-        def _():
-            far_ref[spot - reach] = own_ref[reach - 1]
-
-        @pl.when(spot < reach)
-        def _():
-            far_ref[spot - reach + SIDE] = back_ref[reach - 1]
+    keep_ref[...] = jnp.zeros(keep_ref.shape, BF16)
+    give_ref[...] = jnp.zeros(give_ref.shape, BF16)
+    for parity, own, other in ((0, keep_ref, give_ref), (1, give_ref, keep_ref)):
+        for reach in range(1, own_ref.shape[0] + 1):
+
+            @pl.when((spot % 2 == parity) & (spot >= reach))
+            def _():
+                own[spot - reach] = own_ref[reach - 1, :length]
+                other[spot - reach] = own_ref[reach - 1, length:]
+
+            @pl.when((spot % 2 == parity) & (spot < reach))
+            def _():
+                own[spot - reach + SIDE] = back_ref[reach - 1, :length]
+                other[spot - reach + SIDE] = back_ref[reach - 1, length:]
 
 
 def column_sum_kernel(r_ref, o_ref):
@@ -307,14 +313,16 @@
 
 
 def make_last_kernel(scale):
-    def last_kernel(r_ref, carried_ref, far_ref, o_ref):
+    def last_kernel(r_ref, carried_ref, keep_ref, got_ref, o_ref):
         step = r_ref.shape[1]
         high, low = split(jnp.sum(r_ref[...].astype(F32), axis=0) * scale)
         o_ref[:, :step] = carried_ref[...]
         for spot in range(SIDE):
             o_ref[spot, step : 2 * step] = high
             o_ref[spot, 2 * step : 3 * step] = low
-        o_ref[:, 3 * step :] = far_ref[...]
+        for spot in range(SIDE):
+            far = keep_ref[spot].astype(F32) + got_ref[spot].astype(F32)
+            o_ref[spot, 3 * step :] = far.astype(BF16)
 
     return last_kernel
 
@@ -326,18 +334,20 @@
     values = v_ref[0]
     w = w_ref[...]
     step = w.shape[1] // SIDE
-    length = keys.shape[0]
     carried = whole(r_ref[:, :step])
     weight = whole(r_ref[:, step : 2 * step]).astype(F32)
     weight = weight + whole(r_ref[:, 2 * step : 3 * step]).astype(F32)
     wo_ref[...] = weight.T
-    back = jnp.sum(r_ref[:, 3 * step :].astype(F32), axis=0)
+    key_back, value_back = (
+        sum(r_ref[spot, 3 * step :].astype(F32) for spot in range(parity, SIDE, 2))
+        for parity in range(2)
+    )
     feat, slope = features(nn(keys, w))
     feat = feat.astype(BF16)
     feat_grad = nt(values, carried) + kloc_ref[...]
     raw_grad = (feat_grad * slope).astype(BF16)
-    ko_ref[0] = (dk_ref[...] + back[:length] + nt(raw_grad, w)).astype(BF16)
-    vo_ref[0] = (dv_ref[...] + back[length:] + nn(feat, carried)).astype(BF16)
+    ko_ref[0] = (dk_ref[...] + key_back + nt(raw_grad, w)).astype(BF16)
+    vo_ref[0] = (dv_ref[...] + value_back + nn(feat, carried)).astype(BF16)
 
 
 def call(kernel, *outs, grant=8, space=pltpu.VMEM, scratch=()):
@@ -376,7 +386,7 @@
     down = [(i, i + SIDE) for i in range(shards - SIDE)]
     rows = (queries.shape[2] // size * length, size)
     square = (length, size)
-    pair = (SIDE, 2 * length, size)
+    single = (SIDE, length, size)
     sent = call(
         send_state_kernel,
         ((SIDE, step + 2 * length, size), BF16),
@@ -395,7 +405,8 @@
         ((rows[0], features_n), F32),
         ((length, features_n), F32),
         ((rows[0], length), BF16),
-    )(queries, keys, w_feat)
+        (gain_lin.shape, F32),
+    )(queries, keys, w_feat, gain_lin)
     query_sparse, back, key_near, value_near = call(
         sparse_kernel,
         (rows, F32),
@@ -414,7 +425,7 @@
         ((length, features_n), F32),
         ((rows[0], features_n), BF16),
         (rows, BF16),
-    )(queries, keys, values, out_grad, gain_lin, got, *local)
+    )(queries, keys, values, out_grad, got, *local)
     cots = swap(sent, "ctx", in_row)
     returned = lax.ppermute(back, "ctx", [(b, a) for a, b in down])
     query_out, value_near = call(finish_kernel, (queries.shape, BF16), (square, F32))(
@@ -422,14 +433,15 @@
     )
     sent = call(total_kernel, (piece, BF16))(cots)
     got = swap(sent, "ctx", in_column)
-    sent, carried, far = call(
-        weight_part_kernel, (piece, BF16), (piece, BF16), (pair, BF16)
+    sent, carried, keep, give = call(
+        weight_part_kernel, (piece, BF16), (piece, BF16), (single, BF16), (single, BF16)
     )(row, slopes, cots, got, back, returned)
+    taken = lax.ppermute(give, "ctx", [(i, i ^ 1) for i in range(shards)])
     got = swap(sent, "ctx", in_column)
     sent = call(column_sum_kernel, ((groups, step, size), BF16))(got)
     got = swap(sent, "heads")
-    sent = call(make_last_kernel(scale), ((SIDE, 3 * step + 2 * length, size), BF16))(
-        got, carried, far
+    sent = call(make_last_kernel(scale), ((SIDE, 3 * step + length, size), BF16))(
+        got, carried, keep, taken
     )
     got = swap(sent, "ctx", in_row)
     key_out, value_out, weight = call(

time: 120 us -> 119 us (level)
  waiting for transfers between devices: 18.6 us -> 15.8 us
  starting transfers between devices: 21.5 us -> 23.4 us
    ppermute x0 -> x1, starting transfers between devices: none -> 4.24 us  [per_device(): taken = lax.ppermute(give, 'ctx', [(i, i ^ 1) for i in range(shards)])]
    all_to_all x3, waiting for transfers between devices: 18.6 us -> 15.8 us  [swap(): lax.all_to_all(value, axis, 0, 0, axis_index_groups=groups, tiled=False)]
    all_to_all x3, starting transfers between devices: 18.9 us -> 16.6 us  [swap(): lax.all_to_all(value, axis, 0, 0, axis_index_groups=groups, tiled=False)]
  transfers between devices with their start and end apart: 5 -> 6, of which waited for: 3 -> 3; matrix products, arithmetic and copies ran while one was open for 0% -> 0% of each run, Pallas kernels for 5% -> 5%
where the time goes in v6:
time: 119 us; the launch traced here: 118 us
  blocking collectives  66.3 us (56%)
  starting transfers between devices  23.4 us (20%)
  waiting for transfers between devices  15.8 us (13%)
  Pallas kernels  9.43 us (8%)
  local copies, waits for them, and re-layouts  2.39 us (2%)
    all_to_all x5, blocking collectives, swap(): lax.all_to_all(value, axis, 0, 0, axis_index_groups=groups, tiled=False)  66.3 us
    all_to_all x3, starting transfers between devices, swap(): lax.all_to_all(value, axis, 0, 0, axis_index_groups=groups, tiled=False)  16.6 us
    all_to_all x3, waiting for transfers between devices, swap(): lax.all_to_all(value, axis, 0, 0, axis_index_groups=groups, tiled=False)  15.8 us
    pallas_call x13, Pallas kernels, run(): pl.pallas_call(kernel, out_shape=shapes if len(shapes) > 1 else shapes[0]...  9.43 us
    ppermute x1, starting transfers between devices, per_device(): taken = lax.ppermute(give, 'ctx', [(i, i ^ 1) for i in range(shards)])  4.24 us
    unnamed x22, local copies, waits for them, and re-layouts  2.39 us
  transfers between devices with their start and end apart: 6, of which 3 were waited for; matrix products, arithmetic and copies ran while one was open for 0% of the time, Pallas kernels for 5%

profile of v6, /device:TPU:1, one launch (start us, length us, event | category | flops | bytes accessed | tf_op | source)
XLA Modules:
  0.0 118.1 jit_solution(6614522851956429281)
XLA Ops:
  0.6 0.0 copy-start
  0.6 0.8 copy-done
  1.5 0.0 copy-start.3
  1.5 0.8 copy-done.3
  2.2 0.0 copy-start.6
  2.2 0.8 copy-done.6
  3.0 0.5 shard_map.111
  3.5 19.5 %all_to_all.40.r_ref.row_ref = bf16[8,288,128]{2,1,0:T(8,128)(2,1)S(1)} all-to-all(bf16[8,288,128]{2,1,0:T(8,128)(2,1)S(1)} %shard_map.111), channel_id=1, replica_groups={{0,1,2,3,4,5,6,7},{8,9,10,11,12,13,14,15},{16,17,18,19,20,21,22,23},{24..., dimensions={0} | all-to-all | bytes 1179648 | tf_op jit(solution)/shard_map/all_to_all | solution.py:372
  23.1 1.3 %collective-permute-start = (bf16[4,256,128]{2,1,0:T(8,128)(2,1)S(1)}, bf16[4,256,128]{2,1,0:T(8,128)(2,1)S(1)}, u32[]{:S(2)}, u32[]{:S(2)}) collective-permute-start(bf16[4,256,128]{2,1,0:T(8,128)(2,1)S(1)} %get-tuple-element.34), channel_id=1, source_target_pairs={{0,8},{1,9},{2,10},{3,11},{4,12},{5,13},{6,14},{7,15},{8,16},{9,17... | collective-permute-start | bytes 786440 | tf_op jit(solution)/shard_map/ppermute | solution.py:400
  24.4 11.2 %all_to_all.41.c_ref = bf16[8,32,128]{2,1,0:T(8,128)(2,1)S(1)} all-to-all(bf16[8,32,128]{2,1,0:T(8,128)(2,1)S(1)} %get-tuple-element.27), channel_id=1, replica_groups={{0,8,16,24,32,40,48,56},{1,9,17,25,33,41,49,57},{2,10,18,26,34,42,50,58..., dimensions={0} | all-to-all | bytes 131072 | tf_op jit(solution)/shard_map/all_to_all | solution.py:372
  35.6 0.0 copy-start.4
  35.6 0.0 copy-start.5
  35.6 0.0 copy-start.7
  35.6 0.0 copy-start.8
  35.6 0.0 copy-start.9
  35.6 0.7 shard_map.113
  36.3 0.0 copy-start.2
  36.3 5.8 %all-to-all-start.2 = ((bf16[8,32,128]{2,1,0:T(8,128)(2,1)}), bf16[8,32,128]{2,1,0:T(8,128)(2,1)S(1)}, u32[]{:S(2)}, u32[]{:S(2)}) async-start(bf16[8,32,128]{2,1,0:T(8,128)(2,1)} %shard_map.113), calls=%async_computation.2 | async-start | bytes 131072 | tf_op jit(solution)/shard_map/all_to_all | solution.py:372
  42.2 0.0 collective-permute-done.prev_ref
  42.2 0.0 copy-done.4
  42.2 0.0 copy-done.5
  42.2 0.0 copy-done.7
  42.2 0.0 copy-done.8
  42.2 0.0 copy-done.9
  42.2 0.0 copy-done.2
  42.2 0.0 copy-start.1
  42.2 0.0 copy-start.10
  42.2 1.8 %shard_map.116 = (f32[512,128]{1,0:T(8,128)S(1)}, bf16[4,256,128]{2,1,0:T(8,128)(2,1)S(1)}, f32[128,128]{1,0:T(8,128)S(1)}, f32[128,128]{1,0:T(8,128)S(1)}) custom-call(bf16[1,128,512]{2,1,0:T(8,128)(2,1)S(1)} %copy-done.2, bf16[1,128,128]{2,1,0:T(8,128)(2,1)S(1)} %copy-done.4, bf16[1,128,128]{2,1,0:T(8,128)(2,1)S(1)} %copy-done.7, ...), custom_call_target="tpu_custom_call" | custom-call | tf_op jit(solution)/shard_map/pallas_call | solution.py:358
  44.1 1.3 %collective-permute-start.1 = (bf16[4,256,128]{2,1,0:T(8,128)(2,1)S(1)}, bf16[4,256,128]{2,1,0:T(8,128)(2,1)S(1)}, u32[]{:S(2)}, u32[]{:S(2)}) collective-permute-start(bf16[4,256,128]{2,1,0:T(8,128)(2,1)S(1)} %get-tuple-element.39.own_ref), channel_id=1, source_target_pairs={{8,0},{9,1},{10,2},{11,3},{12,4},{13,5},{14,6},{15,7},{16,8},{17,9... | collective-permute-start | bytes 786440 | tf_op jit(solution)/shard_map/ppermute | solution.py:430
  45.4 0.0 copy-done.1
  45.4 0.0 copy-done.10
  45.4 0.4 shard_map.114
  45.8 1.2 %all-to-all-done.2.r_ref = bf16[8,32,128]{2,1,0:T(8,128)(2,1)S(1)} async-done(((bf16[8,32,128]{2,1,0:T(8,128)(2,1)}), bf16[8,32,128]{2,1,0:T(8,128)(2,1)S(1)}, u32[]{:S(2)}, u32[]{:S(2)}) %all-to-all-start.2) | async-done | bytes 65568 | tf_op jit(solution)/shard_map/all_to_all | solution.py:372
  47.0 1.2 shard_map.115
  48.2 8.7 %all_to_all.42.r_ref = bf16[8,64,128]{2,1,0:T(8,128)(2,1)S(1)} all-to-all(bf16[8,64,128]{2,1,0:T(8,128)(2,1)S(1)} %get-tuple-element.38), channel_id=1, replica_groups={{0,1,2,3,4,5,6,7},{8,9,10,11,12,13,14,15},{16,17,18,19,20,21,22,23},{24..., dimensions={0} | all-to-all | bytes 262144 | tf_op jit(solution)/shard_map/all_to_all | solution.py:372
  56.9 0.6 shard_map.119
  57.5 4.7 %all-to-all-start.4 = ((bf16[8,32,128]{2,1,0:T(8,128)(2,1)}), bf16[8,32,128]{2,1,0:T(8,128)(2,1)S(1)}, u32[]{:S(2)}, u32[]{:S(2)}) async-start(bf16[8,32,128]{2,1,0:T(8,128)(2,1)} %shard_map.119), calls=%async_computation.4 | async-start | bytes 131072 | tf_op jit(solution)/shard_map/all_to_all | solution.py:372
  62.2 0.4 shard_map.118.slope_ref
  62.6 6.8 %all-to-all-done.4.c_ref = bf16[8,32,128]{2,1,0:T(8,128)(2,1)S(1)} async-done(((bf16[8,32,128]{2,1,0:T(8,128)(2,1)}), bf16[8,32,128]{2,1,0:T(8,128)(2,1)S(1)}, u32[]{:S(2)}, u32[]{:S(2)}) %all-to-all-start.4) | async-done | bytes 65568 | tf_op jit(solution)/shard_map/all_to_all | solution.py:372
  69.5 0.0 collective-permute-done.1.back_ref
  69.5 0.9 shard_map.120
  70.4 4.2 %collective-permute-start.2 = (bf16[8,128,128]{2,1,0:T(8,128)(2,1)S(1)}, bf16[8,128,128]{2,1,0:T(8,128)(2,1)S(1)}, u32[]{:S(2)}, u32[]{:S(2)}) collective-permute-start(bf16[8,128,128]{2,1,0:T(8,128)(2,1)S(1)} %get-tuple-element.43), channel_id=1, source_target_pairs={{0,1},{1,0},{2,3},{3,2},{4,5},{5,4},{6,7},{7,6},{8,9},{9,8},{10,11... | collective-permute-start | bytes 786440 | tf_op jit(solution)/shard_map/ppermute | solution.py:439
  74.7 9.7 %all_to_all.43.r_ref = bf16[8,32,128]{2,1,0:T(8,128)(2,1)S(1)} all-to-all(bf16[8,32,128]{2,1,0:T(8,128)(2,1)S(1)} %get-tuple-element.40), channel_id=1, replica_groups={{0,8,16,24,32,40,48,56},{1,9,17,25,33,41,49,57},{2,10,18,26,34,42,50,58..., dimensions={0} | all-to-all | bytes 131072 | tf_op jit(solution)/shard_map/all_to_all | solution.py:372
  84.4 17.1 %all_to_all.44.r_ref = bf16[8,32,128]{2,1,0:T(8,128)(2,1)S(1)} all-to-all(bf16[8,32,128]{2,1,0:T(8,128)(2,1)S(1)} %shard_map.121), channel_id=1, replica_groups=mesh['heads'=8,'ctx'=64] {'heads'}, dimensions={0} | all-to-all | bytes 131072 | tf_op jit(solution)/shard_map/all_to_all | solution.py:372
  101.5 0.0 collective-permute-done.2.got_ref
  101.5 0.9 shard_map.122
  102.4 6.1 %all-to-all-start.7 = ((bf16[8,224,128]{2,1,0:T(8,128)(2,1)}), bf16[8,224,128]{2,1,0:T(8,128)(2,1)S(1)}, u32[]{:S(2)}, u32[]{:S(2)}) async-start(bf16[8,224,128]{2,1,0:T(8,128)(2,1)} %shard_map.122), calls=%async_computation.7 | async-start | bytes 917504 | tf_op jit(solution)/shard_map/all_to_all | solution.py:372
  108.4 0.9 shard_map.117
  109.3 7.7 %all-to-all-done.7.r_ref = bf16[8,224,128]{2,1,0:T(8,128)(2,1)S(1)} async-done(((bf16[8,224,128]{2,1,0:T(8,128)(2,1)}), bf16[8,224,128]{2,1,0:T(8,128)(2,1)S(1)}, u32[]{:S(2)}, u32[]{:S(2)}) %all-to-all-start.7) | async-done | bytes 458784 | tf_op jit(solution)/shard_map/all_to_all | solution.py:372
  117.1 1.0 shard_map.123
  (2 shorter events, 0.0 us)
Async XLA Ops:
  0.6 0.8 copy-start
  1.5 0.8 copy-start.3
  2.2 0.8 copy-start.6
  23.1 19.1 %collective-permute-start = (bf16[4,256,128]{2,1,0:T(8,128)(2,1)S(1)}, bf16[4,256,128]{2,1,0:T(8,128)(2,1)S(1)}, u32[]{:S(2)}, u32[]{:S(2)}) collective-permute-start(bf16[4,256,128]{2,1,0:T(8,128)(2,1)S(1)} %get-tuple-element.34), channel_id=1, source_target_pairs={{0,8},{1,9},{2,10},{3,11},{4,12},{5,13},{6,14},{7,15},{8,16},{9,17... | collective-permute-start | bytes 786440 | tf_op jit(solution)/shard_map/ppermute | solution.py:400
  35.6 6.5 %copy-start.4 = (bf16[1,128,128]{2,1,0:T(8,128)(2,1)S(1)}, bf16[1,128,128]{2,1,0:T(8,128)(2,1)}, u32[]{:S(2)}) copy-start(bf16[1,128,128]{2,1,0:T(8,128)(2,1)} %k_ref.7) | copy-start | bytes 98308
  35.6 6.5 %copy-start.5 = (bf16[1,128,512]{2,1,0:T(8,128)(2,1)S(1)}, bf16[1,128,512]{2,1,0:T(8,128)(2,1)}, u32[]{:S(2)}) copy-start(bf16[1,128,512]{2,1,0:T(8,128)(2,1)} %g_ref.3) | copy-start | bytes 393220
  35.6 6.5 %copy-start.7 = (bf16[1,128,128]{2,1,0:T(8,128)(2,1)S(1)}, bf16[1,128,128]{2,1,0:T(8,128)(2,1)}, u32[]{:S(2)}) copy-start(bf16[1,128,128]{2,1,0:T(8,128)(2,1)} %v_ref.5) | copy-start | bytes 98308
  35.6 6.6 %copy-start.8 = (f32[1,512]{1,0:T(1,128)S(1)}, f32[1,512]{1,0:T(1,128)}, u32[]{:S(2)}) copy-start(f32[1,512]{1,0:T(1,128)} %gs_ref.1) | copy-start | bytes 6148
  35.6 6.6 %copy-start.9 = (s32[1,64,4]{1,2,0:T(4,128)S(1)}, s32[1,64,4]{1,2,0:T(4,128)}, u32[]{:S(2)}) copy-start(s32[1,64,4]{1,2,0:T(4,128)} %param.14) | copy-start | bytes 3076
  36.3 5.9 %copy-start.2 = (bf16[1,128,512]{2,1,0:T(8,128)(2,1)S(1)}, bf16[1,128,512]{2,1,0:T(8,128)(2,1)}, u32[]{:S(2)}) copy-start(bf16[1,128,512]{2,1,0:T(8,128)(2,1)} %q_ref.5) | copy-start | bytes 393220
  36.3 10.7 %all-to-all-start.2 = ((bf16[8,32,128]{2,1,0:T(8,128)(2,1)}), bf16[8,32,128]{2,1,0:T(8,128)(2,1)S(1)}, u32[]{:S(2)}, u32[]{:S(2)}) async-start(bf16[8,32,128]{2,1,0:T(8,128)(2,1)} %shard_map.113), calls=%async_computation.2 | async-start | bytes 131072 | tf_op jit(solution)/shard_map/all_to_all | solution.py:372
  42.2 3.2 %copy-start.1 = (bf16[128,256]{1,0:T(8,128)(2,1)S(1)}, bf16[128,256]{1,0:T(8,128)(2,1)}, u32[]{:S(2)}) copy-start(bf16[128,256]{1,0:T(8,128)(2,1)} %w_ref.7) | copy-start | bytes 196612
  42.2 3.2 %copy-start.10 = (f32[1,512]{1,0:T(1,128)S(1)}, f32[1,512]{1,0:T(1,128)}, u32[]{:S(2)}) copy-start(f32[1,512]{1,0:T(1,128)} %gl_ref.1) | copy-start | bytes 6148
  44.1 25.4 %collective-permute-start.1 = (bf16[4,256,128]{2,1,0:T(8,128)(2,1)S(1)}, bf16[4,256,128]{2,1,0:T(8,128)(2,1)S(1)}, u32[]{:S(2)}, u32[]{:S(2)}) collective-permute-start(bf16[4,256,128]{2,1,0:T(8,128)(2,1)S(1)} %get-tuple-element.39.own_ref), channel_id=1, source_target_pairs={{8,0},{9,1},{10,2},{11,3},{12,4},{13,5},{14,6},{15,7},{16,8},{17,9... | collective-permute-start | bytes 786440 | tf_op jit(solution)/shard_map/ppermute | solution.py:430
  57.5 11.9 %all-to-all-start.4 = ((bf16[8,32,128]{2,1,0:T(8,128)(2,1)}), bf16[8,32,128]{2,1,0:T(8,128)(2,1)S(1)}, u32[]{:S(2)}, u32[]{:S(2)}) async-start(bf16[8,32,128]{2,1,0:T(8,128)(2,1)} %shard_map.119), calls=%async_computation.4 | async-start | bytes 131072 | tf_op jit(solution)/shard_map/all_to_all | solution.py:372
  70.4 31.1 %collective-permute-start.2 = (bf16[8,128,128]{2,1,0:T(8,128)(2,1)S(1)}, bf16[8,128,128]{2,1,0:T(8,128)(2,1)S(1)}, u32[]{:S(2)}, u32[]{:S(2)}) collective-permute-start(bf16[8,128,128]{2,1,0:T(8,128)(2,1)S(1)} %get-tuple-element.43), channel_id=1, source_target_pairs={{0,1},{1,0},{2,3},{3,2},{4,5},{5,4},{6,7},{7,6},{8,9},{9,8},{10,11... | collective-permute-start | bytes 786440 | tf_op jit(solution)/shard_map/ppermute | solution.py:439
  102.4 14.7 %all-to-all-start.7 = ((bf16[8,224,128]{2,1,0:T(8,128)(2,1)}), bf16[8,224,128]{2,1,0:T(8,128)(2,1)S(1)}, u32[]{:S(2)}, u32[]{:S(2)}) async-start(bf16[8,224,128]{2,1,0:T(8,128)(2,1)} %shard_map.122), calls=%async_computation.7 | async-start | bytes 917504 | tf_op jit(solution)/shard_map/all_to_all | solution.py:372

commit v7 on v6

--- a/solution.py
+++ b/solution.py
@@ -87,19 +87,24 @@
     values = v_ref[0]
     feat = features(nn(keys, w_ref[...]))[0].astype(BF16)
     total = pieces(tn(feat, values).astype(BF16))
-    step, length = total.shape[1], keys.shape[0]
+    step = total.shape[1]
     o_ref[:, :step] = total
     for spot in range(SIDE):
-        o_ref[spot, step : step + length] = keys
-        o_ref[spot, step + length :] = values
-
-
-def row_total_kernel(r_ref, o_ref, kv_ref):
+        o_ref[spot, step:] = values if spot % 2 else keys
+
+
+def row_total_kernel(r_ref, o_ref, half_ref, moved_ref):
     step = o_ref.shape[1]
     total = jnp.sum(r_ref[:, :step].astype(F32), axis=0).astype(BF16)
     for place in range(SIDE):
         o_ref[place] = total
-    kv_ref[...] = r_ref[SIDE // 2 :, step:]
+    half_ref[...] = r_ref[:, step:]
+    moved_ref[...] = r_ref[SIDE // 2 :, step:]
+
+
+def pack_kernel(a_ref, b_ref, o_ref):
+    o_ref[:SIDE] = a_ref[...]
+    o_ref[SIDE:] = b_ref[...]
 
 
 def prefix_kernel(r_ref, c_ref, o_ref):
@@ -135,7 +140,8 @@
 
 
 def local_kernel(
-    q_ref, k_ref, w_ref, gl_ref, feat_ref, kf_ref, lw_ref, gain_ref,
+    q_ref, k_ref, w_ref, gl_ref, gs_ref, kb_ref,
+    feat_ref, kf_ref, lw_ref, gain_ref, sparse_gain_ref, table_ref,
 ):
     keys = k_ref[0]
     w = w_ref[...]
@@ -149,6 +155,8 @@
     kf_ref[...] = key_feat
     lw_ref[...] = jnp.where(causal, scores, 0.0).astype(BF16)
     gain_ref[...] = gl_ref[...]
+    sparse_gain_ref[...] = gs_ref[...]
+    table_ref[...] = kb_ref[...]
 
 
 def linear_kernel(
@@ -184,7 +192,7 @@
 
 
 def sparse_kernel(
-    q_ref, k_ref, v_ref, g_ref, gs_ref, kb_ref, row_ref, prev_ref,
+    q_ref, k_ref, v_ref, g_ref, gs_ref, kb_ref, rk_ref, rv_ref, pf_ref, ps_ref,
     qs_ref, back_ref, dk_ref, dv_ref,
 ):
     spot, shard = spots()[1:]
@@ -199,17 +207,27 @@
     table = kb_ref[0]
     column = lax.broadcasted_iota(jnp.int32, table.shape, 1)
     listed = jnp.max(jnp.where(column == shard, table, -1), axis=1, keepdims=True)
-    far = []
+    even = flag(spot % 2 == 0)
+    key_far = []
+    value_far = []
     live = []
     for reach in range(1, reaches + 1):
-        own = row_ref[jnp.maximum(spot - reach, 0), -2 * length :].astype(F32)
-        other = prev_ref[jnp.clip(spot - reach + SIDE // 2, 0, SIDE // 2 - 1)].astype(F32)
+        near = jnp.maximum(spot - reach, 0)
+        other = jnp.clip(spot - reach + SIDE // 2, 0, SIDE // 2 - 1)
+        first = pf_ref[other].astype(F32)
+        second = ps_ref[SIDE + other].astype(F32)
         inside = flag(spot >= reach)
-        far.append((inside * own + (1.0 - inside) * other).astype(BF16))
+        for ref, here, there, out in (
+            (rk_ref, first, second, key_far),
+            (rv_ref, second, first, value_far),
+        ):
+            outside = even * here + (1.0 - even) * there
+            own = ref[near].astype(F32)
+            out.append((inside * own + (1.0 - inside) * outside).astype(BF16))
         here = jnp.where(listed[reach - 1 : reach] >= 0, 1.0, 0.0)
         live.append(jnp.broadcast_to(here, (1, length)))
-    key_far = jnp.concatenate([item[:length] for item in far], axis=0)
-    value_far = jnp.concatenate([item[length:] for item in far], axis=0)
+    key_far = jnp.concatenate(key_far, axis=0)
+    value_far = jnp.concatenate(value_far, axis=0)
     live = jnp.concatenate(live, axis=1)
     near_logits = jnp.where(causal, scaling * nt(queries, keys), -jnp.inf)
     far_logits = jnp.where(live > 0.5, scaling * nt(queries, key_far), -jnp.inf)
@@ -258,18 +276,29 @@
         o_ref[place] = total
 
 
-def slope_kernel(row_ref, w_ref, slope_ref):
+def slope_kernel(half_ref, other_ref, w_ref, slope_ref, rk_ref, rv_ref):
     spot = spots()[1]
     w = w_ref[...]
-    step, length = slope_ref.shape[1:]
+    step, _ = slope_ref.shape[1:]
+
+    @pl.when(spot % 2 == 0)
+    def _():
+        rk_ref[...] = half_ref[...]
+        rv_ref[...] = other_ref[:SIDE]
+
+    @pl.when(spot % 2 == 1)
+    def _():
+        rk_ref[...] = other_ref[:SIDE]
+        rv_ref[...] = half_ref[...]
+
     row, col = iotas((step, w.shape[1]))
     own = nt(ones_where(col == row + step * spot), w).astype(BF16)
     for source in range(SIDE):
-        slope_ref[source] = features(nt(own, row_ref[source, step : step + length]))[1]
+        slope_ref[source] = features(nt(own, rk_ref[source]))[1]
 
 
 def weight_part_kernel(
-    row_ref, slope_ref, r_ref, c_ref, own_ref, back_ref,
+    rk_ref, rv_ref, slope_ref, r_ref, c_ref, own_ref, back_ref,
     send_ref, o_ref, keep_ref, give_ref,
 ):
     line, spot = spots()[:2]
@@ -281,8 +310,8 @@
     for source in range(SIDE - 1, -1, -1):
         high, low = split(total)
         o_ref[source] = high
-        keys = row_ref[source, step : step + length]
-        values = row_ref[source, step + length :]
+        keys = rk_ref[source]
+        values = rv_ref[source]
         slope = slope_ref[source]
         grad_high, grad_low = split((nt(high, values) + nt(low, values)) * slope)
         weight = weight + nn(grad_high, keys) + nn(grad_low, keys)
@@ -381,7 +410,6 @@
     step = features_n // SIDE
     in_row = [[line * SIDE + spot for spot in range(SIDE)] for line in range(shards // SIDE)]
     in_column = [[line * SIDE + spot for line in range(shards // SIDE)] for spot in range(SIDE)]
-    half = (SIDE // 2, 2 * length, size)
     piece = (SIDE, step, size)
     down = [(i, i + SIDE) for i in range(shards - SIDE)]
     rows = (queries.shape[2] // size * length, size)
@@ -389,24 +417,41 @@
     single = (SIDE, length, size)
     sent = call(
         send_state_kernel,
-        ((SIDE, step + 2 * length, size), BF16),
+        ((SIDE, step + length, size), BF16),
         space=pltpu.HBM,
         scratch=[pltpu.VMEM(item.shape, BF16) for item in (keys, values, w_feat)]
         + [pltpu.SemaphoreType.DMA((3,))],
     )(keys, values, w_feat)
     row = swap(sent, "ctx", in_row)
-    sent, moved = call(row_total_kernel, (piece, BF16), (half, BF16))(row)
+    sent, own, moved = call(
+        row_total_kernel,
+        (piece, BF16),
+        ((SIDE, length, size), BF16),
+        ((SIDE // 2, length, size), BF16),
+    )(row)
     got = swap(sent, "ctx", in_column)
     previous = lax.ppermute(moved, "ctx", down)
+    twins = [(i, i ^ 1) for i in range(shards)]
+    packed = call(pack_kernel, ((3 * SIDE // 2, length, size), BF16))(own, previous)
+    other = lax.ppermute(packed, "ctx", twins)
     sent = call(prefix_kernel, (piece, BF16))(row, got)
     got = swap(sent, "ctx", in_row)
-    local = call(
+    table = jnp.swapaxes(key_blocks, 1, 2)
+    *local, sparse_gain, table = call(
         local_kernel,
         ((rows[0], features_n), F32),
         ((length, features_n), F32),
         ((rows[0], length), BF16),
         (gain_lin.shape, F32),
-    )(queries, keys, w_feat, gain_lin)
+        (gain_sparse.shape, F32),
+        (table.shape, table.dtype),
+    )(queries, keys, w_feat, gain_lin, gain_sparse, table)
+    slopes, row_keys, row_values = call(
+        slope_kernel,
+        ((SIDE, step, length), F32),
+        ((SIDE, length, size), BF16),
+        ((SIDE, length, size), BF16),
+    )(own, other, w_feat)
     query_sparse, back, key_near, value_near = call(
         sparse_kernel,
         (rows, F32),
@@ -415,10 +460,9 @@
         (square, F32),
         grant=12,
     )(
-        queries, keys, values, out_grad, gain_sparse, jnp.swapaxes(key_blocks, 1, 2),
-        row, previous,
-    )
-    slopes = call(slope_kernel, ((SIDE, step, length), F32))(row, w_feat)
+        queries, keys, values, out_grad, sparse_gain, table,
+        row_keys, row_values, previous, other,
+    )
     sent, key_local, raw_grad, lin_grad = call(
         linear_kernel,
         ((SIDE, 2 * step, size), BF16),
@@ -435,7 +479,7 @@
     got = swap(sent, "ctx", in_column)
     sent, carried, keep, give = call(
         weight_part_kernel, (piece, BF16), (piece, BF16), (single, BF16), (single, BF16)
-    )(row, slopes, cots, got, back, returned)
+    )(row_keys, row_values, slopes, cots, got, back, returned)
     taken = lax.ppermute(give, "ctx", [(i, i ^ 1) for i in range(shards)])
     got = swap(sent, "ctx", in_column)
     sent = call(column_sum_kernel, ((groups, step, size), BF16))(got)

time: 119 us -> 124 us (1.042)
  blocking collectives: 66.3 us -> 79 us
  waiting for transfers between devices: 15.8 us -> 10.4 us
  starting transfers between devices: 23.4 us -> 21.1 us
    all_to_all x5 -> x6, blocking collectives: 66.3 us -> 79 us  [swap(): lax.all_to_all(value, axis, 0, 0, axis_index_groups=groups, tiled=False)]
    all_to_all x3 -> x2, waiting for transfers between devices: 15.8 us -> 8.03 us  [swap(): lax.all_to_all(value, axis, 0, 0, axis_index_groups=groups, tiled=False)]
    all_to_all x3 -> x2, starting transfers between devices: 16.6 us -> 11 us  [swap(): lax.all_to_all(value, axis, 0, 0, axis_index_groups=groups, tiled=False)]
    ppermute x0 -> x1, starting transfers between devices: none -> 3.23 us  [per_device(): other = lax.ppermute(packed, 'ctx', twins)]
    ppermute x1, waiting for transfers between devices: 0.01 us -> 2.36 us  [per_device(): previous = lax.ppermute(moved, 'ctx', down)]
    pallas_call x13 -> x14, Pallas kernels: 9.43 us -> 8.93 us  [run(): pl.pallas_call(kernel, out_shape=shapes if len(shapes) > 1 else shapes[0]...]
  transfers between devices with their start and end apart: 6 -> 6, of which waited for: 3 -> 3; matrix products, arithmetic and copies ran while one was open for 0% -> 0% of each run, Pallas kernels for 5% -> 4%
where the time goes in v7:
time: 124 us; the launch traced here: 123 us
  blocking collectives  79 us (64%)
  starting transfers between devices  21.1 us (17%)
  waiting for transfers between devices  10.4 us (8%)
  Pallas kernels  8.93 us (7%)
  local copies, waits for them, and re-layouts  2.83 us (2%)
    all_to_all x6, blocking collectives, swap(): lax.all_to_all(value, axis, 0, 0, axis_index_groups=groups, tiled=False)  79 us
    all_to_all x2, starting transfers between devices, swap(): lax.all_to_all(value, axis, 0, 0, axis_index_groups=groups, tiled=False)  11 us
    pallas_call x14, Pallas kernels, run(): pl.pallas_call(kernel, out_shape=shapes if len(shapes) > 1 else shapes[0]...  8.93 us
    all_to_all x2, waiting for transfers between devices, swap(): lax.all_to_all(value, axis, 0, 0, axis_index_groups=groups, tiled=False)  8.03 us
    ppermute x1, starting transfers between devices, per_device(): taken = lax.ppermute(give, 'ctx', [(i, i ^ 1) for i in range(shards)])  4.24 us
    ppermute x1, starting transfers between devices, per_device(): other = lax.ppermute(packed, 'ctx', twins)  3.23 us
    unnamed x22, local copies, waits for them, and re-layouts  2.83 us
  transfers between devices with their start and end apart: 6, of which 3 were waited for; matrix products, arithmetic and copies ran while one was open for 0% of the time, Pallas kernels for 4%

profile of v7, /device:TPU:1, one launch (start us, length us, event | category | flops | bytes accessed | tf_op | source)
XLA Modules:
  0.0 123.0 jit_solution(11351677690130794457)
XLA Ops:
  0.6 0.0 copy-start
  0.6 0.8 copy-done
  1.5 0.0 copy-start.3
  1.5 0.8 copy-done.3
  2.2 0.0 copy-start.5
  2.2 0.8 copy-done.5
  3.0 0.5 shard_map.111
  3.5 16.7 %all_to_all.40.r_ref = bf16[8,160,128]{2,1,0:T(8,128)(2,1)S(1)} all-to-all(bf16[8,160,128]{2,1,0:T(8,128)(2,1)S(1)} %shard_map.111), channel_id=1, replica_groups={{0,1,2,3,4,5,6,7},{8,9,10,11,12,13,14,15},{16,17,18,19,20,21,22,23},{24..., dimensions={0} | all-to-all | bytes 655360 | tf_op jit(solution)/shard_map/all_to_all | solution.py:401
  20.2 0.1 shard_map.112
  20.3 1.3 %collective-permute-start = (bf16[4,128,128]{2,1,0:T(8,128)(2,1)S(1)}, bf16[4,128,128]{2,1,0:T(8,128)(2,1)S(1)}, u32[]{:S(2)}, u32[]{:S(2)}) collective-permute-start(bf16[4,128,128]{2,1,0:T(8,128)(2,1)S(1)} %get-tuple-element.43), channel_id=1, source_target_pairs={{0,8},{1,9},{2,10},{3,11},{4,12},{5,13},{6,14},{7,15},{8,16},{9,17... | collective-permute-start | bytes 393224 | tf_op jit(solution)/shard_map/ppermute | solution.py:433
  21.6 2.4 %collective-permute-done.b_ref.pf_ref = bf16[4,128,128]{2,1,0:T(8,128)(2,1)S(1)} collective-permute-done((bf16[4,128,128]{2,1,0:T(8,128)(2,1)S(1)}, bf16[4,128,128]{2,1,0:T(8,128)(2,1)S(1)}, u32[]{:S(2)}, u32[]{:S(2)}) %collective-permute-start) | collective-permute-done | bytes 131104 | tf_op jit(solution)/shard_map/ppermute | solution.py:433
  24.0 3.2 %collective-permute-start.1 = (bf16[12,128,128]{2,1,0:T(8,128)(2,1)S(1)}, bf16[12,128,128]{2,1,0:T(8,128)(2,1)S(1)}, u32[]{:S(2)}, u32[]{:S(2)}) collective-permute-start(bf16[12,128,128]{2,1,0:T(8,128)(2,1)S(1)} %shard_map.116), channel_id=1, source_target_pairs={{0,1},{1,0},{2,3},{3,2},{4,5},{5,4},{6,7},{7,6},{8,9},{9,8},{10,11... | collective-permute-start | bytes 1179656 | tf_op jit(solution)/shard_map/ppermute | solution.py:436
  27.2 14.2 %all_to_all.41.c_ref = bf16[8,32,128]{2,1,0:T(8,128)(2,1)S(1)} all-to-all(bf16[8,32,128]{2,1,0:T(8,128)(2,1)S(1)} %get-tuple-element.33), channel_id=1, replica_groups={{0,8,16,24,32,40,48,56},{1,9,17,25,33,41,49,57},{2,10,18,26,34,42,50,58..., dimensions={0} | all-to-all | bytes 131072 | tf_op jit(solution)/shard_map/all_to_all | solution.py:401
  41.4 0.0 copy-start.2
  41.4 0.7 shard_map.113
  42.0 0.0 copy-start.1
  42.0 0.0 copy-start.4
  42.0 0.0 copy-start.8
  42.0 0.0 copy-start.9
  42.0 0.0 copy-start.10
  42.0 4.9 %all-to-all-start.2 = ((bf16[8,32,128]{2,1,0:T(8,128)(2,1)}), bf16[8,32,128]{2,1,0:T(8,128)(2,1)S(1)}, u32[]{:S(2)}, u32[]{:S(2)}) async-start(bf16[8,32,128]{2,1,0:T(8,128)(2,1)} %shard_map.113), calls=%async_computation.2 | async-start | bytes 131072 | tf_op jit(solution)/shard_map/all_to_all | solution.py:401
  47.0 0.0 copy-done.2
  47.0 0.0 copy-done.1
  47.0 0.0 copy-done.4
  47.0 0.0 copy-done.8
  47.0 0.0 copy-done.9
  47.0 0.0 copy-done.10
  47.0 0.4 shard_map.114
  47.5 0.0 copy-start.6
  47.5 0.0 copy-start.7
  47.5 0.0 collective-permute-done.1.other_ref.ps_ref
  47.5 0.4 shard_map.117
  48.0 0.3 copy-done.6
  48.2 0.2 copy-done.7
  48.4 1.9 %shard_map.118 = (f32[512,128]{1,0:T(8,128)S(1)}, bf16[4,256,128]{2,1,0:T(8,128)(2,1)S(1)}, f32[128,128]{1,0:T(8,128)S(1)}, f32[128,128]{1,0:T(8,128)S(1)}) custom-call(bf16[1,128,512]{2,1,0:T(8,128)(2,1)S(1)} %copy-done.2, bf16[1,128,128]{2,1,0:T(8,128)(2,1)S(1)} %copy-done.4, bf16[1,128,128]{2,1,0:T(8,128)(2,1)S(1)} %copy-done.6, ...), custom_call_target="tpu_custom_call" | custom-call | tf_op jit(solution)/shard_map/pallas_call | solution.py:387
  50.3 1.3 %collective-permute-start.2 = (bf16[4,256,128]{2,1,0:T(8,128)(2,1)S(1)}, bf16[4,256,128]{2,1,0:T(8,128)(2,1)S(1)}, u32[]{:S(2)}, u32[]{:S(2)}) collective-permute-start(bf16[4,256,128]{2,1,0:T(8,128)(2,1)S(1)} %get-tuple-element.51.own_ref), channel_id=1, source_target_pairs={{8,0},{9,1},{10,2},{11,3},{12,4},{13,5},{14,6},{15,7},{16,8},{17,9... | collective-permute-start | bytes 786440 | tf_op jit(solution)/shard_map/ppermute | solution.py:474
  51.6 0.3 all-to-all-done.2.r_ref
  51.9 1.2 shard_map.115
  53.0 9.6 %all_to_all.42.r_ref = bf16[8,64,128]{2,1,0:T(8,128)(2,1)S(1)} all-to-all(bf16[8,64,128]{2,1,0:T(8,128)(2,1)S(1)} %get-tuple-element.50), channel_id=1, replica_groups={{0,1,2,3,4,5,6,7},{8,9,10,11,12,13,14,15},{16,17,18,19,20,21,22,23},{24..., dimensions={0} | all-to-all | bytes 262144 | tf_op jit(solution)/shard_map/all_to_all | solution.py:401
  62.6 11.8 %all_to_all.43.c_ref = bf16[8,32,128]{2,1,0:T(8,128)(2,1)S(1)} all-to-all(bf16[8,32,128]{2,1,0:T(8,128)(2,1)S(1)} %shard_map.120), channel_id=1, replica_groups={{0,8,16,24,32,40,48,56},{1,9,17,25,33,41,49,57},{2,10,18,26,34,42,50,58..., dimensions={0} | all-to-all | bytes 131072 | tf_op jit(solution)/shard_map/all_to_all | solution.py:401
  74.4 0.0 collective-permute-done.2.back_ref
  74.4 0.9 shard_map.121
  75.4 4.2 %collective-permute-start.3 = (bf16[8,128,128]{2,1,0:T(8,128)(2,1)S(1)}, bf16[8,128,128]{2,1,0:T(8,128)(2,1)S(1)}, u32[]{:S(2)}, u32[]{:S(2)}) collective-permute-start(bf16[8,128,128]{2,1,0:T(8,128)(2,1)S(1)} %get-tuple-element.55), channel_id=1, source_target_pairs={{0,1},{1,0},{2,3},{3,2},{4,5},{5,4},{6,7},{7,6},{8,9},{9,8},{10,11... | collective-permute-start | bytes 786440 | tf_op jit(solution)/shard_map/ppermute | solution.py:483
  79.6 9.7 %all_to_all.44.r_ref = bf16[8,32,128]{2,1,0:T(8,128)(2,1)S(1)} all-to-all(bf16[8,32,128]{2,1,0:T(8,128)(2,1)S(1)} %get-tuple-element.52), channel_id=1, replica_groups={{0,8,16,24,32,40,48,56},{1,9,17,25,33,41,49,57},{2,10,18,26,34,42,50,58..., dimensions={0} | all-to-all | bytes 131072 | tf_op jit(solution)/shard_map/all_to_all | solution.py:401
  89.4 17.1 %all_to_all.45.r_ref = bf16[8,32,128]{2,1,0:T(8,128)(2,1)S(1)} all-to-all(bf16[8,32,128]{2,1,0:T(8,128)(2,1)S(1)} %shard_map.122), channel_id=1, replica_groups=mesh['heads'=8,'ctx'=64] {'heads'}, dimensions={0} | all-to-all | bytes 131072 | tf_op jit(solution)/shard_map/all_to_all | solution.py:401
  106.4 0.0 collective-permute-done.3.got_ref
  106.4 0.9 shard_map.123
  107.3 6.1 %all-to-all-start.7 = ((bf16[8,224,128]{2,1,0:T(8,128)(2,1)}), bf16[8,224,128]{2,1,0:T(8,128)(2,1)S(1)}, u32[]{:S(2)}, u32[]{:S(2)}) async-start(bf16[8,224,128]{2,1,0:T(8,128)(2,1)} %shard_map.123), calls=%async_computation.7 | async-start | bytes 917504 | tf_op jit(solution)/shard_map/all_to_all | solution.py:401
  113.4 0.9 shard_map.119
  114.3 7.7 %all-to-all-done.7.r_ref = bf16[8,224,128]{2,1,0:T(8,128)(2,1)S(1)} async-done(((bf16[8,224,128]{2,1,0:T(8,128)(2,1)}), bf16[8,224,128]{2,1,0:T(8,128)(2,1)S(1)}, u32[]{:S(2)}, u32[]{:S(2)}) %all-to-all-start.7) | async-done | bytes 458784 | tf_op jit(solution)/shard_map/all_to_all | solution.py:401
  122.0 1.0 shard_map.124
  (3 shorter events, 0.1 us)
Async XLA Ops:
  0.6 0.8 copy-start
  1.5 0.8 copy-start.3
  2.2 0.8 copy-start.5
  20.3 3.7 %collective-permute-start = (bf16[4,128,128]{2,1,0:T(8,128)(2,1)S(1)}, bf16[4,128,128]{2,1,0:T(8,128)(2,1)S(1)}, u32[]{:S(2)}, u32[]{:S(2)}) collective-permute-start(bf16[4,128,128]{2,1,0:T(8,128)(2,1)S(1)} %get-tuple-element.43), channel_id=1, source_target_pairs={{0,8},{1,9},{2,10},{3,11},{4,12},{5,13},{6,14},{7,15},{8,16},{9,17... | collective-permute-start | bytes 393224 | tf_op jit(solution)/shard_map/ppermute | solution.py:433
  24.0 23.5 %collective-permute-start.1 = (bf16[12,128,128]{2,1,0:T(8,128)(2,1)S(1)}, bf16[12,128,128]{2,1,0:T(8,128)(2,1)S(1)}, u32[]{:S(2)}, u32[]{:S(2)}) collective-permute-start(bf16[12,128,128]{2,1,0:T(8,128)(2,1)S(1)} %shard_map.116), channel_id=1, source_target_pairs={{0,1},{1,0},{2,3},{3,2},{4,5},{5,4},{6,7},{7,6},{8,9},{9,8},{10,11... | collective-permute-start | bytes 1179656 | tf_op jit(solution)/shard_map/ppermute | solution.py:436
  41.4 5.6 %copy-start.2 = (bf16[1,128,512]{2,1,0:T(8,128)(2,1)S(1)}, bf16[1,128,512]{2,1,0:T(8,128)(2,1)}, u32[]{:S(2)}) copy-start(bf16[1,128,512]{2,1,0:T(8,128)(2,1)} %q_ref.5) | copy-start | bytes 393220
  42.0 5.0 %copy-start.1 = (bf16[128,256]{1,0:T(8,128)(2,1)S(1)}, bf16[128,256]{1,0:T(8,128)(2,1)}, u32[]{:S(2)}) copy-start(bf16[128,256]{1,0:T(8,128)(2,1)} %w_ref.7) | copy-start | bytes 196612
  42.0 5.0 %copy-start.4 = (bf16[1,128,128]{2,1,0:T(8,128)(2,1)S(1)}, bf16[1,128,128]{2,1,0:T(8,128)(2,1)}, u32[]{:S(2)}) copy-start(bf16[1,128,128]{2,1,0:T(8,128)(2,1)} %k_ref.7) | copy-start | bytes 98308
  42.0 5.0 %copy-start.8 = (f32[1,512]{1,0:T(1,128)S(1)}, f32[1,512]{1,0:T(1,128)}, u32[]{:S(2)}) copy-start(f32[1,512]{1,0:T(1,128)} %gl_ref.1) | copy-start | bytes 6148
  42.0 5.0 %copy-start.9 = (f32[1,512]{1,0:T(1,128)S(1)}, f32[1,512]{1,0:T(1,128)}, u32[]{:S(2)}) copy-start(f32[1,512]{1,0:T(1,128)} %gs_ref.1) | copy-start | bytes 6148
  42.0 5.0 %copy-start.10 = (s32[1,64,4]{1,2,0:T(4,128)S(1)}, s32[1,64,4]{1,2,0:T(4,128)}, u32[]{:S(2)}) copy-start(s32[1,64,4]{1,2,0:T(4,128)} %param.14) | copy-start | bytes 3076
  42.0 9.8 %all-to-all-start.2 = ((bf16[8,32,128]{2,1,0:T(8,128)(2,1)}), bf16[8,32,128]{2,1,0:T(8,128)(2,1)S(1)}, u32[]{:S(2)}, u32[]{:S(2)}) async-start(bf16[8,32,128]{2,1,0:T(8,128)(2,1)} %shard_map.113), calls=%async_computation.2 | async-start | bytes 131072 | tf_op jit(solution)/shard_map/all_to_all | solution.py:401
  47.5 0.8 copy-start.6
  47.5 0.9 copy-start.7
  50.3 24.1 %collective-permute-start.2 = (bf16[4,256,128]{2,1,0:T(8,128)(2,1)S(1)}, bf16[4,256,128]{2,1,0:T(8,128)(2,1)S(1)}, u32[]{:S(2)}, u32[]{:S(2)}) collective-permute-start(bf16[4,256,128]{2,1,0:T(8,128)(2,1)S(1)} %get-tuple-element.51.own_ref), channel_id=1, source_target_pairs={{8,0},{9,1},{10,2},{11,3},{12,4},{13,5},{14,6},{15,7},{16,8},{17,9... | collective-permute-start | bytes 786440 | tf_op jit(solution)/shard_map/ppermute | solution.py:474
  75.4 31.1 %collective-permute-start.3 = (bf16[8,128,128]{2,1,0:T(8,128)(2,1)S(1)}, bf16[8,128,128]{2,1,0:T(8,128)(2,1)S(1)}, u32[]{:S(2)}, u32[]{:S(2)}) collective-permute-start(bf16[8,128,128]{2,1,0:T(8,128)(2,1)S(1)} %get-tuple-element.55), channel_id=1, source_target_pairs={{0,1},{1,0},{2,3},{3,2},{4,5},{5,4},{6,7},{7,6},{8,9},{9,8},{10,11... | collective-permute-start | bytes 786440 | tf_op jit(solution)/shard_map/ppermute | solution.py:483
  107.3 14.7 %all-to-all-start.7 = ((bf16[8,224,128]{2,1,0:T(8,128)(2,1)}), bf16[8,224,128]{2,1,0:T(8,128)(2,1)S(1)}, u32[]{:S(2)}, u32[]{:S(2)}) async-start(bf16[8,224,128]{2,1,0:T(8,128)(2,1)} %shard_map.123), calls=%async_computation.7 | async-start | bytes 917504 | tf_op jit(solution)/shard_map/all_to_all | solution.py:401

commit v8 on v7

--- a/solution.py
+++ b/solution.py
@@ -344,14 +344,13 @@
 def make_last_kernel(scale):
     def last_kernel(r_ref, carried_ref, keep_ref, got_ref, o_ref):
         step = r_ref.shape[1]
-        high, low = split(jnp.sum(r_ref[...].astype(F32), axis=0) * scale)
+        part = (jnp.sum(r_ref[...].astype(F32), axis=0) * scale).astype(BF16)
         o_ref[:, :step] = carried_ref[...]
         for spot in range(SIDE):
-            o_ref[spot, step : 2 * step] = high
-            o_ref[spot, 2 * step : 3 * step] = low
+            o_ref[spot, step : 2 * step] = part
         for spot in range(SIDE):
             far = keep_ref[spot].astype(F32) + got_ref[spot].astype(F32)
-            o_ref[spot, 3 * step :] = far.astype(BF16)
+            o_ref[spot, 2 * step :] = far.astype(BF16)
 
     return last_kernel
 
@@ -365,10 +364,9 @@
     step = w.shape[1] // SIDE
     carried = whole(r_ref[:, :step])
     weight = whole(r_ref[:, step : 2 * step]).astype(F32)
-    weight = weight + whole(r_ref[:, 2 * step : 3 * step]).astype(F32)
     wo_ref[...] = weight.T
     key_back, value_back = (
-        sum(r_ref[spot, 3 * step :].astype(F32) for spot in range(parity, SIDE, 2))
+        sum(r_ref[spot, 2 * step :].astype(F32) for spot in range(parity, SIDE, 2))
         for parity in range(2)
     )
     feat, slope = features(nn(keys, w))
@@ -484,7 +482,7 @@
     got = swap(sent, "ctx", in_column)
     sent = call(column_sum_kernel, ((groups, step, size), BF16))(got)
     got = swap(sent, "heads")
-    sent = call(make_last_kernel(scale), ((SIDE, 3 * step + length, size), BF16))(
+    sent = call(make_last_kernel(scale), ((SIDE, 2 * step + length, size), BF16))(
         got, carried, keep, taken
     )
     got = swap(sent, "ctx", in_row)

time: 124 us -> 123 us (level)
  transfers between devices with their start and end apart: 6 -> 6, of which waited for: 3 -> 3; matrix products, arithmetic and copies ran while one was open for 0% -> 0% of each run, Pallas kernels for 4% -> 5%
where the time goes in v8:
time: 123 us; the launch traced here: 122 us
  blocking collectives  79 us (64%)
  starting transfers between devices  21 us (17%)
  waiting for transfers between devices  9.45 us (8%)
  Pallas kernels  8.89 us (7%)
  local copies, waits for them, and re-layouts  2.83 us (2%)
    all_to_all x6, blocking collectives, swap(): lax.all_to_all(value, axis, 0, 0, axis_index_groups=groups, tiled=False)  79 us
    all_to_all x2, starting transfers between devices, swap(): lax.all_to_all(value, axis, 0, 0, axis_index_groups=groups, tiled=False)  11 us
    pallas_call x14, Pallas kernels, run(): pl.pallas_call(kernel, out_shape=shapes if len(shapes) > 1 else shapes[0]...  8.89 us
    all_to_all x2, waiting for transfers between devices, swap(): lax.all_to_all(value, axis, 0, 0, axis_index_groups=groups, tiled=False)  7.08 us
    ppermute x1, starting transfers between devices, per_device(): taken = lax.ppermute(give, 'ctx', [(i, i ^ 1) for i in range(shards)])  4.24 us
    ppermute x1, starting transfers between devices, per_device(): other = lax.ppermute(packed, 'ctx', twins)  3.23 us
    unnamed x22, local copies, waits for them, and re-layouts  2.83 us
  transfers between devices with their start and end apart: 6, of which 3 were waited for; matrix products, arithmetic and copies ran while one was open for 0% of the time, Pallas kernels for 5%

profile of v8, /device:TPU:1, one launch (start us, length us, event | category | flops | bytes accessed | tf_op | source)
XLA Modules:
  0.0 122.0 jit_solution(8293275473028105181)
XLA Ops:
  0.6 0.0 copy-start
  0.6 0.8 copy-done
  1.5 0.0 copy-start.3
  1.5 0.8 copy-done.3
  2.2 0.0 copy-start.5
  2.2 0.8 copy-done.5
  3.0 0.5 shard_map.111
  3.5 16.7 %all_to_all.40.r_ref = bf16[8,160,128]{2,1,0:T(8,128)(2,1)S(1)} all-to-all(bf16[8,160,128]{2,1,0:T(8,128)(2,1)S(1)} %shard_map.111), channel_id=1, replica_groups={{0,1,2,3,4,5,6,7},{8,9,10,11,12,13,14,15},{16,17,18,19,20,21,22,23},{24..., dimensions={0} | all-to-all | bytes 655360 | tf_op jit(solution)/shard_map/all_to_all | solution.py:399
  20.2 0.1 shard_map.112
  20.3 1.3 %collective-permute-start = (bf16[4,128,128]{2,1,0:T(8,128)(2,1)S(1)}, bf16[4,128,128]{2,1,0:T(8,128)(2,1)S(1)}, u32[]{:S(2)}, u32[]{:S(2)}) collective-permute-start(bf16[4,128,128]{2,1,0:T(8,128)(2,1)S(1)} %get-tuple-element.43), channel_id=1, source_target_pairs={{0,8},{1,9},{2,10},{3,11},{4,12},{5,13},{6,14},{7,15},{8,16},{9,17... | collective-permute-start | bytes 393224 | tf_op jit(solution)/shard_map/ppermute | solution.py:431
  21.6 2.4 %collective-permute-done.b_ref.pf_ref = bf16[4,128,128]{2,1,0:T(8,128)(2,1)S(1)} collective-permute-done((bf16[4,128,128]{2,1,0:T(8,128)(2,1)S(1)}, bf16[4,128,128]{2,1,0:T(8,128)(2,1)S(1)}, u32[]{:S(2)}, u32[]{:S(2)}) %collective-permute-start) | collective-permute-done | bytes 131104 | tf_op jit(solution)/shard_map/ppermute | solution.py:431
  24.0 3.2 %collective-permute-start.1 = (bf16[12,128,128]{2,1,0:T(8,128)(2,1)S(1)}, bf16[12,128,128]{2,1,0:T(8,128)(2,1)S(1)}, u32[]{:S(2)}, u32[]{:S(2)}) collective-permute-start(bf16[12,128,128]{2,1,0:T(8,128)(2,1)S(1)} %shard_map.116), channel_id=1, source_target_pairs={{0,1},{1,0},{2,3},{3,2},{4,5},{5,4},{6,7},{7,6},{8,9},{9,8},{10,11... | collective-permute-start | bytes 1179656 | tf_op jit(solution)/shard_map/ppermute | solution.py:434
  27.2 14.2 %all_to_all.41.c_ref = bf16[8,32,128]{2,1,0:T(8,128)(2,1)S(1)} all-to-all(bf16[8,32,128]{2,1,0:T(8,128)(2,1)S(1)} %get-tuple-element.33), channel_id=1, replica_groups={{0,8,16,24,32,40,48,56},{1,9,17,25,33,41,49,57},{2,10,18,26,34,42,50,58..., dimensions={0} | all-to-all | bytes 131072 | tf_op jit(solution)/shard_map/all_to_all | solution.py:399
  41.4 0.0 copy-start.2
  41.4 0.7 shard_map.113
  42.0 0.0 copy-start.1
  42.0 0.0 copy-start.4
  42.0 0.0 copy-start.8
  42.0 0.0 copy-start.9
  42.0 0.0 copy-start.10
  42.0 4.9 %all-to-all-start.2 = ((bf16[8,32,128]{2,1,0:T(8,128)(2,1)}), bf16[8,32,128]{2,1,0:T(8,128)(2,1)S(1)}, u32[]{:S(2)}, u32[]{:S(2)}) async-start(bf16[8,32,128]{2,1,0:T(8,128)(2,1)} %shard_map.113), calls=%async_computation.2 | async-start | bytes 131072 | tf_op jit(solution)/shard_map/all_to_all | solution.py:399
  47.0 0.0 copy-done.2
  47.0 0.0 copy-done.1
  47.0 0.0 copy-done.4
  47.0 0.0 copy-done.8
  47.0 0.0 copy-done.9
  47.0 0.0 copy-done.10
  47.0 0.4 shard_map.114
  47.5 0.0 copy-start.6
  47.5 0.0 copy-start.7
  47.5 0.0 collective-permute-done.1.other_ref.ps_ref
  47.5 0.4 shard_map.117
  48.0 0.3 copy-done.6
  48.2 0.2 copy-done.7
  48.4 1.9 %shard_map.118 = (f32[512,128]{1,0:T(8,128)S(1)}, bf16[4,256,128]{2,1,0:T(8,128)(2,1)S(1)}, f32[128,128]{1,0:T(8,128)S(1)}, f32[128,128]{1,0:T(8,128)S(1)}) custom-call(bf16[1,128,512]{2,1,0:T(8,128)(2,1)S(1)} %copy-done.2, bf16[1,128,128]{2,1,0:T(8,128)(2,1)S(1)} %copy-done.4, bf16[1,128,128]{2,1,0:T(8,128)(2,1)S(1)} %copy-done.6, ...), custom_call_target="tpu_custom_call" | custom-call | tf_op jit(solution)/shard_map/pallas_call | solution.py:385
  50.3 1.3 %collective-permute-start.2 = (bf16[4,256,128]{2,1,0:T(8,128)(2,1)S(1)}, bf16[4,256,128]{2,1,0:T(8,128)(2,1)S(1)}, u32[]{:S(2)}, u32[]{:S(2)}) collective-permute-start(bf16[4,256,128]{2,1,0:T(8,128)(2,1)S(1)} %get-tuple-element.51.own_ref), channel_id=1, source_target_pairs={{8,0},{9,1},{10,2},{11,3},{12,4},{13,5},{14,6},{15,7},{16,8},{17,9... | collective-permute-start | bytes 786440 | tf_op jit(solution)/shard_map/ppermute | solution.py:472
  51.6 0.3 all-to-all-done.2.r_ref
  51.9 1.2 shard_map.115
  53.0 9.6 %all_to_all.42.r_ref = bf16[8,64,128]{2,1,0:T(8,128)(2,1)S(1)} all-to-all(bf16[8,64,128]{2,1,0:T(8,128)(2,1)S(1)} %get-tuple-element.50), channel_id=1, replica_groups={{0,1,2,3,4,5,6,7},{8,9,10,11,12,13,14,15},{16,17,18,19,20,21,22,23},{24..., dimensions={0} | all-to-all | bytes 262144 | tf_op jit(solution)/shard_map/all_to_all | solution.py:399
  62.6 11.8 %all_to_all.43.c_ref = bf16[8,32,128]{2,1,0:T(8,128)(2,1)S(1)} all-to-all(bf16[8,32,128]{2,1,0:T(8,128)(2,1)S(1)} %shard_map.120), channel_id=1, replica_groups={{0,8,16,24,32,40,48,56},{1,9,17,25,33,41,49,57},{2,10,18,26,34,42,50,58..., dimensions={0} | all-to-all | bytes 131072 | tf_op jit(solution)/shard_map/all_to_all | solution.py:399
  74.4 0.0 collective-permute-done.2.back_ref
  74.4 0.9 shard_map.121
  75.4 4.2 %collective-permute-start.3 = (bf16[8,128,128]{2,1,0:T(8,128)(2,1)S(1)}, bf16[8,128,128]{2,1,0:T(8,128)(2,1)S(1)}, u32[]{:S(2)}, u32[]{:S(2)}) collective-permute-start(bf16[8,128,128]{2,1,0:T(8,128)(2,1)S(1)} %get-tuple-element.55), channel_id=1, source_target_pairs={{0,1},{1,0},{2,3},{3,2},{4,5},{5,4},{6,7},{7,6},{8,9},{9,8},{10,11... | collective-permute-start | bytes 786440 | tf_op jit(solution)/shard_map/ppermute | solution.py:481
  79.6 9.7 %all_to_all.44.r_ref = bf16[8,32,128]{2,1,0:T(8,128)(2,1)S(1)} all-to-all(bf16[8,32,128]{2,1,0:T(8,128)(2,1)S(1)} %get-tuple-element.52), channel_id=1, replica_groups={{0,8,16,24,32,40,48,56},{1,9,17,25,33,41,49,57},{2,10,18,26,34,42,50,58..., dimensions={0} | all-to-all | bytes 131072 | tf_op jit(solution)/shard_map/all_to_all | solution.py:399
  89.4 17.1 %all_to_all.45.r_ref = bf16[8,32,128]{2,1,0:T(8,128)(2,1)S(1)} all-to-all(bf16[8,32,128]{2,1,0:T(8,128)(2,1)S(1)} %shard_map.122), channel_id=1, replica_groups=mesh['heads'=8,'ctx'=64] {'heads'}, dimensions={0} | all-to-all | bytes 131072 | tf_op jit(solution)/shard_map/all_to_all | solution.py:399
  106.4 0.0 collective-permute-done.3.got_ref
  106.4 0.8 shard_map.123
  107.3 6.0 %all-to-all-start.7 = ((bf16[8,192,128]{2,1,0:T(8,128)(2,1)}), bf16[8,192,128]{2,1,0:T(8,128)(2,1)S(1)}, u32[]{:S(2)}, u32[]{:S(2)}) async-start(bf16[8,192,128]{2,1,0:T(8,128)(2,1)} %shard_map.123), calls=%async_computation.7 | async-start | bytes 786432 | tf_op jit(solution)/shard_map/all_to_all | solution.py:399
  113.3 0.9 shard_map.119
  114.2 6.8 %all-to-all-done.7.r_ref = bf16[8,192,128]{2,1,0:T(8,128)(2,1)S(1)} async-done(((bf16[8,192,128]{2,1,0:T(8,128)(2,1)}), bf16[8,192,128]{2,1,0:T(8,128)(2,1)S(1)}, u32[]{:S(2)}, u32[]{:S(2)}) %all-to-all-start.7) | async-done | bytes 393248 | tf_op jit(solution)/shard_map/all_to_all | solution.py:399
  121.0 1.0 shard_map.124
  (3 shorter events, 0.1 us)
Async XLA Ops:
  0.6 0.8 copy-start
  1.5 0.8 copy-start.3
  2.2 0.8 copy-start.5
  20.3 3.7 %collective-permute-start = (bf16[4,128,128]{2,1,0:T(8,128)(2,1)S(1)}, bf16[4,128,128]{2,1,0:T(8,128)(2,1)S(1)}, u32[]{:S(2)}, u32[]{:S(2)}) collective-permute-start(bf16[4,128,128]{2,1,0:T(8,128)(2,1)S(1)} %get-tuple-element.43), channel_id=1, source_target_pairs={{0,8},{1,9},{2,10},{3,11},{4,12},{5,13},{6,14},{7,15},{8,16},{9,17... | collective-permute-start | bytes 393224 | tf_op jit(solution)/shard_map/ppermute | solution.py:431
  24.0 23.5 %collective-permute-start.1 = (bf16[12,128,128]{2,1,0:T(8,128)(2,1)S(1)}, bf16[12,128,128]{2,1,0:T(8,128)(2,1)S(1)}, u32[]{:S(2)}, u32[]{:S(2)}) collective-permute-start(bf16[12,128,128]{2,1,0:T(8,128)(2,1)S(1)} %shard_map.116), channel_id=1, source_target_pairs={{0,1},{1,0},{2,3},{3,2},{4,5},{5,4},{6,7},{7,6},{8,9},{9,8},{10,11... | collective-permute-start | bytes 1179656 | tf_op jit(solution)/shard_map/ppermute | solution.py:434
  41.4 5.6 %copy-start.2 = (bf16[1,128,512]{2,1,0:T(8,128)(2,1)S(1)}, bf16[1,128,512]{2,1,0:T(8,128)(2,1)}, u32[]{:S(2)}) copy-start(bf16[1,128,512]{2,1,0:T(8,128)(2,1)} %q_ref.5) | copy-start | bytes 393220
  42.0 5.0 %copy-start.1 = (bf16[128,256]{1,0:T(8,128)(2,1)S(1)}, bf16[128,256]{1,0:T(8,128)(2,1)}, u32[]{:S(2)}) copy-start(bf16[128,256]{1,0:T(8,128)(2,1)} %w_ref.7) | copy-start | bytes 196612
  42.0 5.0 %copy-start.4 = (bf16[1,128,128]{2,1,0:T(8,128)(2,1)S(1)}, bf16[1,128,128]{2,1,0:T(8,128)(2,1)}, u32[]{:S(2)}) copy-start(bf16[1,128,128]{2,1,0:T(8,128)(2,1)} %k_ref.7) | copy-start | bytes 98308
  42.0 5.0 %copy-start.8 = (f32[1,512]{1,0:T(1,128)S(1)}, f32[1,512]{1,0:T(1,128)}, u32[]{:S(2)}) copy-start(f32[1,512]{1,0:T(1,128)} %gl_ref.1) | copy-start | bytes 6148
  42.0 5.0 %copy-start.9 = (f32[1,512]{1,0:T(1,128)S(1)}, f32[1,512]{1,0:T(1,128)}, u32[]{:S(2)}) copy-start(f32[1,512]{1,0:T(1,128)} %gs_ref.1) | copy-start | bytes 6148
  42.0 5.0 %copy-start.10 = (s32[1,64,4]{1,2,0:T(4,128)S(1)}, s32[1,64,4]{1,2,0:T(4,128)}, u32[]{:S(2)}) copy-start(s32[1,64,4]{1,2,0:T(4,128)} %param.14) | copy-start | bytes 3076
  42.0 9.8 %all-to-all-start.2 = ((bf16[8,32,128]{2,1,0:T(8,128)(2,1)}), bf16[8,32,128]{2,1,0:T(8,128)(2,1)S(1)}, u32[]{:S(2)}, u32[]{:S(2)}) async-start(bf16[8,32,128]{2,1,0:T(8,128)(2,1)} %shard_map.113), calls=%async_computation.2 | async-start | bytes 131072 | tf_op jit(solution)/shard_map/all_to_all | solution.py:399
  47.5 0.8 copy-start.6
  47.5 0.9 copy-start.7
  50.3 24.1 %collective-permute-start.2 = (bf16[4,256,128]{2,1,0:T(8,128)(2,1)S(1)}, bf16[4,256,128]{2,1,0:T(8,128)(2,1)S(1)}, u32[]{:S(2)}, u32[]{:S(2)}) collective-permute-start(bf16[4,256,128]{2,1,0:T(8,128)(2,1)S(1)} %get-tuple-element.51.own_ref), channel_id=1, source_target_pairs={{8,0},{9,1},{10,2},{11,3},{12,4},{13,5},{14,6},{15,7},{16,8},{17,9... | collective-permute-start | bytes 786440 | tf_op jit(solution)/shard_map/ppermute | solution.py:472
  75.4 31.1 %collective-permute-start.3 = (bf16[8,128,128]{2,1,0:T(8,128)(2,1)S(1)}, bf16[8,128,128]{2,1,0:T(8,128)(2,1)S(1)}, u32[]{:S(2)}, u32[]{:S(2)}) collective-permute-start(bf16[8,128,128]{2,1,0:T(8,128)(2,1)S(1)} %get-tuple-element.55), channel_id=1, source_target_pairs={{0,1},{1,0},{2,3},{3,2},{4,5},{5,4},{6,7},{7,6},{8,9},{9,8},{10,11... | collective-permute-start | bytes 786440 | tf_op jit(solution)/shard_map/ppermute | solution.py:481
  107.3 13.8 %all-to-all-start.7 = ((bf16[8,192,128]{2,1,0:T(8,128)(2,1)}), bf16[8,192,128]{2,1,0:T(8,128)(2,1)S(1)}, u32[]{:S(2)}, u32[]{:S(2)}) async-start(bf16[8,192,128]{2,1,0:T(8,128)(2,1)} %shard_map.123), calls=%async_computation.7 | async-start | bytes 786432 | tf_op jit(solution)/shard_map/all_to_all | solution.py:399
